TPU v7x, 128 devices: a whole 4x4x4 slice. The times are simulated.
128 devices in a mesh: variant: 8 (over z_lo, x), vocab: 16 (over y, z_hi, core).
Axes of the slice: x: 4, y: 4, z: 4 (z_hi: 2, z_lo: 2; z = z_hi * 2 + z_lo), core: 2. Of those that a mesh axis runs over, the one named last changes fastest.
Arguments:
- teacher_hidden: bfloat16 [8, 256, 4096], P(None, None, ('variant', 'vocab')), may hold values from -24 to 24
- teacher_weight: bfloat16 [4096, 64128], P(None, ('vocab', 'variant')), may hold values from -1 to 1
- variant_ids: int32 [8], replicated, may hold values from 0 to 13
- temps: float32 [14], replicated, may hold values from 0.7 to 1.5
- student_hidden: bfloat16 [256, 2048], P(None, 'variant'), may hold values from -24 to 24
- student_weight: bfloat16 [2048, 64128], P('variant', 'vocab'), may hold values from -1 to 1
- token_ids: int32 [256], P('variant'), may hold values from 0 to 64127
- loss_mask: int32 [256], P('variant'), may hold values 0 or 1
Outputs:
- token_loss: float32 [256], P('variant')
- student_grad: float32 [2048, 64128], P('variant', 'vocab')
All inputs are finite; a program needn't handle non-finite values. No bound on the sum of `loss_mask` on one device may be relied on, other than what follows from the above.
Results may differ from a plain program's by a relative error of at most 0.0025.
Values may be sent and summed in bfloat16 or wider, within the bound.
No kernel may reach another device: no remote copies, remote signals or barrier semaphores. Data moves between devices by JAX's collectives and lax.ppermute only.
A program may use at most 192 MiB of HBM per device.

v0:
```python
import jax
import jax.numpy as jnp
from jax import lax
from jax.sharding import PartitionSpec as P

mix_weight = 0.5
loss_scale = 4096.0


def on_device(
    teacher_hidden,
    teacher_weight,
    variant_ids,
    temps,
    student_hidden,
    student_weight,
    token_ids,
    loss_mask,
):
    n_variant = lax.axis_size("variant")
    categories = jnp.arange(temps.shape[0], dtype=jnp.int32)
    taus = jnp.sum(
        jnp.where(variant_ids[:, None] == categories[None, :], temps[None, :], 0.0), axis=1
    )
    hidden_all = lax.all_gather(teacher_hidden, ("variant", "vocab"), axis=2, tiled=True)
    scaled = (
        jnp.einsum("vtd,dc->vtc", hidden_all, teacher_weight, preferred_element_type=jnp.float32)
        / taus[:, None, None]
    )
    local_max = jnp.max(scaled, axis=2)
    top = lax.pmax(local_max, ("variant", "vocab"))
    total = lax.psum(jnp.sum(jnp.exp(scaled - top[:, :, None]), axis=2), ("variant", "vocab"))
    probs = jnp.exp(scaled - top[:, :, None]) / total[:, :, None]
    averaged_cols = jnp.sum(probs, axis=0) / n_variant
    averaged = lax.all_to_all(
        averaged_cols.astype(jnp.bfloat16), "variant", split_axis=0, concat_axis=1, tiled=True
    ).astype(averaged_cols.dtype)
    block = student_hidden
    logits = lax.psum_scatter(
        jnp.dot(block, student_weight, preferred_element_type=jnp.float32),
        "variant",
        scatter_dimension=0,
        tiled=True,
    )
    local_max = jnp.max(logits, axis=1)
    top = lax.pmax(local_max, "vocab")
    total = lax.psum(jnp.sum(jnp.exp(logits - top[:, None]), axis=1), "vocab")
    log_probs = logits - (top + jnp.log(total))[:, None]
    probs_student = jnp.exp(log_probs)
    columns = lax.axis_index("vocab") * logits.shape[1] + jnp.arange(
        logits.shape[1], dtype=jnp.int32
    )
    onehot = token_ids[:, None] == columns[None, :]
    soft, hard = lax.psum(
        (jnp.sum(averaged * log_probs, axis=1), jnp.sum(jnp.where(onehot, log_probs, 0.0), axis=1)),
        "vocab",
    )
    maskf = loss_mask.astype(jnp.float32)
    token_loss = maskf * (-mix_weight * soft - (1.0 - mix_weight) * hard)
    error = (
        loss_scale
        * maskf[:, None]
        * (probs_student - mix_weight * averaged - (1.0 - mix_weight) * onehot.astype(jnp.float32))
    ).astype(jnp.bfloat16)
    block = student_hidden
    student_grad = lax.dot_general(
        block,
        lax.all_gather(error, "variant", axis=0, tiled=True),
        (((0,), (0,)), ((), ())),
        preferred_element_type=jnp.float32,
    )
    return (token_loss, student_grad)


def solution(mesh):
    in_specs = (
        P(None, None, ("variant", "vocab")),
        P(None, ("vocab", "variant")),
        P(),
        P(),
        P(None, "variant"),
        P("variant", "vocab"),
        P("variant"),
        P("variant"),
    )
    out_specs = (P("variant"), P("variant", "vocab"))
    return jax.shard_map(
        on_device, mesh=mesh, in_specs=in_specs, out_specs=out_specs, check_vma=False
    )
```

profile of v0, /device:TPU:2, one launch (start us, length us, event | category | flops | bytes accessed | tf_op | source)
XLA Modules:
  0.0 503.3 jit_solution(16824957268856968234)
XLA Ops:
  8.1 1.5 copy-done
  9.6 3.6 fusion.11
  13.2 0.5 all-gather.3.cloned.1.call-update
  13.8 0.2 select_reduce_fusion
  14.0 59.1 %reduce-scatter.2.cloned.1.call-done = f32[32,4008]{1,0:T(8,128)} async-done(((f32[256,4008]{1,0:T(8,128)}), f32[32,4008]{1,0:T(8,128)}) %reduce-scatter.2.cloned.1.call-update) | async-done | bytes 513040 | tf_op jit(solution)/shard_map/reduce_scatter | solution.py:39
  73.1 1.2 reduce_max.19
  74.3 40.9 %pmax.15 = f32[32]{0:T(128)S(1)} all-reduce(f32[32]{0:T(128)S(1)} %reduce_max.19), channel_id=1, replica_groups=mesh['variant'=8,'vocab'=16] {'vocab'}, use_global_device_ids=true, to_apply=%region_8.9 | all-reduce | flops 32 | bytes 256 | tf_op jit(solution)/shard_map/pmax | solution.py:46
  115.2 148.7 %all-gather.3.cloned.1.call-done = bf16[8,256,4096]{1,2,0:T(8,128)(2,1)} async-done(((bf16[8,256,32]{1,2,0:T(8,128)(2,1)}), bf16[8,256,4096]{1,2,0:T(8,128)(2,1)}) %all-gather.3.cloned.1.call-update) | async-done | bytes 16777232 | tf_op jit(solution)/shard_map/all_gather | solution.py:25
  263.9 14.8 %fusion.10 = (f32[8,256]{1,0:T(8,128)S(1)}, f32[8,256,501]{1,2,0:T(8,128)}) fusion(f32[8]{0:T(128)S(1)} %select_reduce_fusion, bf16[8,256,4096]{1,2,0:T(8,128)(2,1)} %all-gather.3.cloned.1.call-done, bf16[4096,501]{0,1:T(8,128)(2,1)} %param.9), kind=kOutput, calls=%fused_computation.23 | convolution fusion | flops 8407435264 | bytes 24993824 | tf_op jit(solution)/shard_map/vtd,dc->vtc/dot_general | solution.py:27
  278.6 64.7 %pmax.14 = f32[8,256]{1,0:T(8,128)S(1)} all-reduce(f32[8,256]{1,0:T(8,128)S(1)} %get-tuple-element.7), channel_id=1, replica_groups=mesh['variant'=8,'vocab'=16] {'variant','vocab'}, use_global_device_ids=true, to_apply=%region_2.3 | all-reduce | flops 2048 | bytes 16384 | tf_op jit(solution)/shard_map/pmax | solution.py:31
  343.3 2.7 fusion.2
  346.1 61.9 %psum.28 = f32[8,256]{1,0:T(8,128)S(1)} all-reduce(f32[8,256]{1,0:T(8,128)S(1)} %fusion.2), channel_id=1, replica_groups=mesh['variant'=8,'vocab'=16] {'variant','vocab'}, use_global_device_ids=true, to_apply=%region_4.5 | all-reduce | flops 2048 | bytes 16384 | tf_op jit(solution)/shard_map/psum | solution.py:32
  408.0 2.9 divide_reduce_fusion
  411.0 0.8 copy.13
  411.9 5.8 %all-to-all-start = ((bf16[8,32,501]{2,1,0:T(8,128)(2,1)}), bf16[8,32,501]{2,1,0:T(8,128)(2,1)S(1)}, u32[]{:S(2)}, u32[]{:S(2)}) async-start(bf16[8,32,501]{2,1,0:T(8,128)(2,1)} %bitcast.1), calls=%async_computation | async-start | bytes 524288 | tf_op jit(solution)/shard_map/all_to_all | solution.py:35
  417.6 0.3 exponential_reduce_fusion
  417.9 33.9 %psum.29 = f32[32]{0:T(128)S(1)} all-reduce(f32[32]{0:T(128)S(1)} %exponential_reduce_fusion), channel_id=1, replica_groups=mesh['variant'=8,'vocab'=16] {'vocab'}, use_global_device_ids=true, to_apply=%region_10.11 | all-reduce | flops 32 | bytes 256 | tf_op jit(solution)/shard_map/psum | solution.py:47
  451.9 1.1 copy.14
  453.0 1.4 reshape.27
  454.4 1.1 multiply_reduce_fusion
  455.5 33.2 %all-reduce = (f32[32]{0:T(128)S(1)}, f32[32]{0:T(128)S(1)}) all-reduce(f32[32]{0:T(128)S(1)} %get-tuple-element.3, f32[32]{0:T(128)S(1)} %get-tuple-element.2), channel_id=1, replica_groups=mesh['variant'=8,'vocab'=16] {'vocab'}, use_global_device_ids=true, to_apply=%region_14.15 | all-reduce | flops 64 | bytes 512 | tf_op jit(solution)/shard_map/psum | solution.py:54
  488.7 0.5 subtract_multiply_fusion
  489.2 2.3 all-gather.5.cloned.1.call-done
  491.5 4.3 convolution_bitcast_fusion
  (24 shorter events, 0.3 us)
Async XLA Ops:
  8.0 1.6 copy-start
  8.0 5.8 %copy-start.5 = (f32[14]{0:T(128)S(1)}, f32[14]{0:T(128)}, u32[]{:S(2)}) copy-start(f32[14]{0:T(128)} %param.11) | copy-start | bytes 172
  8.0 5.8 %copy-start.6 = (s32[8]{0:T(128)S(1)}, s32[8]{0:T(128)}, u32[]{:S(2)}) copy-start(s32[8]{0:T(128)} %param.10) | copy-start | bytes 100
  8.0 5.9 %copy-start.4 = (s32[32]{0:T(128)S(1)}, s32[32]{0:T(128)}, u32[]{:S(2)}) copy-start(s32[32]{0:T(128)} %param.15) | copy-start | bytes 388
  8.0 65.1 %reduce-scatter.2.cloned.1.call-start = ((), (), s32[]{:S(2)}) async-start(), calls=%async_computation.3 | async-start | bytes 4718592 | tf_op jit(solution)/shard_map/reduce_scatter | solution.py:39
  13.2 250.7 %all-gather.3.cloned.1.call-start = ((), (), s32[]{:S(2)}) async-start(), calls=%async_computation.2 | async-start | bytes 16908288 | tf_op jit(solution)/shard_map/all_gather | solution.py:25
  346.1 71.5 %copy-start.1 = (f32[32,4008]{1,0:T(8,128)S(1)}, f32[32,4008]{1,0:T(8,128)}, u32[]{:S(2)}) copy-start(f32[32,4008]{1,0:T(8,128)} %reduce-scatter.2.cloned.1.call-done) | copy-start | bytes 1539076
  408.0 46.3 %copy-start.3 = (s32[32]{0:T(128)S(1)}, s32[32]{0:T(128)}, u32[]{:S(2)}) copy-start(s32[32]{0:T(128)} %param.14) | copy-start | bytes 388
  411.0 80.6 %copy-start.2 = (bf16[256,256]{1,0:T(8,128)(2,1)S(1)}, bf16[256,256]{1,0:T(8,128)(2,1)}, u32[]{:S(2)}) copy-start(bf16[256,256]{1,0:T(8,128)(2,1)} %param.12) | copy-start | bytes 393220
  411.9 40.0 %all-to-all-start = ((bf16[8,32,501]{2,1,0:T(8,128)(2,1)}), bf16[8,32,501]{2,1,0:T(8,128)(2,1)S(1)}, u32[]{:S(2)}, u32[]{:S(2)}) async-start(bf16[8,32,501]{2,1,0:T(8,128)(2,1)} %bitcast.1), calls=%async_computation | async-start | bytes 524288 | tf_op jit(solution)/shard_map/all_to_all | solution.py:35
  417.6 73.9 %all-gather.5.cloned.1.call-start = ((), (), s32[]{:S(2)}) async-start(), calls=%async_computation.4 | async-start | bytes 2359296 | tf_op jit(solution)/shard_map/all_gather | solution.py:68
Sparse Core Ops, SparseCore 0:
  13.3 59.7 reduce-scatter.1
  455.6 35.8 all-gather.4
Sparse Core Ops, SparseCore 1:
  15.4 248.4 all-gather.2
where the time goes:
time: 506 us; the launch traced here: 503 us
  blocking collectives  235 us (46%)
  waiting for transfers between devices  211 us (42%)
  matrix products  22.7 us (4%)
  between operations  15.6 us (3%)
  other arithmetic  9.05 us (2%)
  starting transfers between devices  5.84 us (1%)
    all_gather x1, waiting for transfers between devices, on_device(): lax.all_gather(teacher_hidden, ('variant', 'vocab'), axis=2, tiled=True)  149 us
    pmax x1, blocking collectives, on_device(): top = lax.pmax(local_max, ('variant', 'vocab'))  64.7 us
    psum x1, blocking collectives, on_device(): lax.psum(jnp.sum(jnp.exp(scaled - top[:, :, None]), axis=2), ('variant',...  61.9 us
    reduce_scatter x1, waiting for transfers between devices, on_device(): lax.psum_scatter(jnp.dot(block, student_weight, preferred_element_type=jn...  59.1 us
    pmax x1, blocking collectives, on_device(): top = lax.pmax(local_max, 'vocab')  40.9 us
    psum x1, blocking collectives, on_device(): total = lax.psum(jnp.sum(jnp.exp(logits - top[:, None]), axis=1), 'vocab')  33.9 us
    psum x1, blocking collectives, on_device(): lax.psum((jnp.sum(averaged * log_probs, axis=1), jnp.sum(jnp.where(onehot...  33.2 us
    dot_general x1, matrix products, on_device(): jnp.einsum('vtd,dc->vtc', hidden_all, teacher_weight, preferred_element_t...  14.8 us
  transfers between devices with their start and end apart: 4, of which 3 were waited for; matrix products, arithmetic and copies ran while one was open for 0% of the time, Pallas kernels for 0%

commit v1 on v0

v1 whole, which is shorter than its diff:
```python
import functools
import jax
import jax.numpy as jnp
from jax import lax
from jax.experimental import pallas as pl
from jax.experimental.pallas import tpu as pltpu
from jax.sharding import PartitionSpec as P

mix_weight = 0.5
loss_scale = 4096.0

AXES = ("variant", "vocab")
SIDE = 4
SPLIT = 768
OFFSETS = (0, -1, 1, 2)


def device_index(x, y, z, c):
    x, y, z = x % SIDE, y % SIDE, z % SIDE
    return ((z % 2) * SIDE + x) * 16 + y * 4 + (z // 2) * 2 + c


def permutation(move):
    return [
        (device_index(x, y, z, c), device_index(*move(x, y, z, c)))
        for x in range(SIDE)
        for y in range(SIDE)
        for z in range(SIDE)
        for c in range(2)
    ]


def ring_shift(axes, step):
    def move(x, y, z, c):
        at = {"x": x, "y": y, "z": z}
        at[axes[c]] += step
        return at["x"], at["y"], at["z"], c

    return permutation(move)


def sibling(value):
    return lax.ppermute(value, AXES, permutation(lambda x, y, z, c: (x, y, z, 1 - c)))


def ring_gather(value, axes):
    return [value] + [
        lax.ppermute(value, AXES, ring_shift(axes, step)) for step in (1, -1, 2)
    ]


def ordered(core, own, other, axis):
    return jnp.where(
        core == 0,
        jnp.concatenate([own, other], axis=axis),
        jnp.concatenate([other, own], axis=axis),
    )


def teacher_kernel(table, inv_tau, *refs):
    first, second = refs[0:4], refs[4:8]
    w_refs, l_refs = refs[8:10], refs[10:12]
    e_refs, stat_ref = refs[12:14], refs[14]
    hidden, w_own, w_sib, sem = refs[15:19]
    w_bufs = (w_own, w_sib)
    copies = [pltpu.make_async_copy(w_refs[i], w_bufs[i], sem.at[i]) for i in range(2)]
    for copy in copies:
        copy.start()

    def chunk_copy(part, ref, s3, n, lanes):
        row = pl.multiple_of(table[part, s3 * 16 + n] * 64, 64)
        return pltpu.make_async_copy(
            ref.at[n], hidden.at[pl.ds(row, 64), lanes], sem.at[2 + part]
        )

    parts = ((first, pl.ds(0, SPLIT)), (second, pl.ds(SPLIT, 1024 - SPLIT)))
    for part, (group, lanes) in enumerate(parts):
        for s3 in range(4):
            def start(n, _, part=part, ref=group[s3], s3=s3, lanes=lanes):
                chunk_copy(part, ref, s3, n, lanes).start()
                return 0
            lax.fori_loop(0, 16, start, 0)
    for part, (group, lanes) in enumerate(parts):
        for s3 in range(4):
            def wait(n, _, part=part, ref=group[s3], s3=s3, lanes=lanes):
                chunk_copy(part, ref, s3, n, lanes).wait()
                return 0
            lax.fori_loop(0, 16, wait, 0)
    for copy in copies:
        copy.wait()

    def tile(j, _):
        lanes = pl.ds(pl.multiple_of(j * 256, 256), 256)
        scale = inv_tau[:, lanes]
        block = hidden[:, lanes]
        scores = [
            jnp.dot(w[...], block, preferred_element_type=jnp.float32) * scale for w in w_bufs
        ]
        top = jnp.maximum(
            jnp.max(scores[0], axis=0, keepdims=True), jnp.max(scores[1], axis=0, keepdims=True)
        )
        total = jnp.zeros((1, 256), jnp.float32)
        cross = jnp.zeros((1, 256), jnp.float32)
        for i in range(2):
            e = jnp.exp(scores[i] - top)
            e_refs[i][:, lanes] = e
            logits = l_refs[i][...]
            total += jnp.sum(e, axis=0, keepdims=True)
            cross += jnp.sum(
                e * jnp.concatenate([logits, logits], axis=1), axis=0, keepdims=True
            )
        stat_ref[0:1, lanes] = top
        stat_ref[1:2, lanes] = total
        stat_ref[2:3, lanes] = cross
        return 0

    lax.fori_loop(0, 4, tile, 0)


def teacher_scores(table, inv_tau, first, second, weights, logits):
    cols, width = weights[0].shape
    vmem = pl.BlockSpec(memory_space=pltpu.VMEM)
    hbm = pl.BlockSpec(memory_space=pl.ANY)
    return pl.pallas_call(
        teacher_kernel,
        out_shape=[
            jax.ShapeDtypeStruct((cols, 1024), jnp.float32),
            jax.ShapeDtypeStruct((cols, 1024), jnp.float32),
            jax.ShapeDtypeStruct((8, 1024), jnp.float32),
        ],
        in_specs=[pl.BlockSpec(memory_space=pltpu.SMEM), vmem] + [hbm] * 10 + [vmem] * 2,
        out_specs=[vmem] * 3,
        scratch_shapes=[
            pltpu.VMEM((width, 1024), jnp.bfloat16),
            pltpu.VMEM((cols, width), jnp.bfloat16),
            pltpu.VMEM((cols, width), jnp.bfloat16),
            pltpu.SemaphoreType.DMA((4,)),
        ],
        compiler_params=pltpu.CompilerParams(vmem_limit_bytes=44 << 20),
        cost_estimate=pl.CostEstimate(
            flops=2 * 2 * cols * width * 1024,
            bytes_accessed=2 * (2 * cols * width + width * 1024) + 8 * cols * 1024,
            transcendentals=2 * cols * 1024,
        ),
    )(table, inv_tau, *first, *second, *weights, *logits)


def on_device(
    teacher_hidden,
    teacher_weight,
    variant_ids,
    temps,
    student_hidden,
    student_weight,
    token_ids,
    loss_mask,
):
    a = lax.axis_index("variant")
    b = lax.axis_index("vocab")
    core = b % 2
    x, y, z = a % 4, b // 4, (b // 2) % 2 * 2 + a // 4
    cols = teacher_weight.shape[1]
    half = 128

    meta = jnp.concatenate(
        [token_ids // 256, token_ids % 256, loss_mask, jnp.zeros((160,), jnp.int32)]
    ).astype(jnp.bfloat16)[None, None]
    mine = lax.dynamic_slice_in_dim(student_hidden, core * half, half, axis=0)
    send = jnp.concatenate(
        [
            jnp.broadcast_to(mine[None], (8, half, 256)),
            student_weight.T.reshape(8, cols, 256),
            jnp.broadcast_to(meta, (8, 1, 256)),
        ],
        axis=1,
    )
    got = lax.all_to_all(send, "variant", 0, 0, tiled=True)
    flat = jnp.transpose(got, (1, 0, 2)).reshape(half + cols + 1, 2048)
    hs, ws = flat[:half], flat[half : half + cols]
    ws_other = sibling(ws)
    meta_all = got[:, half + cols]
    ids = (meta_all[:, 0:32].astype(jnp.int32) * 256 + meta_all[:, 32:64].astype(jnp.int32)).reshape(256)
    maskf = meta_all[:, 64:96].astype(jnp.float32).reshape(256)
    ids_half = lax.dynamic_slice_in_dim(ids, core * half, half)
    mask_half = lax.dynamic_slice_in_dim(maskf, core * half, half)

    halves = [
        lax.dynamic_slice_in_dim(teacher_hidden, start * half, half, axis=1)
        .transpose(2, 0, 1)
        .reshape(32, 1024)
        for start in (core, 1 - core)
    ]
    unit = ordered(core, halves[0], sibling(halves[1]), 0)
    w_own = teacher_weight.T
    w_other = sibling(w_own)
    stage1 = jnp.stack(ring_gather(unit, "zx"))
    first = jnp.stack(ring_gather(stage1[:, :, :SPLIT], "yy")).reshape(16, 64, SPLIT)
    second = jnp.stack(ring_gather(stage1[:, :, SPLIT:], "xz")).reshape(16, 64, 1024 - SPLIT)
    first = ring_gather(first, "xz")
    second = ring_gather(second, "yy")

    offsets = jnp.array(OFFSETS, jnp.int32)
    o1, o2, o3 = (
        offsets.reshape(shape) for shape in ((1, 1, 4), (1, 4, 1), (4, 1, 1))
    )
    zero = jnp.zeros((4, 4, 4), jnp.int32)

    def place(dx, dy, dz):
        px, py, pz = (x + dx) % 4, (y + dy) % 4, (z + dz) % 4
        return ((pz % 2 * 4 + px) * 8 + py * 2 + pz // 2 + zero).reshape(64)

    table = jnp.where(
        core == 0,
        jnp.stack([place(o3, o2, o1), place(o2, o3, o1)]),
        jnp.stack([place(o1, o2, o3), place(o1, o3, o2)]),
    )
    categories = jnp.arange(temps.shape[0], dtype=jnp.int32)
    taus = jnp.sum(
        jnp.where(variant_ids[:, None] == categories[None, :], temps[None, :], 0.0), axis=1
    )
    inv_tau = jnp.repeat(1.0 / taus, half)[None]

    dims = (((1,), (1,)), ((), ()))
    logits = [
        lax.dot_general(w, hs, dims, preferred_element_type=jnp.float32) for w in (ws, ws_other)
    ]
    s_top = jnp.maximum(jnp.max(logits[0], axis=0), jnp.max(logits[1], axis=0))
    s_sum = sum(jnp.sum(jnp.exp(l - s_top), axis=0) for l in logits)
    rows = jnp.arange(cols, dtype=jnp.int32)[:, None]
    onehots = [
        (block * 8 + a) * cols + rows == ids_half[None, :] for block in (b, b + 1 - 2 * core)
    ]
    s_hard = sum(jnp.sum(jnp.where(o, l, 0.0), axis=0) for o, l in zip(onehots, logits))

    e_own, e_other, stats = teacher_scores(
        table, inv_tau, first, second, (w_own, w_other), logits
    )
    e = (e_own, e_other)
    t_stats = stats[:3].reshape(24, half)
    packed = jnp.concatenate(
        [t_stats, jnp.stack([s_top, s_sum, s_hard]), jnp.zeros((5, half), jnp.float32)]
    )
    def merge(g):
        n = g.shape[0]
        top = jnp.max(g[:, 0:8], axis=0)
        scale = jnp.exp(g[:, 0:8] - top)
        total = jnp.sum(g[:, 8:16] * scale, axis=0)
        cross = jnp.sum(g[:, 16:24] * scale, axis=0)
        stop = jnp.max(g[:, 24], axis=0)
        ssum = jnp.sum(g[:, 25] * jnp.exp(g[:, 24] - stop), axis=0)
        hard = jnp.sum(g[:, 26], axis=0)
        return jnp.concatenate(
            [top, total, cross, jnp.stack([stop, ssum, hard]), jnp.zeros((5, half), jnp.float32)]
        )

    tile8 = jnp.broadcast_to(packed[None], (8, 32, half))
    by_variant = merge(lax.all_to_all(tile8, "variant", 0, 0, tiled=True))
    tile16 = jnp.broadcast_to(by_variant[None], (16, 32, half))
    over = lax.all_to_all(tile16, "vocab", 0, 0, tiled=True).reshape(8, 2, 32, half)
    merged = merge(lax.dynamic_index_in_dim(over, core, 1, keepdims=False))
    top, total, cross = merged[0:8], merged[8:16], merged[16:24]
    lse = merged[24] + jnp.log(merged[25])
    hard = merged[26] - lse
    soft = jnp.sum(cross / total, axis=0) / 8 - lse
    loss_half = mask_half * (-mix_weight * soft - (1.0 - mix_weight) * hard)
    loss_all = ordered(core, loss_half, sibling(loss_half), 0)
    token_loss = lax.dynamic_slice_in_dim(loss_all, a * 32, 32)

    local_top = stats[0].reshape(8, half)
    coef = jnp.exp(local_top - top) / (8 * total)
    errors = []
    for i in range(2):
        averaged = sum(e[i][:, v * half : (v + 1) * half] * coef[v] for v in range(8))
        q = jnp.exp(logits[i] - lse)
        errors.append(
            (
                loss_scale
                * mask_half
                * (q - mix_weight * averaged - (1.0 - mix_weight) * onehots[i].astype(jnp.float32))
            ).astype(jnp.bfloat16)
        )
    error = ordered(core, errors[0], sibling(errors[1]), 1)
    error_all = lax.all_to_all(
        jnp.broadcast_to(error[None], (8, cols, 256)), "variant", 0, 0, tiled=True
    ).reshape(8 * cols, 256)
    grad_t = jnp.dot(error_all, student_hidden, preferred_element_type=jnp.float32)
    return token_loss, grad_t.T


def solution(mesh):
    in_specs = (
        P(None, None, ("variant", "vocab")),
        P(None, ("vocab", "variant")),
        P(),
        P(),
        P(None, "variant"),
        P("variant", "vocab"),
        P("variant"),
        P("variant"),
    )
    out_specs = (P("variant"), P("variant", "vocab"))
    return jax.shard_map(
        on_device, mesh=mesh, in_specs=in_specs, out_specs=out_specs, check_vma=False
    )
```

time: 506 us -> 226 us (0.45)
  blocking collectives: 235 us -> 10.7 us
  waiting for transfers between devices: 211 us -> 111 us
  starting transfers between devices: 5.84 us -> 41.6 us
  local copies, waits for them, and re-layouts: 4.83 us -> 24.7 us
  Pallas kernels: 0 us -> 18.2 us
  matrix products: 22.7 us -> 7.41 us
  between operations: 15.6 us -> 1.07 us
    all_gather x2 -> x0, waiting for transfers between devices: 151 us -> none  [the longest x1 149 us: on_device(): lax.all_gather(teacher_hidden, ('variant', 'vocab'), axis=2, tiled=True)]
    psum x3 -> x0, blocking collectives: 129 us -> none  [the longest x1 61.9 us: on_device(): lax.psum(jnp.sum(jnp.exp(scaled - top[:, :, None]), axis=2), ('variant',...]
    pmax x2 -> x0, blocking collectives: 106 us -> none  [the longest x1 64.7 us: on_device(): top = lax.pmax(local_max, ('variant', 'vocab'))]
    ppermute x0 -> x20, waiting for transfers between devices: none -> 75.2 us  [the longest x15 66.9 us: ring_gather(): lax.ppermute(value, AXES, ring_shift(axes, step))]
    reduce_scatter x1 -> x0, waiting for transfers between devices: 59.1 us -> none  [on_device(): lax.psum_scatter(jnp.dot(block, student_weight, preferred_element_type=jn...]
    all_to_all x1 -> x3, waiting for transfers between devices: 0.01 us -> 35.4 us  [the longest x1 26.4 us: on_device(): lax.all_to_all(jnp.broadcast_to(error[None], (8, cols, 256)), 'variant',...]
    ppermute x0 -> x20, starting transfers between devices: none -> 26.4 us  [the longest x15 21.7 us: ring_gather(): lax.ppermute(value, AXES, ring_shift(axes, step))]
    pallas_call x0 -> x1, Pallas kernels: none -> 18.2 us  [teacher_scores(): pl.pallas_call(teacher_kernel, out_shape=[jax.ShapeDtypeStruct((cols, 102...]
  transfers between devices with their start and end apart: 4 -> 23, of which waited for: 3 -> 13; matrix products, arithmetic and copies ran while one was open for 0% -> 11% of each run, Pallas kernels for 0% -> 0%
where the time goes in v1:
time: 226 us; the launch traced here: 223 us
  waiting for transfers between devices  111 us (49%)
  starting transfers between devices  41.6 us (18%)
  local copies, waits for them, and re-layouts  24.7 us (11%)
  Pallas kernels  18.2 us (8%)
  blocking collectives  10.7 us (5%)
  other arithmetic  8.83 us (4%)
  matrix products  7.41 us (3%)
    ppermute x15, waiting for transfers between devices, ring_gather(): lax.ppermute(value, AXES, ring_shift(axes, step))  66.9 us
    all_to_all x1, waiting for transfers between devices, on_device(): lax.all_to_all(jnp.broadcast_to(error[None], (8, cols, 256)), 'variant',...  26.4 us
    ppermute x15, starting transfers between devices, ring_gather(): lax.ppermute(value, AXES, ring_shift(axes, step))  21.7 us
    pallas_call x1, Pallas kernels, teacher_scores(): pl.pallas_call(teacher_kernel, out_shape=[jax.ShapeDtypeStruct((cols, 102...  18.2 us
    slice x5, local copies, waits for them, and re-layouts, on_device(): hs, ws = (flat[:half], flat[half:half + cols])  13.4 us
    all_to_all x1, blocking collectives, on_device(): by_variant = merge(lax.all_to_all(tile8, 'variant', 0, 0, tiled=True))  10.7 us
    all_to_all x1, waiting for transfers between devices, on_device(): lax.all_to_all(tile16, 'vocab', 0, 0, tiled=True).reshape(8, 2, 32, half)  9 us
    ppermute x5, waiting for transfers between devices, sibling(): lax.ppermute(value, AXES, permutation(lambda x, y, z, c: (x, y, z, 1 - c)))  8.27 us
  transfers between devices with their start and end apart: 23, of which 13 were waited for; matrix products, arithmetic and copies ran while one was open for 11% of the time, Pallas kernels for 0%

profile of v1, /device:TPU:2, one launch (start us, length us, event | category | flops | bytes accessed | tf_op | source)
XLA Modules:
  0.0 223.1 jit_solution(15848391475132399889)
XLA Ops:
  6.0 6.3 %all-to-all-start = ((bf16[8,630,256]{2,1,0:T(8,128)(2,1)}), bf16[8,630,256]{2,1,0:T(8,128)(2,1)S(1)}, u32[]{:S(2)}, u32[]{:S(2)}) async-start(bf16[8,630,256]{2,1,0:T(8,128)(2,1)} %pad_maximum_fusion), calls=%async_computation | async-start | bytes 5177344 | tf_op jit(solution)/shard_map/all_to_all | solution.py:177
  13.0 6.1 %collective-permute-done = bf16[32,1024]{1,0:T(8,128)(2,1)S(1)} collective-permute-done((bf16[32,1024]{1,0:T(8,128)(2,1)S(1)}, bf16[32,1024]{1,0:T(8,128)(2,1)S(1)}, u32[]{:S(2)}, u32[]{:S(2)}) %collective-permute-start) | collective-permute-done | bytes 65568 | tf_op jit(solution)/shard_map/ppermute | solution.py:43
  20.7 2.2 collective-permute-start.2
  25.0 15.8 %collective-permute-done.1 = bf16[64,1024]{1,0:T(8,128)(2,1)S(1)} collective-permute-done((bf16[64,1024]{1,0:T(8,128)(2,1)S(1)}, bf16[64,1024]{1,0:T(8,128)(2,1)S(1)}, u32[]{:S(2)}, u32[]{:S(2)}) %collective-permute-start.1) | collective-permute-done | bytes 131104 | tf_op jit(solution)/shard_map/ppermute | solution.py:48
  40.8 2.4 %collective-permute-done.2 = bf16[64,1024]{1,0:T(8,128)(2,1)S(1)} collective-permute-done((bf16[64,1024]{1,0:T(8,128)(2,1)S(1)}, bf16[64,1024]{1,0:T(8,128)(2,1)S(1)}, u32[]{:S(2)}, u32[]{:S(2)}) %collective-permute-start.2) | collective-permute-done | bytes 131104 | tf_op jit(solution)/shard_map/ppermute | solution.py:48
  43.3 4.5 %collective-permute-done.3 = bf16[64,1024]{1,0:T(8,128)(2,1)S(1)} collective-permute-done((bf16[64,1024]{1,0:T(8,128)(2,1)S(1)}, bf16[64,1024]{1,0:T(8,128)(2,1)S(1)}, u32[]{:S(2)}, u32[]{:S(2)}) %collective-permute-start.3) | collective-permute-done | bytes 131104 | tf_op jit(solution)/shard_map/ppermute | solution.py:48
  51.8 3.0 %collective-permute-start.5 = (bf16[4,64,768]{2,1,0:T(8,128)(2,1)}, bf16[4,64,768]{2,1,0:T(8,128)(2,1)}, u32[]{:S(2)}, u32[]{:S(2)}) collective-permute-start(bf16[4,64,768]{2,1,0:T(8,128)(2,1)} %get-tuple-element.23), channel_id=1, source_target_pairs={{0,12},{1,13},{64,76},{65,77},{2,14},{3,15},{66,78},{67,79},{4,0},... | collective-permute-start | bytes 1179656 | tf_op jit(solution)/shard_map/ppermute | solution.py:48
  57.0 3.9 %copy.52 = bf16[501,8,256]{0,2,1:T(8,128)(2,1)} copy(bf16[501,8,256]{2,0,1:T(8,128)(2,1)} %slice.207) | data formatting | bytes 4104192 | tf_op jit(solution)/shard_map/slice | solution.py:179
  60.9 4.0 %copy.53 = bf16[501,2048]{1,0:T(8,128)(2,1)} copy(bf16[501,2048]{0,1:T(8,128)(2,1)} %bitcast.95) | data formatting | bytes 4104192 | tf_op jit(solution)/shard_map/slice | solution.py:179
  65.5 3.9 %collective-permute-start.17 = (bf16[501,2048]{1,0:T(8,128)(2,1)}, bf16[501,2048]{1,0:T(8,128)(2,1)}, u32[]{:S(2)}, u32[]{:S(2)}) collective-permute-start(bf16[501,2048]{1,0:T(8,128)(2,1)} %copy.53), channel_id=1, source_target_pairs={{0,1},{1,0},{64,65},{65,64},{2,3},{3,2},{66,67},{67,66},{4,5},{5,4... | collective-permute-start | bytes 6156296 | tf_op jit(solution)/shard_map/ppermute | solution.py:43
  76.1 11.0 %collective-permute-done.4 = bf16[4,64,768]{2,1,0:T(8,128)(2,1)S(1)} collective-permute-done((bf16[4,64,768]{2,1,0:T(8,128)(2,1)}, bf16[4,64,768]{2,1,0:T(8,128)(2,1)S(1)}, u32[]{:S(2)}, u32[]{:S(2)}) %collective-permute-start.4) | collective-permute-done | bytes 393248 | tf_op jit(solution)/shard_map/ppermute | solution.py:48
  90.1 8.2 %collective-permute-done.13.refs_5_ = bf16[16,64,256]{2,1,0:T(8,128)(2,1)S(1)} collective-permute-done((bf16[16,64,256]{2,1,0:T(8,128)(2,1)S(1)}, bf16[16,64,256]{2,1,0:T(8,128)(2,1)S(1)}, u32[]{:S(2)}, u32[]{:S(2)}) %collective-permute-start.13) | collective-permute-done | bytes 524320 | tf_op jit(solution)/shard_map/ppermute | solution.py:48
  108.8 2.4 %fusion.23 = (f32[128]{0:T(128)S(1)}, f32[501,128]{1,0:T(8,128)S(1)}) fusion(bf16[630,8,256]{2,0,1:T(8,128)(2,1)} %bitcast.94), kind=kOutput, calls=%fused_computation.109 | convolution fusion | flops 262732288 | bytes 2837504 | tf_op jit(solution)/shard_map/dot_general | solution.py:225
  111.2 2.4 %fusion.24 = (f32[128]{0:T(128)S(1)}, f32[501,128]{1,0:T(8,128)S(1)}) fusion(bf16[501,2048]{1,0:T(8,128)(2,1)} %collective-permute-done.17, bf16[128,2048]{0,1:T(8,128)(2,1)S(1)} %bitcast.96), kind=kOutput, calls=%fused_computation.110 | convolution fusion | flops 262732288 | bytes 2833408 | tf_op jit(solution)/shard_map/dot_general | solution.py:225
  113.6 9.4 %collective-permute-done.15.refs_7_ = bf16[16,64,256]{2,1,0:T(8,128)(2,1)S(1)} collective-permute-done((bf16[16,64,256]{2,1,0:T(8,128)(2,1)S(1)}, bf16[16,64,256]{2,1,0:T(8,128)(2,1)S(1)}, u32[]{:S(2)}, u32[]{:S(2)}) %collective-permute-start.15) | collective-permute-done | bytes 524320 | tf_op jit(solution)/shard_map/ppermute | solution.py:48
  123.0 13.8 %collective-permute-done.9.refs_3_ = bf16[16,64,768]{2,1,0:T(8,128)(2,1)} collective-permute-done((bf16[16,64,768]{2,1,0:T(8,128)(2,1)S(1)}, bf16[16,64,768]{2,1,0:T(8,128)(2,1)}, u32[]{:S(2)}, u32[]{:S(2)}) %collective-permute-start.9) | collective-permute-done | bytes 1572896 | tf_op jit(solution)/shard_map/ppermute | solution.py:48
  136.9 18.2 %shard_map.104 = (f32[501,1024]{1,0:T(8,128)}, f32[501,1024]{1,0:T(8,128)}, f32[8,1024]{1,0:T(8,128)S(1)}) custom-call(s32[2,64]{1,0:T(2,128)S(1)} %add_select_fusion.table, f32[1,1024]{1,0:T(1,128)S(1)} %bitcast.91, bf16[16,64,768]{2,1,0:T(8,128)(2,1)S(1)} %bitcast.86, bf16[16,64,768]{2,1,0:T(8,128)(2,1)} %collective-permute-done.7.refs_1_, ...), custom_call_target="tpu_custom_call" | custom-call | flops 8405385216 | bytes 20701184 | tf_op jit(solution)/shard_map/pallas_call | solution.py:124
  155.4 10.7 %all_to_all.20 = f32[8,32,128]{2,1,0:T(8,128)S(1)} all-to-all(f32[8,32,128]{2,1,0:T(8,128)S(1)} %broadcast_in_dim.38), channel_id=1, replica_groups=mesh['variant'=8,'vocab'=16] {'variant'}, dimensions={0} | all-to-all | bytes 262144 | tf_op jit(solution)/shard_map/all_to_all | solution.py:257
  166.9 3.5 %all-to-all-start.2 = ((f32[16,32,128]{2,1,0:T(8,128)}), f32[16,32,128]{2,1,0:T(8,128)S(1)}, u32[]{:S(2)}, u32[]{:S(2)}) async-start(f32[16,32,128]{2,1,0:T(8,128)} %broadcast_in_dim.39), calls=%async_computation.2 | async-start | bytes 524288 | tf_op jit(solution)/shard_map/all_to_all | solution.py:259
  170.6 9.0 %all-to-all-done.2 = f32[16,32,128]{2,1,0:T(8,128)S(1)} async-done(((f32[16,32,128]{2,1,0:T(8,128)}), f32[16,32,128]{2,1,0:T(8,128)S(1)}, u32[]{:S(2)}, u32[]{:S(2)}) %all-to-all-start.2) | async-done | bytes 262176 | tf_op jit(solution)/shard_map/all_to_all | solution.py:259
  184.7 5.4 %all-to-all-start.3 = ((bf16[8,501,256]{2,1,0:T(8,128)(2,1)}), bf16[8,501,256]{2,1,0:T(8,128)(2,1)}, u32[]{:S(2)}, u32[]{:S(2)}) async-start(bf16[8,501,256]{2,1,0:T(8,128)(2,1)} %broadcast_in_dim.40), calls=%async_computation.3 | async-start | bytes 4128768 | tf_op jit(solution)/shard_map/all_to_all | solution.py:283
  191.8 26.4 %all-to-all-done.3 = bf16[8,501,256]{2,1,0:T(8,128)(2,1)} async-done(((bf16[8,501,256]{2,1,0:T(8,128)(2,1)}), bf16[8,501,256]{2,1,0:T(8,128)(2,1)}, u32[]{:S(2)}, u32[]{:S(2)}) %all-to-all-start.3) | async-done | bytes 2052128 | tf_op jit(solution)/shard_map/all_to_all | solution.py:283
  218.2 2.2 reshape.634
  220.4 2.7 %convolution_bitcast_fusion = f32[256,4008]{0,1:T(8,128)} fusion(bf16[4008,256]{1,0:T(8,128)(2,1)S(1)} %reshape.634, bf16[256,256]{1,0:T(8,128)(2,1)S(1)} %copy-done), kind=kOutput, calls=%fused_computation | convolution fusion | flops 525336576 | bytes 6287360 | tf_op jit(solution)/shard_map/dot_general | solution.py:286
  (130 shorter events, 44.7 us)
Async XLA Ops:
  6.0 48.8 %all-to-all-start = ((bf16[8,630,256]{2,1,0:T(8,128)(2,1)}), bf16[8,630,256]{2,1,0:T(8,128)(2,1)S(1)}, u32[]{:S(2)}, u32[]{:S(2)}) async-start(bf16[8,630,256]{2,1,0:T(8,128)(2,1)} %pad_maximum_fusion), calls=%async_computation | async-start | bytes 5177344 | tf_op jit(solution)/shard_map/all_to_all | solution.py:177
  12.4 124.4 %collective-permute-start.16 = (bf16[501,4096]{1,0:T(8,128)(2,1)}, bf16[501,4096]{1,0:T(8,128)(2,1)}, u32[]{:S(2)}, u32[]{:S(2)}) collective-permute-start(bf16[501,4096]{1,0:T(8,128)(2,1)} %bitcast.128), channel_id=1, source_target_pairs={{0,1},{1,0},{64,65},{65,64},{2,3},{3,2},{66,67},{67,66},{4,5},{5,4... | collective-permute-start | bytes 12312584 | tf_op jit(solution)/shard_map/ppermute | solution.py:43
  12.4 6.7 %collective-permute-start = (bf16[32,1024]{1,0:T(8,128)(2,1)S(1)}, bf16[32,1024]{1,0:T(8,128)(2,1)S(1)}, u32[]{:S(2)}, u32[]{:S(2)}) collective-permute-start(bf16[32,1024]{1,0:T(8,128)(2,1)S(1)} %bitcast.113), channel_id=1, source_target_pairs={{0,1},{1,0},{64,65},{65,64},{2,3},{3,2},{66,67},{67,66},{4,5},{5,4... | collective-permute-start | bytes 196616 | tf_op jit(solution)/shard_map/ppermute | solution.py:43
  19.2 21.7 %collective-permute-start.1 = (bf16[64,1024]{1,0:T(8,128)(2,1)S(1)}, bf16[64,1024]{1,0:T(8,128)(2,1)S(1)}, u32[]{:S(2)}, u32[]{:S(2)}) collective-permute-start(bf16[64,1024]{1,0:T(8,128)(2,1)S(1)} %maximum_select_fusion.2), channel_id=1, source_target_pairs={{0,64},{1,17},{64,2},{65,81},{2,66},{3,19},{66,0},{67,83},{4,68},{... | collective-permute-start | bytes 393224 | tf_op jit(solution)/shard_map/ppermute | solution.py:48
  20.7 22.5 %collective-permute-start.2 = (bf16[64,1024]{1,0:T(8,128)(2,1)S(1)}, bf16[64,1024]{1,0:T(8,128)(2,1)S(1)}, u32[]{:S(2)}, u32[]{:S(2)}) collective-permute-start(bf16[64,1024]{1,0:T(8,128)(2,1)S(1)} %maximum_select_fusion.2), channel_id=1, source_target_pairs={{0,66},{1,49},{64,0},{65,113},{2,64},{3,51},{66,2},{67,115},{4,70}... | collective-permute-start | bytes 393224 | tf_op jit(solution)/shard_map/ppermute | solution.py:48
  22.9 24.8 %collective-permute-start.3 = (bf16[64,1024]{1,0:T(8,128)(2,1)S(1)}, bf16[64,1024]{1,0:T(8,128)(2,1)S(1)}, u32[]{:S(2)}, u32[]{:S(2)}) collective-permute-start(bf16[64,1024]{1,0:T(8,128)(2,1)S(1)} %maximum_select_fusion.2), channel_id=1, source_target_pairs={{0,2},{1,33},{64,66},{65,97},{2,0},{3,35},{66,64},{67,99},{4,6},{5... | collective-permute-start | bytes 393224 | tf_op jit(solution)/shard_map/ppermute | solution.py:48
  47.7 17.2 %collective-permute-start.10 = (bf16[4,64,256]{2,1,0:T(8,128)(2,1)S(1)}, bf16[4,64,256]{2,1,0:T(8,128)(2,1)S(1)}, u32[]{:S(2)}, u32[]{:S(2)}) collective-permute-start(bf16[4,64,256]{2,1,0:T(8,128)(2,1)S(1)} %pad_maximum_fusion.4), channel_id=1, source_target_pairs={{0,16},{1,65},{64,80},{65,3},{2,18},{3,67},{66,82},{67,1},{4,20},{... | collective-permute-start | bytes 393224 | tf_op jit(solution)/shard_map/ppermute | solution.py:48
  48.1 17.4 %collective-permute-start.11 = (bf16[4,64,256]{2,1,0:T(8,128)(2,1)S(1)}, bf16[4,64,256]{2,1,0:T(8,128)(2,1)}, u32[]{:S(2)}, u32[]{:S(2)}) collective-permute-start(bf16[4,64,256]{2,1,0:T(8,128)(2,1)S(1)} %pad_maximum_fusion.4), channel_id=1, source_target_pairs={{0,48},{1,67},{64,112},{65,1},{2,50},{3,65},{66,114},{67,3},{4,52}... | collective-permute-start | bytes 393224 | tf_op jit(solution)/shard_map/ppermute | solution.py:48
  49.8 19.7 %collective-permute-start.12 = (bf16[4,64,256]{2,1,0:T(8,128)(2,1)S(1)}, bf16[4,64,256]{2,1,0:T(8,128)(2,1)}, u32[]{:S(2)}, u32[]{:S(2)}) collective-permute-start(bf16[4,64,256]{2,1,0:T(8,128)(2,1)S(1)} %pad_maximum_fusion.4), channel_id=1, source_target_pairs={{0,32},{1,3},{64,96},{65,67},{2,34},{3,1},{66,98},{67,65},{4,36},{... | collective-permute-start | bytes 393224 | tf_op jit(solution)/shard_map/ppermute | solution.py:48
  51.8 19.8 %collective-permute-start.5 = (bf16[4,64,768]{2,1,0:T(8,128)(2,1)}, bf16[4,64,768]{2,1,0:T(8,128)(2,1)}, u32[]{:S(2)}, u32[]{:S(2)}) collective-permute-start(bf16[4,64,768]{2,1,0:T(8,128)(2,1)} %get-tuple-element.23), channel_id=1, source_target_pairs={{0,12},{1,13},{64,76},{65,77},{2,14},{3,15},{66,78},{67,79},{4,0},... | collective-permute-start | bytes 1179656 | tf_op jit(solution)/shard_map/ppermute | solution.py:48
  64.9 10.5 %collective-permute-start.6 = (bf16[4,64,768]{2,1,0:T(8,128)(2,1)}, bf16[4,64,768]{2,1,0:T(8,128)(2,1)S(1)}, u32[]{:S(2)}, u32[]{:S(2)}) collective-permute-start(bf16[4,64,768]{2,1,0:T(8,128)(2,1)} %get-tuple-element.23), channel_id=1, source_target_pairs={{0,8},{1,9},{64,72},{65,73},{2,10},{3,11},{66,74},{67,75},{4,12},{... | collective-permute-start | bytes 1179656 | tf_op jit(solution)/shard_map/ppermute | solution.py:48
  65.5 42.4 %collective-permute-start.17 = (bf16[501,2048]{1,0:T(8,128)(2,1)}, bf16[501,2048]{1,0:T(8,128)(2,1)}, u32[]{:S(2)}, u32[]{:S(2)}) collective-permute-start(bf16[501,2048]{1,0:T(8,128)(2,1)} %copy.53), channel_id=1, source_target_pairs={{0,1},{1,0},{64,65},{65,64},{2,3},{3,2},{66,67},{67,66},{4,5},{5,4... | collective-permute-start | bytes 6156296 | tf_op jit(solution)/shard_map/ppermute | solution.py:43
  69.5 17.6 %collective-permute-start.4 = (bf16[4,64,768]{2,1,0:T(8,128)(2,1)}, bf16[4,64,768]{2,1,0:T(8,128)(2,1)S(1)}, u32[]{:S(2)}, u32[]{:S(2)}) collective-permute-start(bf16[4,64,768]{2,1,0:T(8,128)(2,1)} %get-tuple-element.23), channel_id=1, source_target_pairs={{0,4},{1,5},{64,68},{65,69},{2,6},{3,7},{66,70},{67,71},{4,8},{5,9... | collective-permute-start | bytes 1179656 | tf_op jit(solution)/shard_map/ppermute | solution.py:48
  70.6 32.3 %copy-start.10 = (s32[8]{0:T(128)S(1)}, s32[8]{0:T(128)}, u32[]{:S(2)}) copy-start(s32[8]{0:T(128)} %param.11) | copy-start | bytes 100
  71.6 26.6 %collective-permute-start.13 = (bf16[16,64,256]{2,1,0:T(8,128)(2,1)S(1)}, bf16[16,64,256]{2,1,0:T(8,128)(2,1)S(1)}, u32[]{:S(2)}, u32[]{:S(2)}) collective-permute-start(bf16[16,64,256]{2,1,0:T(8,128)(2,1)S(1)} %bitcast.87), channel_id=1, source_target_pairs={{0,4},{1,5},{64,68},{65,69},{2,6},{3,7},{66,70},{67,71},{4,8},{5,9... | collective-permute-start | bytes 1572872 | tf_op jit(solution)/shard_map/ppermute | solution.py:48
  75.4 24.3 %collective-permute-start.14 = (bf16[16,64,256]{2,1,0:T(8,128)(2,1)S(1)}, bf16[16,64,256]{2,1,0:T(8,128)(2,1)S(1)}, u32[]{:S(2)}, u32[]{:S(2)}) collective-permute-start(bf16[16,64,256]{2,1,0:T(8,128)(2,1)S(1)} %bitcast.88), channel_id=1, source_target_pairs={{0,12},{1,13},{64,76},{65,77},{2,14},{3,15},{66,78},{67,79},{4,0},... | collective-permute-start | bytes 1572872 | tf_op jit(solution)/shard_map/ppermute | solution.py:48
  88.3 34.7 %collective-permute-start.7 = (bf16[16,64,768]{2,1,0:T(8,128)(2,1)S(1)}, bf16[16,64,768]{2,1,0:T(8,128)(2,1)}, u32[]{:S(2)}, u32[]{:S(2)}) collective-permute-start(bf16[16,64,768]{2,1,0:T(8,128)(2,1)S(1)} %bitcast.83), channel_id=1, source_target_pairs={{0,16},{1,65},{64,80},{65,3},{2,18},{3,67},{66,82},{67,1},{4,20},{... | collective-permute-start | bytes 4718600 | tf_op jit(solution)/shard_map/ppermute | solution.py:48
  98.3 24.7 %collective-permute-start.8 = (bf16[16,64,768]{2,1,0:T(8,128)(2,1)S(1)}, bf16[16,64,768]{2,1,0:T(8,128)(2,1)}, u32[]{:S(2)}, u32[]{:S(2)}) collective-permute-start(bf16[16,64,768]{2,1,0:T(8,128)(2,1)S(1)} %bitcast.84), channel_id=1, source_target_pairs={{0,48},{1,67},{64,112},{65,1},{2,50},{3,65},{66,114},{67,3},{4,52}... | collective-permute-start | bytes 4718600 | tf_op jit(solution)/shard_map/ppermute | solution.py:48
  100.6 36.2 %collective-permute-start.9 = (bf16[16,64,768]{2,1,0:T(8,128)(2,1)S(1)}, bf16[16,64,768]{2,1,0:T(8,128)(2,1)}, u32[]{:S(2)}, u32[]{:S(2)}) collective-permute-start(bf16[16,64,768]{2,1,0:T(8,128)(2,1)S(1)} %bitcast.85), channel_id=1, source_target_pairs={{0,32},{1,3},{64,96},{65,67},{2,34},{3,1},{66,98},{67,65},{4,36},{... | collective-permute-start | bytes 4718600 | tf_op jit(solution)/shard_map/ppermute | solution.py:48
  108.0 15.0 %collective-permute-start.15 = (bf16[16,64,256]{2,1,0:T(8,128)(2,1)S(1)}, bf16[16,64,256]{2,1,0:T(8,128)(2,1)S(1)}, u32[]{:S(2)}, u32[]{:S(2)}) collective-permute-start(bf16[16,64,256]{2,1,0:T(8,128)(2,1)S(1)} %bitcast.89), channel_id=1, source_target_pairs={{0,8},{1,9},{64,72},{65,73},{2,10},{3,11},{66,74},{67,75},{4,12},{... | collective-permute-start | bytes 1572872 | tf_op jit(solution)/shard_map/ppermute | solution.py:48
  166.9 12.7 %all-to-all-start.2 = ((f32[16,32,128]{2,1,0:T(8,128)}), f32[16,32,128]{2,1,0:T(8,128)S(1)}, u32[]{:S(2)}, u32[]{:S(2)}) async-start(f32[16,32,128]{2,1,0:T(8,128)} %broadcast_in_dim.39), calls=%async_computation.2 | async-start | bytes 524288 | tf_op jit(solution)/shard_map/all_to_all | solution.py:259
  181.8 1.4 collective-permute-start.19
  184.7 33.5 %all-to-all-start.3 = ((bf16[8,501,256]{2,1,0:T(8,128)(2,1)}), bf16[8,501,256]{2,1,0:T(8,128)(2,1)}, u32[]{:S(2)}, u32[]{:S(2)}) async-start(bf16[8,501,256]{2,1,0:T(8,128)(2,1)} %broadcast_in_dim.40), calls=%async_computation.3 | async-start | bytes 4128768 | tf_op jit(solution)/shard_map/all_to_all | solution.py:283
  190.1 1.1 collective-permute-start.18
  (10 other events, 124.8 us)

commit v2 on v1

--- a/solution.py
+++ b/solution.py
@@ -1,4 +1,4 @@
-import functools
+import math
 import jax
 import jax.numpy as jnp
 from jax import lax
@@ -12,6 +12,7 @@
 AXES = ("variant", "vocab")
 SIDE = 4
 SPLIT = 768
+ROWS = 640
 OFFSETS = (0, -1, 1, 2)
 
 
@@ -49,6 +50,122 @@
     ]
 
 
+def pack_kernel(*refs):
+    blocks, first_ref, second_ref = refs[0:4], refs[5], refs[6]
+    for i, block in enumerate(blocks):
+        first_ref[i] = block[:, :SPLIT]
+        second_ref[i] = block[:, SPLIT:]
+
+
+def pack(blocks, after):
+    vmem = pl.BlockSpec(memory_space=pltpu.VMEM)
+    rows, lanes = blocks[0].shape
+    return pl.pallas_call(
+        pack_kernel,
+        out_shape=[
+            jax.ShapeDtypeStruct((4, rows, SPLIT), jnp.bfloat16),
+            jax.ShapeDtypeStruct((4, rows, lanes - SPLIT), jnp.bfloat16),
+        ],
+        in_specs=[vmem] * 4 + [pl.BlockSpec(memory_space=pl.ANY)],
+        out_specs=[vmem] * 2,
+        cost_estimate=pl.CostEstimate(
+            flops=0, bytes_accessed=16 * rows * lanes, transcendentals=0
+        ),
+    )(*blocks, after)
+
+
+def stack_kernel(*refs):
+    for part in range(2):
+        for i in range(4):
+            refs[8 + part][i] = refs[4 * part + i][...]
+
+
+def stack_parts(first, second):
+    vmem = pl.BlockSpec(memory_space=pltpu.VMEM)
+    shapes = [(4,) + group[0].shape for group in (first, second)]
+    return pl.pallas_call(
+        stack_kernel,
+        out_shape=[jax.ShapeDtypeStruct(shape, jnp.bfloat16) for shape in shapes],
+        in_specs=[vmem] * 8,
+        out_specs=[vmem] * 2,
+        cost_estimate=pl.CostEstimate(
+            flops=0, bytes_accessed=4 * sum(math.prod(shape) for shape in shapes), transcendentals=0
+        ),
+    )(*first, *second)
+
+
+def halves_kernel(before, after, *refs):
+    before_half, after_half = refs[-4:-2]
+    before_half[...] = before[...]
+    after_half[...] = after[...]
+
+
+def forward_halves(before, after, through, others):
+    n, rows, lanes = before.shape
+    block = (n // 2, rows, lanes)
+    hbm = pl.BlockSpec(memory_space=pl.ANY)
+    lower = pl.BlockSpec(block, lambda i: (0, 0, 0))
+    return pl.pallas_call(
+        halves_kernel,
+        grid=(1,),
+        out_shape=[jax.ShapeDtypeStruct(block, before.dtype)] * 2
+        + [jax.ShapeDtypeStruct(t.shape, t.dtype) for t in through],
+        in_specs=[lower, pl.BlockSpec(block, lambda i: (1, 0, 0))] + [hbm] * (2 + len(others)),
+        out_specs=[lower, lower, hbm, hbm],
+        input_output_aliases={2: 2, 3: 3},
+        cost_estimate=pl.CostEstimate(
+            flops=0, bytes_accessed=4 * n * rows * lanes, transcendentals=0
+        ),
+    )(before, after, *through, *others)
+
+
+def student_kernel(own_ref, other_ref, ids_ref, base_ref, l_own, l_other, stat_ref):
+    half, cols = l_own.shape[1], l_own.shape[0]
+    dims = (((1,), (1,)), ((), ()))
+    logits = []
+    for ref, out in ((own_ref, l_own), (other_ref, l_other)):
+        total = jnp.zeros((cols, half), jnp.float32)
+        for block in range(8):
+            total += lax.dot_general(
+                ref[block, half : half + cols, :],
+                own_ref[block, :half, :],
+                dims,
+                preferred_element_type=jnp.float32,
+            )
+        out[...] = total
+        logits.append(total)
+    top = jnp.maximum(
+        jnp.max(logits[0], axis=0, keepdims=True), jnp.max(logits[1], axis=0, keepdims=True)
+    )
+    total = jnp.zeros((1, half), jnp.float32)
+    hard = jnp.zeros((1, half), jnp.float32)
+    rows = lax.broadcasted_iota(jnp.int32, (cols, half), 0)
+    for i in range(2):
+        total += jnp.sum(jnp.exp(logits[i] - top), axis=0, keepdims=True)
+        hit = rows + base_ref[i] == ids_ref[...]
+        hard += jnp.sum(jnp.where(hit, logits[i], 0.0), axis=0, keepdims=True)
+    stat_ref[...] = jnp.concatenate([top, total, hard, jnp.zeros((5, half), jnp.float32)])
+
+
+def student_logits(own, other, ids, base, cols):
+    half = ids.shape[1]
+    vmem = pl.BlockSpec(memory_space=pltpu.VMEM)
+    return pl.pallas_call(
+        student_kernel,
+        out_shape=[
+            jax.ShapeDtypeStruct((cols, half), jnp.float32),
+            jax.ShapeDtypeStruct((cols, half), jnp.float32),
+            jax.ShapeDtypeStruct((8, half), jnp.float32),
+        ],
+        in_specs=[vmem] * 3 + [pl.BlockSpec(memory_space=pltpu.SMEM)],
+        out_specs=[vmem] * 3,
+        compiler_params=pltpu.CompilerParams(vmem_limit_bytes=24 << 20),
+        cost_estimate=pl.CostEstimate(
+            flops=2 * 2 * cols * half * 2048, bytes_accessed=12 << 20, transcendentals=2 * cols * half
+        ),
+    )(own, other, ids, base)
+
+
 def ordered(core, own, other, axis):
     return jnp.where(
         core == 0,
@@ -58,34 +175,38 @@
 
 
 def teacher_kernel(table, inv_tau, *refs):
-    first, second = refs[0:4], refs[4:8]
-    w_refs, l_refs = refs[8:10], refs[10:12]
-    e_refs, stat_ref = refs[12:14], refs[14]
-    hidden, w_own, w_sib, sem = refs[15:19]
+    first, second = refs[0:5], refs[5:9]
+    w_refs, l_refs = refs[9:11], refs[11:13]
+    e_refs, stat_ref = refs[13:15], refs[15]
+    hidden, w_own, w_sib, sem = refs[16:20]
     w_bufs = (w_own, w_sib)
     copies = [pltpu.make_async_copy(w_refs[i], w_bufs[i], sem.at[i]) for i in range(2)]
     for copy in copies:
         copy.start()
 
-    def chunk_copy(part, ref, s3, n, lanes):
-        row = pl.multiple_of(table[part, s3 * 16 + n] * 64, 64)
+    def chunk_copy(part, ref, base, n, lanes):
+        row = pl.multiple_of(table[part, base + n] * 64, 64)
         return pltpu.make_async_copy(
             ref.at[n], hidden.at[pl.ds(row, 64), lanes], sem.at[2 + part]
         )
 
     parts = ((first, pl.ds(0, SPLIT)), (second, pl.ds(SPLIT, 1024 - SPLIT)))
+    blocks = []
     for part, (group, lanes) in enumerate(parts):
-        for s3 in range(4):
-            def start(n, _, part=part, ref=group[s3], s3=s3, lanes=lanes):
-                chunk_copy(part, ref, s3, n, lanes).start()
-                return 0
-            lax.fori_loop(0, 16, start, 0)
-    for part, (group, lanes) in enumerate(parts):
-        for s3 in range(4):
-            def wait(n, _, part=part, ref=group[s3], s3=s3, lanes=lanes):
-                chunk_copy(part, ref, s3, n, lanes).wait()
-                return 0
-            lax.fori_loop(0, 16, wait, 0)
+        base = 0
+        for ref in group:
+            blocks.append((part, ref, base, lanes))
+            base += ref.shape[0]
+    for part, ref, base, lanes in blocks:
+        def start(n, _, part=part, ref=ref, base=base, lanes=lanes):
+            chunk_copy(part, ref, base, n, lanes).start()
+            return 0
+        lax.fori_loop(0, ref.shape[0], start, 0)
+    for part, ref, base, lanes in blocks:
+        def wait(n, _, part=part, ref=ref, base=base, lanes=lanes):
+            chunk_copy(part, ref, base, n, lanes).wait()
+            return 0
+        lax.fori_loop(0, ref.shape[0], wait, 0)
     for copy in copies:
         copy.wait()
 
@@ -128,7 +249,7 @@
             jax.ShapeDtypeStruct((cols, 1024), jnp.float32),
             jax.ShapeDtypeStruct((8, 1024), jnp.float32),
         ],
-        in_specs=[pl.BlockSpec(memory_space=pltpu.SMEM), vmem] + [hbm] * 10 + [vmem] * 2,
+        in_specs=[pl.BlockSpec(memory_space=pltpu.SMEM), vmem] + [hbm] * 11 + [vmem] * 2,
         out_specs=[vmem] * 3,
         scratch_shapes=[
             pltpu.VMEM((width, 1024), jnp.bfloat16),
@@ -162,28 +283,6 @@
     cols = teacher_weight.shape[1]
     half = 128
 
-    meta = jnp.concatenate(
-        [token_ids // 256, token_ids % 256, loss_mask, jnp.zeros((160,), jnp.int32)]
-    ).astype(jnp.bfloat16)[None, None]
-    mine = lax.dynamic_slice_in_dim(student_hidden, core * half, half, axis=0)
-    send = jnp.concatenate(
-        [
-            jnp.broadcast_to(mine[None], (8, half, 256)),
-            student_weight.T.reshape(8, cols, 256),
-            jnp.broadcast_to(meta, (8, 1, 256)),
-        ],
-        axis=1,
-    )
-    got = lax.all_to_all(send, "variant", 0, 0, tiled=True)
-    flat = jnp.transpose(got, (1, 0, 2)).reshape(half + cols + 1, 2048)
-    hs, ws = flat[:half], flat[half : half + cols]
-    ws_other = sibling(ws)
-    meta_all = got[:, half + cols]
-    ids = (meta_all[:, 0:32].astype(jnp.int32) * 256 + meta_all[:, 32:64].astype(jnp.int32)).reshape(256)
-    maskf = meta_all[:, 64:96].astype(jnp.float32).reshape(256)
-    ids_half = lax.dynamic_slice_in_dim(ids, core * half, half)
-    mask_half = lax.dynamic_slice_in_dim(maskf, core * half, half)
-
     halves = [
         lax.dynamic_slice_in_dim(teacher_hidden, start * half, half, axis=1)
         .transpose(2, 0, 1)
@@ -193,11 +292,46 @@
     unit = ordered(core, halves[0], sibling(halves[1]), 0)
     w_own = teacher_weight.T
     w_other = sibling(w_own)
-    stage1 = jnp.stack(ring_gather(unit, "zx"))
-    first = jnp.stack(ring_gather(stage1[:, :, :SPLIT], "yy")).reshape(16, 64, SPLIT)
-    second = jnp.stack(ring_gather(stage1[:, :, SPLIT:], "xz")).reshape(16, 64, 1024 - SPLIT)
-    first = ring_gather(first, "xz")
-    second = ring_gather(second, "yy")
+    first, second = pack(ring_gather(unit, "zx"), w_other)
+
+    meta = jnp.concatenate(
+        [token_ids // 256, token_ids % 256, loss_mask, jnp.zeros((32,), jnp.int32)]
+    ).astype(jnp.bfloat16)
+    meta = jnp.concatenate([meta, first[0, 0, :128]])[None, None]
+    mine = lax.dynamic_slice_in_dim(student_hidden, core * half, half, axis=0)
+    send = jnp.concatenate(
+        [
+            jnp.broadcast_to(mine[None], (8, half, 256)),
+            student_weight.T.reshape(8, cols, 256),
+            jnp.broadcast_to(meta, (8, ROWS - half - cols, 256)),
+        ],
+        axis=1,
+    )
+    got = lax.all_to_all(send, "variant", 0, 0, tiled=True)
+
+    first, second = stack_parts(ring_gather(first, "yy"), ring_gather(second, "xz"))
+    first = first.reshape(16, 64, SPLIT)
+    second = second.reshape(16, 64, 1024 - SPLIT)
+    plus, minus = ring_shift("xz", 1), ring_shift("xz", -1)
+    before = lax.ppermute(first, AXES, plus)
+    after = lax.ppermute(first, AXES, minus)
+    near = [lax.ppermute(second, AXES, ring_shift("yy", step)) for step in (1, -1)]
+    lower, upper, got, second = forward_halves(before, after, (got, second), near)
+    second = [second] + near + [lax.ppermute(second, AXES, ring_shift("yy", 2))]
+    first = [
+        first,
+        before,
+        after,
+        lax.ppermute(lower, AXES, plus),
+        lax.ppermute(upper, AXES, minus),
+    ]
+
+    got_other = sibling(got)
+    meta_all = got[:, half + cols]
+    ids = (meta_all[:, 0:32].astype(jnp.int32) * 256 + meta_all[:, 32:64].astype(jnp.int32)).reshape(256)
+    maskf = meta_all[:, 64:96].astype(jnp.float32).reshape(256)
+    ids_half = lax.dynamic_slice_in_dim(ids, core * half, half)
+    mask_half = lax.dynamic_slice_in_dim(maskf, core * half, half)
 
     offsets = jnp.array(OFFSETS, jnp.int32)
     o1, o2, o3 = (
@@ -220,17 +354,11 @@
     )
     inv_tau = jnp.repeat(1.0 / taus, half)[None]
 
-    dims = (((1,), (1,)), ((), ()))
-    logits = [
-        lax.dot_general(w, hs, dims, preferred_element_type=jnp.float32) for w in (ws, ws_other)
-    ]
-    s_top = jnp.maximum(jnp.max(logits[0], axis=0), jnp.max(logits[1], axis=0))
-    s_sum = sum(jnp.sum(jnp.exp(l - s_top), axis=0) for l in logits)
+    base = jnp.stack([(b * 8 + a) * cols, ((b + 1 - 2 * core) * 8 + a) * cols])
+    l_own, l_other, s_stats = student_logits(got, got_other, ids_half[None], base, cols)
+    logits = (l_own, l_other)
     rows = jnp.arange(cols, dtype=jnp.int32)[:, None]
-    onehots = [
-        (block * 8 + a) * cols + rows == ids_half[None, :] for block in (b, b + 1 - 2 * core)
-    ]
-    s_hard = sum(jnp.sum(jnp.where(o, l, 0.0), axis=0) for o, l in zip(onehots, logits))
+    onehots = [base[i] + rows == ids_half[None, :] for i in range(2)]
 
     e_own, e_other, stats = teacher_scores(
         table, inv_tau, first, second, (w_own, w_other), logits
@@ -238,7 +366,7 @@
     e = (e_own, e_other)
     t_stats = stats[:3].reshape(24, half)
     packed = jnp.concatenate(
-        [t_stats, jnp.stack([s_top, s_sum, s_hard]), jnp.zeros((5, half), jnp.float32)]
+        [t_stats, s_stats]
     )
     def merge(g):
         n = g.shape[0]

time: 226 us -> 208 us (0.920)
  waiting for transfers between devices: 111 us -> 97.2 us
  starting transfers between devices: 41.6 us -> 53.7 us
  blocking collectives: 10.7 us -> 0 us
  Pallas kernels: 18.2 us -> 27.2 us
  local copies, waits for them, and re-layouts: 24.7 us -> 17.6 us
  matrix products: 7.41 us -> 2.68 us
  other arithmetic: 8.83 us -> 6.14 us
    ppermute x15 -> x9, waiting for transfers between devices: 66.9 us -> 27 us  [ring_gather(): lax.ppermute(value, AXES, ring_shift(axes, step))]
    ppermute x0 -> x7, waiting for transfers between devices: none -> 21.5 us  [the longest x2 12 us: on_device(): lax.ppermute(second, AXES, ring_shift('yy', step))]
    slice x5 -> x0, local copies, waits for them, and re-layouts: 13.4 us -> none  [on_device(): hs, ws = (flat[:half], flat[half:half + cols])]
    ppermute x0 -> x7, starting transfers between devices: none -> 11.3 us  [the longest x2 3.24 us: on_device(): lax.ppermute(second, AXES, ring_shift('yy', step))]
    all_to_all x1 -> x0, blocking collectives: 10.7 us -> none  [on_device(): by_variant = merge(lax.all_to_all(tile8, 'variant', 0, 0, tiled=True))]
    pallas_call x0 -> x4, Pallas kernels: none -> 9.38 us  [the longest x1 2.95 us: stack_parts(): pl.pallas_call(stack_kernel, out_shape=[jax.ShapeDtypeStruct(shape, jnp.b...]
    all_to_all x0 -> x1, starting transfers between devices: none -> 8.1 us  [on_device(): by_variant = merge(lax.all_to_all(tile8, 'variant', 0, 0, tiled=True))]
    ppermute x15 -> x9, starting transfers between devices: 21.7 us -> 14.9 us  [ring_gather(): lax.ppermute(value, AXES, ring_shift(axes, step))]
  transfers between devices with their start and end apart: 23 -> 25, of which waited for: 13 -> 13; matrix products, arithmetic and copies ran while one was open for 11% -> 4% of each run, Pallas kernels for 0% -> 2%
where the time goes in v2:
time: 208 us; the launch traced here: 206 us
  waiting for transfers between devices  97.2 us (47%)
  starting transfers between devices  53.7 us (26%)
  Pallas kernels  27.2 us (13%)
  local copies, waits for them, and re-layouts  17.6 us (8%)
  other arithmetic  6.14 us (3%)
  matrix products  2.68 us (1%)
    ppermute x9, waiting for transfers between devices, ring_gather(): lax.ppermute(value, AXES, ring_shift(axes, step))  27 us
    all_to_all x1, waiting for transfers between devices, on_device(): lax.all_to_all(jnp.broadcast_to(error[None], (8, cols, 256)), 'variant',...  26.4 us
    pallas_call x1, Pallas kernels, teacher_scores(): pl.pallas_call(teacher_kernel, out_shape=[jax.ShapeDtypeStruct((cols, 102...  17.8 us
    ppermute x9, starting transfers between devices, ring_gather(): lax.ppermute(value, AXES, ring_shift(axes, step))  14.9 us
    ppermute x2, waiting for transfers between devices, on_device(): lax.ppermute(second, AXES, ring_shift('yy', step))  12 us
    all_to_all x1, waiting for transfers between devices, on_device(): lax.all_to_all(tile16, 'vocab', 0, 0, tiled=True).reshape(8, 2, 32, half)  8.94 us
    all_to_all x1, starting transfers between devices, on_device(): lax.all_to_all(tile16, 'vocab', 0, 0, tiled=True).reshape(8, 2, 32, half)  8.15 us
    all_to_all x1, starting transfers between devices, on_device(): by_variant = merge(lax.all_to_all(tile8, 'variant', 0, 0, tiled=True))  8.1 us
  transfers between devices with their start and end apart: 25, of which 13 were waited for; matrix products, arithmetic and copies ran while one was open for 4% of the time, Pallas kernels for 2%

profile of v2, /device:TPU:2, one launch (start us, length us, event | category | flops | bytes accessed | tf_op | source)
XLA Modules:
  0.0 205.6 jit_solution(8232985789253740263)
XLA Ops:
  2.2 5.6 %collective-permute-done = bf16[32,1024]{1,0:T(8,128)(2,1)S(1)} collective-permute-done((bf16[32,1024]{1,0:T(8,128)(2,1)S(1)}, bf16[32,1024]{1,0:T(8,128)(2,1)S(1)}, u32[]{:S(2)}, u32[]{:S(2)}) %collective-permute-start) | collective-permute-done | bytes 65568 | tf_op jit(solution)/shard_map/ppermute | solution.py:44
  9.9 2.2 %collective-permute-start.2 = (bf16[64,1024]{1,0:T(8,128)(2,1)S(1)}, bf16[64,1024]{1,0:T(8,128)(2,1)S(1)}, u32[]{:S(2)}, u32[]{:S(2)}) collective-permute-start(bf16[64,1024]{1,0:T(8,128)(2,1)S(1)} %maximum_select_fusion.1.refs_0_), channel_id=1, source_target_pairs={{0,66},{1,49},{64,0},{65,113},{2,64},{3,51},{66,2},{67,115},{4,70}... | collective-permute-start | bytes 393224 | tf_op jit(solution)/shard_map/ppermute | solution.py:49
  15.2 2.2 %reshape.504 = bf16[8,501,256]{2,1,0:T(8,128)(2,1)S(1)} reshape(bf16[4008,256]{1,0:T(8,128)(2,1)} %bitcast.69) | data formatting | bytes 4104192 | tf_op jit(solution)/shard_map/reshape | solution.py:305
  23.7 5.1 %all-to-all-start = ((bf16[8,640,256]{2,1,0:T(8,128)(2,1)}), bf16[8,640,256]{2,1,0:T(8,128)(2,1)S(1)}, u32[]{:S(2)}, u32[]{:S(2)}) async-start(bf16[8,640,256]{2,1,0:T(8,128)(2,1)} %pad_maximum_fusion), calls=%async_computation | async-start | bytes 5242880 | tf_op jit(solution)/shard_map/all_to_all | solution.py:310
  34.0 2.1 %collective-permute-start.10 = (bf16[4,64,256]{2,1,0:T(8,128)(2,1)}, bf16[4,64,256]{2,1,0:T(8,128)(2,1)S(1)}, u32[]{:S(2)}, u32[]{:S(2)}) collective-permute-start(bf16[4,64,256]{2,1,0:T(8,128)(2,1)} %get-tuple-element.17.refs_4_), channel_id=1, source_target_pairs={{0,32},{1,3},{64,96},{65,67},{2,34},{3,1},{66,98},{67,65},{4,36},{... | collective-permute-start | bytes 393224 | tf_op jit(solution)/shard_map/ppermute | solution.py:49
  36.1 22.3 %collective-permute-done.10.refs_7_ = bf16[4,64,256]{2,1,0:T(8,128)(2,1)S(1)} collective-permute-done((bf16[4,64,256]{2,1,0:T(8,128)(2,1)}, bf16[4,64,256]{2,1,0:T(8,128)(2,1)S(1)}, u32[]{:S(2)}, u32[]{:S(2)}) %collective-permute-start.10) | collective-permute-done | bytes 131104 | tf_op jit(solution)/shard_map/ppermute | solution.py:49
  60.0 3.6 %collective-permute-done.9.refs_6_ = bf16[4,64,256]{2,1,0:T(8,128)(2,1)S(1)} collective-permute-done((bf16[4,64,256]{2,1,0:T(8,128)(2,1)}, bf16[4,64,256]{2,1,0:T(8,128)(2,1)S(1)}, u32[]{:S(2)}, u32[]{:S(2)}) %collective-permute-start.9) | collective-permute-done | bytes 131104 | tf_op jit(solution)/shard_map/ppermute | solution.py:49
  65.0 2.9 %shard_map.105 = (bf16[4,4,64,768]{3,2,1,0:T(8,128)(2,1)}, bf16[4,4,64,256]{3,2,1,0:T(8,128)(2,1)}) custom-call(bf16[4,64,768]{2,1,0:T(8,128)(2,1)} %get-tuple-element.16.refs_0_, bf16[4,64,768]{2,1,0:T(8,128)(2,1)} %copy-done.14, bf16[4,64,768]{2,1,0:T(8,128)(2,1)} %copy-done.15, bf16[4,64,768]{2,1,0:T(8,128)(2,1)} %collective-permute-done.7.refs_3_, ...), custom_call_target="tpu_custom_call" | custom-call | bytes 4194304 | tf_op jit(solution)/shard_map/pallas_call | solution.py:86
  67.9 2.0 collective-permute-start.12
  73.2 12.0 %collective-permute-done.13.refs_2_.refs_6_ = bf16[16,64,256]{2,1,0:T(8,128)(2,1)S(1)} collective-permute-done((bf16[16,64,256]{2,1,0:T(8,128)(2,1)}, bf16[16,64,256]{2,1,0:T(8,128)(2,1)S(1)}, u32[]{:S(2)}, u32[]{:S(2)}) %collective-permute-start.13) | collective-permute-done | bytes 524320 | tf_op jit(solution)/shard_map/ppermute | solution.py:318
  85.2 3.4 %collective-permute-done.11.before.refs_1_ = bf16[16,64,768]{2,1,0:T(8,128)(2,1)S(1)} collective-permute-done((bf16[16,64,768]{2,1,0:T(8,128)(2,1)}, bf16[16,64,768]{2,1,0:T(8,128)(2,1)S(1)}, u32[]{:S(2)}, u32[]{:S(2)}) %collective-permute-start.11) | collective-permute-done | bytes 1572896 | tf_op jit(solution)/shard_map/ppermute | solution.py:316
  91.4 2.6 %shard_map.106 = (bf16[8,64,768]{2,1,0:T(8,128)(2,1)}, bf16[8,64,768]{2,1,0:T(8,128)(2,1)}, bf16[8,640,256]{2,1,0:T(8,128)(2,1)}, bf16[16,64,256]{2,1,0:T(8,128)(2,1)}) custom-call(bf16[16,64,768]{2,1,0:T(8,128)(2,1)} %copy-done.3, bf16[16,64,768]{2,1,0:T(8,128)(2,1)} %collective-permute-done.12.after.refs_2_, ...), custom_call_target="tpu_custom_call", output_to_operand_aliasing={{2}: (2, {}), {3}: (3, {})} | custom-call | bytes 3145728 | tf_op jit(solution)/shard_map/pallas_call | solution.py:108
  94.4 2.1 %collective-permute-start.15 = (bf16[8,64,768]{2,1,0:T(8,128)(2,1)}, bf16[8,64,768]{2,1,0:T(8,128)(2,1)}, u32[]{:S(2)}, u32[]{:S(2)}) collective-permute-start(bf16[8,64,768]{2,1,0:T(8,128)(2,1)} %get-tuple-element.21), channel_id=1, source_target_pairs={{0,16},{1,65},{64,80},{65,3},{2,18},{3,67},{66,82},{67,1},{4,20},{... | collective-permute-start | bytes 2359304 | tf_op jit(solution)/shard_map/ppermute | solution.py:325
  97.2 3.2 %collective-permute-start.17 = (bf16[16,64,256]{2,1,0:T(8,128)(2,1)}, bf16[16,64,256]{2,1,0:T(8,128)(2,1)}, u32[]{:S(2)}, u32[]{:S(2)}) collective-permute-start(bf16[16,64,256]{2,1,0:T(8,128)(2,1)} %get-tuple-element.23.refs_5_), channel_id=1, source_target_pairs={{0,8},{1,9},{64,72},{65,73},{2,10},{3,11},{66,74},{67,75},{4,12},{... | collective-permute-start | bytes 1572872 | tf_op jit(solution)/shard_map/ppermute | solution.py:320
  105.6 5.9 %collective-permute-done.17.refs_8_ = bf16[16,64,256]{2,1,0:T(8,128)(2,1)} collective-permute-done((bf16[16,64,256]{2,1,0:T(8,128)(2,1)}, bf16[16,64,256]{2,1,0:T(8,128)(2,1)}, u32[]{:S(2)}, u32[]{:S(2)}) %collective-permute-start.17) | collective-permute-done | bytes 524320 | tf_op jit(solution)/shard_map/ppermute | solution.py:320
  111.6 17.8 %shard_map.108 = (f32[501,1024]{1,0:T(8,128)}, f32[501,1024]{1,0:T(8,128)}, f32[8,1024]{1,0:T(8,128)S(1)}) custom-call(s32[2,64]{1,0:T(2,128)S(1)} %add_select_fusion.table, f32[1,1024]{1,0:T(1,128)S(1)} %bitcast.65, bf16[16,64,768]{2,1,0:T(8,128)(2,1)S(1)} %bitcast.68, bf16[16,64,768]{2,1,0:T(8,128)(2,1)S(1)} %copy-done.4, ...), custom_call_target="tpu_custom_call" | custom-call | flops 8405385216 | bytes 20701184 | tf_op jit(solution)/shard_map/pallas_call | solution.py:245
  130.1 8.1 %all-to-all-start.1 = ((f32[8,32,128]{2,1,0:T(8,128)}), f32[8,32,128]{2,1,0:T(8,128)S(1)}, u32[]{:S(2)}, u32[]{:S(2)}) async-start(f32[8,32,128]{2,1,0:T(8,128)} %broadcast_in_dim.34), calls=%async_computation.1 | async-start | bytes 262144 | tf_op jit(solution)/shard_map/all_to_all | solution.py:385
  138.2 5.7 %all-to-all-done.1 = f32[8,32,128]{2,1,0:T(8,128)S(1)} async-done(((f32[8,32,128]{2,1,0:T(8,128)}), f32[8,32,128]{2,1,0:T(8,128)S(1)}, u32[]{:S(2)}, u32[]{:S(2)}) %all-to-all-start.1) | async-done | bytes 131104 | tf_op jit(solution)/shard_map/all_to_all | solution.py:385
  144.8 8.2 %all-to-all-start.2 = ((f32[16,32,128]{2,1,0:T(8,128)}), f32[16,32,128]{2,1,0:T(8,128)S(1)}, u32[]{:S(2)}, u32[]{:S(2)}) async-start(f32[16,32,128]{2,1,0:T(8,128)} %broadcast_in_dim.36), calls=%async_computation.2 | async-start | bytes 524288 | tf_op jit(solution)/shard_map/all_to_all | solution.py:387
  153.2 8.9 %all-to-all-done.2 = f32[16,32,128]{2,1,0:T(8,128)S(1)} async-done(((f32[16,32,128]{2,1,0:T(8,128)}), f32[16,32,128]{2,1,0:T(8,128)S(1)}, u32[]{:S(2)}, u32[]{:S(2)}) %all-to-all-start.2) | async-done | bytes 262176 | tf_op jit(solution)/shard_map/all_to_all | solution.py:387
  167.2 5.4 %all-to-all-start.3 = ((bf16[8,501,256]{2,1,0:T(8,128)(2,1)}), bf16[8,501,256]{2,1,0:T(8,128)(2,1)}, u32[]{:S(2)}, u32[]{:S(2)}) async-start(bf16[8,501,256]{2,1,0:T(8,128)(2,1)} %broadcast_in_dim.37), calls=%async_computation.3 | async-start | bytes 4128768 | tf_op jit(solution)/shard_map/all_to_all | solution.py:411
  174.3 26.4 %all-to-all-done.3 = bf16[8,501,256]{2,1,0:T(8,128)(2,1)} async-done(((bf16[8,501,256]{2,1,0:T(8,128)(2,1)}), bf16[8,501,256]{2,1,0:T(8,128)(2,1)}, u32[]{:S(2)}, u32[]{:S(2)}) %all-to-all-start.3) | async-done | bytes 2052128 | tf_op jit(solution)/shard_map/all_to_all | solution.py:411
  200.7 2.2 %reshape.511 = bf16[4008,256]{1,0:T(8,128)(2,1)S(1)} reshape(bf16[8,501,256]{2,1,0:T(8,128)(2,1)} %all-to-all-done.3) | data formatting | bytes 4104192 | tf_op jit(solution)/shard_map/reshape | solution.py:413
  202.9 2.7 %convolution_bitcast_fusion = f32[256,4008]{0,1:T(8,128)} fusion(bf16[4008,256]{1,0:T(8,128)(2,1)S(1)} %reshape.511, bf16[256,256]{1,0:T(8,128)(2,1)S(1)} %copy-done), kind=kOutput, calls=%fused_computation | convolution fusion | flops 525336576 | bytes 6287360 | tf_op jit(solution)/shard_map/dot_general | solution.py:414
  (148 shorter events, 42.1 us)
Async XLA Ops:
  0.6 17.9 %collective-permute-start.4 = (bf16[501,4096]{1,0:T(8,128)(2,1)}, bf16[501,4096]{1,0:T(8,128)(2,1)}, u32[]{:S(2)}, u32[]{:S(2)}) collective-permute-start(bf16[501,4096]{1,0:T(8,128)(2,1)} %bitcast.86), channel_id=1, source_target_pairs={{0,1},{1,0},{64,65},{65,64},{2,3},{3,2},{66,67},{67,66},{4,5},{5,4... | collective-permute-start | bytes 12312584 | tf_op jit(solution)/shard_map/ppermute | solution.py:44
  1.7 6.2 %collective-permute-start = (bf16[32,1024]{1,0:T(8,128)(2,1)S(1)}, bf16[32,1024]{1,0:T(8,128)(2,1)S(1)}, u32[]{:S(2)}, u32[]{:S(2)}) collective-permute-start(bf16[32,1024]{1,0:T(8,128)(2,1)S(1)} %bitcast.72), channel_id=1, source_target_pairs={{0,1},{1,0},{64,65},{65,64},{2,3},{3,2},{66,67},{67,66},{4,5},{5,4... | collective-permute-start | bytes 196616 | tf_op jit(solution)/shard_map/ppermute | solution.py:44
  7.9 9.5 %collective-permute-start.1 = (bf16[64,1024]{1,0:T(8,128)(2,1)S(1)}, bf16[64,1024]{1,0:T(8,128)(2,1)S(1)}, u32[]{:S(2)}, u32[]{:S(2)}) collective-permute-start(bf16[64,1024]{1,0:T(8,128)(2,1)S(1)} %maximum_select_fusion.1.refs_0_), channel_id=1, source_target_pairs={{0,64},{1,17},{64,2},{65,81},{2,66},{3,19},{66,0},{67,83},{4,68},{... | collective-permute-start | bytes 393224 | tf_op jit(solution)/shard_map/ppermute | solution.py:49
  9.9 7.6 %collective-permute-start.2 = (bf16[64,1024]{1,0:T(8,128)(2,1)S(1)}, bf16[64,1024]{1,0:T(8,128)(2,1)S(1)}, u32[]{:S(2)}, u32[]{:S(2)}) collective-permute-start(bf16[64,1024]{1,0:T(8,128)(2,1)S(1)} %maximum_select_fusion.1.refs_0_), channel_id=1, source_target_pairs={{0,66},{1,49},{64,0},{65,113},{2,64},{3,51},{66,2},{67,115},{4,70}... | collective-permute-start | bytes 393224 | tf_op jit(solution)/shard_map/ppermute | solution.py:49
  12.1 6.5 %collective-permute-start.3 = (bf16[64,1024]{1,0:T(8,128)(2,1)S(1)}, bf16[64,1024]{1,0:T(8,128)(2,1)S(1)}, u32[]{:S(2)}, u32[]{:S(2)}) collective-permute-start(bf16[64,1024]{1,0:T(8,128)(2,1)S(1)} %maximum_select_fusion.1.refs_0_), channel_id=1, source_target_pairs={{0,2},{1,33},{64,66},{65,97},{2,0},{3,35},{66,64},{67,99},{4,6},{5... | collective-permute-start | bytes 393224 | tf_op jit(solution)/shard_map/ppermute | solution.py:49
  23.7 66.2 %all-to-all-start = ((bf16[8,640,256]{2,1,0:T(8,128)(2,1)}), bf16[8,640,256]{2,1,0:T(8,128)(2,1)S(1)}, u32[]{:S(2)}, u32[]{:S(2)}) async-start(bf16[8,640,256]{2,1,0:T(8,128)(2,1)} %pad_maximum_fusion), calls=%async_computation | async-start | bytes 5242880 | tf_op jit(solution)/shard_map/all_to_all | solution.py:310
  28.8 34.8 %collective-permute-start.5 = (bf16[4,64,768]{2,1,0:T(8,128)(2,1)S(1)}, bf16[4,64,768]{2,1,0:T(8,128)(2,1)S(1)}, u32[]{:S(2)}, u32[]{:S(2)}) collective-permute-start(bf16[4,64,768]{2,1,0:T(8,128)(2,1)S(1)} %copy-done.13), channel_id=1, source_target_pairs={{0,4},{1,5},{64,68},{65,69},{2,6},{3,7},{66,70},{67,71},{4,8},{5,9... | collective-permute-start | bytes 1179656 | tf_op jit(solution)/shard_map/ppermute | solution.py:49
  30.3 33.2 %collective-permute-start.6 = (bf16[4,64,768]{2,1,0:T(8,128)(2,1)S(1)}, bf16[4,64,768]{2,1,0:T(8,128)(2,1)S(1)}, u32[]{:S(2)}, u32[]{:S(2)}) collective-permute-start(bf16[4,64,768]{2,1,0:T(8,128)(2,1)S(1)} %copy-done.13), channel_id=1, source_target_pairs={{0,12},{1,13},{64,76},{65,77},{2,14},{3,15},{66,78},{67,79},{4,0},... | collective-permute-start | bytes 1179656 | tf_op jit(solution)/shard_map/ppermute | solution.py:49
  32.0 33.0 %collective-permute-start.7 = (bf16[4,64,768]{2,1,0:T(8,128)(2,1)S(1)}, bf16[4,64,768]{2,1,0:T(8,128)(2,1)}, u32[]{:S(2)}, u32[]{:S(2)}) collective-permute-start(bf16[4,64,768]{2,1,0:T(8,128)(2,1)S(1)} %copy-done.13), channel_id=1, source_target_pairs={{0,8},{1,9},{64,72},{65,73},{2,10},{3,11},{66,74},{67,75},{4,12},{... | collective-permute-start | bytes 1179656 | tf_op jit(solution)/shard_map/ppermute | solution.py:49
  34.0 24.4 %collective-permute-start.10 = (bf16[4,64,256]{2,1,0:T(8,128)(2,1)}, bf16[4,64,256]{2,1,0:T(8,128)(2,1)S(1)}, u32[]{:S(2)}, u32[]{:S(2)}) collective-permute-start(bf16[4,64,256]{2,1,0:T(8,128)(2,1)} %get-tuple-element.17.refs_4_), channel_id=1, source_target_pairs={{0,32},{1,3},{64,96},{65,67},{2,34},{3,1},{66,98},{67,65},{4,36},{... | collective-permute-start | bytes 393224 | tf_op jit(solution)/shard_map/ppermute | solution.py:49
  36.0 24.0 %collective-permute-start.8 = (bf16[4,64,256]{2,1,0:T(8,128)(2,1)}, bf16[4,64,256]{2,1,0:T(8,128)(2,1)S(1)}, u32[]{:S(2)}, u32[]{:S(2)}) collective-permute-start(bf16[4,64,256]{2,1,0:T(8,128)(2,1)} %get-tuple-element.17.refs_4_), channel_id=1, source_target_pairs={{0,16},{1,65},{64,80},{65,3},{2,18},{3,67},{66,82},{67,1},{4,20},{... | collective-permute-start | bytes 393224 | tf_op jit(solution)/shard_map/ppermute | solution.py:49
  58.4 5.2 %collective-permute-start.9 = (bf16[4,64,256]{2,1,0:T(8,128)(2,1)}, bf16[4,64,256]{2,1,0:T(8,128)(2,1)S(1)}, u32[]{:S(2)}, u32[]{:S(2)}) collective-permute-start(bf16[4,64,256]{2,1,0:T(8,128)(2,1)} %get-tuple-element.17.refs_4_), channel_id=1, source_target_pairs={{0,48},{1,67},{64,112},{65,1},{2,50},{3,65},{66,114},{67,3},{4,52}... | collective-permute-start | bytes 393224 | tf_op jit(solution)/shard_map/ppermute | solution.py:49
  67.9 20.6 %collective-permute-start.11 = (bf16[16,64,768]{2,1,0:T(8,128)(2,1)}, bf16[16,64,768]{2,1,0:T(8,128)(2,1)S(1)}, u32[]{:S(2)}, u32[]{:S(2)}) collective-permute-start(bf16[16,64,768]{2,1,0:T(8,128)(2,1)} %bitcast.66), channel_id=1, source_target_pairs={{0,16},{1,65},{64,80},{65,3},{2,18},{3,67},{66,82},{67,1},{4,20},{... | collective-permute-start | bytes 4718600 | tf_op jit(solution)/shard_map/ppermute | solution.py:316
  67.9 22.0 %collective-permute-start.12 = (bf16[16,64,768]{2,1,0:T(8,128)(2,1)}, bf16[16,64,768]{2,1,0:T(8,128)(2,1)}, u32[]{:S(2)}, u32[]{:S(2)}) collective-permute-start(bf16[16,64,768]{2,1,0:T(8,128)(2,1)} %bitcast.67), channel_id=1, source_target_pairs={{0,48},{1,67},{64,112},{65,1},{2,50},{3,65},{66,114},{67,3},{4,52}... | collective-permute-start | bytes 4718600 | tf_op jit(solution)/shard_map/ppermute | solution.py:317
  70.0 15.2 %collective-permute-start.13 = (bf16[16,64,256]{2,1,0:T(8,128)(2,1)}, bf16[16,64,256]{2,1,0:T(8,128)(2,1)S(1)}, u32[]{:S(2)}, u32[]{:S(2)}) collective-permute-start(bf16[16,64,256]{2,1,0:T(8,128)(2,1)} %bitcast.62), channel_id=1, source_target_pairs={{0,4},{1,5},{64,68},{65,69},{2,6},{3,7},{66,70},{67,71},{4,8},{5,9... | collective-permute-start | bytes 1572872 | tf_op jit(solution)/shard_map/ppermute | solution.py:318
  71.5 13.6 %collective-permute-start.14 = (bf16[16,64,256]{2,1,0:T(8,128)(2,1)}, bf16[16,64,256]{2,1,0:T(8,128)(2,1)S(1)}, u32[]{:S(2)}, u32[]{:S(2)}) collective-permute-start(bf16[16,64,256]{2,1,0:T(8,128)(2,1)} %bitcast.63), channel_id=1, source_target_pairs={{0,12},{1,13},{64,76},{65,77},{2,14},{3,15},{66,78},{67,79},{4,0},... | collective-permute-start | bytes 1572872 | tf_op jit(solution)/shard_map/ppermute | solution.py:318
  94.0 7.9 %collective-permute-start.18 = (bf16[8,640,256]{2,1,0:T(8,128)(2,1)}, bf16[8,640,256]{2,1,0:T(8,128)(2,1)S(1)}, u32[]{:S(2)}, u32[]{:S(2)}) collective-permute-start(bf16[8,640,256]{2,1,0:T(8,128)(2,1)} %get-tuple-element.20.own_ref), channel_id=1, source_target_pairs={{0,1},{1,0},{64,65},{65,64},{2,3},{3,2},{66,67},{67,66},{4,5},{5,4... | collective-permute-start | bytes 7864328 | tf_op jit(solution)/shard_map/ppermute | solution.py:44
  94.4 17.1 %collective-permute-start.15 = (bf16[8,64,768]{2,1,0:T(8,128)(2,1)}, bf16[8,64,768]{2,1,0:T(8,128)(2,1)}, u32[]{:S(2)}, u32[]{:S(2)}) collective-permute-start(bf16[8,64,768]{2,1,0:T(8,128)(2,1)} %get-tuple-element.21), channel_id=1, source_target_pairs={{0,16},{1,65},{64,80},{65,3},{2,18},{3,67},{66,82},{67,1},{4,20},{... | collective-permute-start | bytes 2359304 | tf_op jit(solution)/shard_map/ppermute | solution.py:325
  96.5 15.0 %collective-permute-start.16 = (bf16[8,64,768]{2,1,0:T(8,128)(2,1)}, bf16[8,64,768]{2,1,0:T(8,128)(2,1)}, u32[]{:S(2)}, u32[]{:S(2)}) collective-permute-start(bf16[8,64,768]{2,1,0:T(8,128)(2,1)} %get-tuple-element.22), channel_id=1, source_target_pairs={{0,48},{1,67},{64,112},{65,1},{2,50},{3,65},{66,114},{67,3},{4,52}... | collective-permute-start | bytes 2359304 | tf_op jit(solution)/shard_map/ppermute | solution.py:326
  97.2 14.3 %collective-permute-start.17 = (bf16[16,64,256]{2,1,0:T(8,128)(2,1)}, bf16[16,64,256]{2,1,0:T(8,128)(2,1)}, u32[]{:S(2)}, u32[]{:S(2)}) collective-permute-start(bf16[16,64,256]{2,1,0:T(8,128)(2,1)} %get-tuple-element.23.refs_5_), channel_id=1, source_target_pairs={{0,8},{1,9},{64,72},{65,73},{2,10},{3,11},{66,74},{67,75},{4,12},{... | collective-permute-start | bytes 1572872 | tf_op jit(solution)/shard_map/ppermute | solution.py:320
  130.1 13.8 %all-to-all-start.1 = ((f32[8,32,128]{2,1,0:T(8,128)}), f32[8,32,128]{2,1,0:T(8,128)S(1)}, u32[]{:S(2)}, u32[]{:S(2)}) async-start(f32[8,32,128]{2,1,0:T(8,128)} %broadcast_in_dim.34), calls=%async_computation.1 | async-start | bytes 262144 | tf_op jit(solution)/shard_map/all_to_all | solution.py:385
  144.8 17.4 %all-to-all-start.2 = ((f32[16,32,128]{2,1,0:T(8,128)}), f32[16,32,128]{2,1,0:T(8,128)S(1)}, u32[]{:S(2)}, u32[]{:S(2)}) async-start(f32[16,32,128]{2,1,0:T(8,128)} %broadcast_in_dim.36), calls=%async_computation.2 | async-start | bytes 524288 | tf_op jit(solution)/shard_map/all_to_all | solution.py:387
  164.3 1.4 collective-permute-start.20
  167.2 33.5 %all-to-all-start.3 = ((bf16[8,501,256]{2,1,0:T(8,128)(2,1)}), bf16[8,501,256]{2,1,0:T(8,128)(2,1)}, u32[]{:S(2)}, u32[]{:S(2)}) async-start(bf16[8,501,256]{2,1,0:T(8,128)(2,1)} %broadcast_in_dim.37), calls=%async_computation.3 | async-start | bytes 4128768 | tf_op jit(solution)/shard_map/all_to_all | solution.py:411
  (26 other events, 207.8 us)

commit v3 on v2

v3 whole, which is shorter than its diff:
```python
import math
import jax
import jax.numpy as jnp
from jax import lax
from jax.experimental import pallas as pl
from jax.experimental.pallas import tpu as pltpu
from jax.sharding import PartitionSpec as P

mix_weight = 0.5
loss_scale = 4096.0

AXES = ("variant", "vocab")
SIDE = 4
ROWS = 640
OFFSETS = (0, -1, 1, 2)


def device_index(x, y, z, c):
    x, y, z = x % SIDE, y % SIDE, z % SIDE
    return ((z % 2) * SIDE + x) * 16 + y * 4 + (z // 2) * 2 + c


def permutation(move):
    return [
        (device_index(x, y, z, c), device_index(*move(x, y, z, c)))
        for x in range(SIDE)
        for y in range(SIDE)
        for z in range(SIDE)
        for c in range(2)
    ]


def ring_shift(axes, step):
    def move(x, y, z, c):
        at = {"x": x, "y": y, "z": z}
        at[axes[c]] += step
        return at["x"], at["y"], at["z"], c

    return permutation(move)


def sibling(value):
    return lax.ppermute(value, AXES, permutation(lambda x, y, z, c: (x, y, z, 1 - c)))


def ring_gather(value, axes):
    return [value] + [
        lax.ppermute(value, AXES, ring_shift(axes, step)) for step in (1, -1, 2)
    ]


def stack_kernel(*refs):
    for i in range(4):
        refs[-1][i] = refs[i][...]


def stack(blocks, after=()):
    vmem = pl.BlockSpec(memory_space=pltpu.VMEM)
    shape = (4,) + blocks[0].shape
    return pl.pallas_call(
        stack_kernel,
        out_shape=jax.ShapeDtypeStruct(shape, jnp.bfloat16),
        in_specs=[vmem] * 4 + [pl.BlockSpec(memory_space=pl.ANY)] * len(after),
        out_specs=vmem,
        cost_estimate=pl.CostEstimate(
            flops=0, bytes_accessed=4 * math.prod(shape), transcendentals=0
        ),
    )(*blocks, *after)


def halves_kernel(before, after, through_in, before_half, after_half, through_out):
    before_half[...] = before[...]
    after_half[...] = after[...]


def forward_halves(before, after, through):
    n, rows, lanes = before.shape
    block = (n // 2, rows, lanes)
    hbm = pl.BlockSpec(memory_space=pl.ANY)
    lower = pl.BlockSpec(block, lambda i: (0, 0, 0))
    return pl.pallas_call(
        halves_kernel,
        grid=(1,),
        out_shape=[jax.ShapeDtypeStruct(block, before.dtype)] * 2
        + [jax.ShapeDtypeStruct(through.shape, through.dtype)],
        in_specs=[lower, pl.BlockSpec(block, lambda i: (1, 0, 0)), hbm],
        out_specs=[lower, lower, hbm],
        input_output_aliases={2: 2},
        cost_estimate=pl.CostEstimate(
            flops=0, bytes_accessed=4 * n * rows * lanes, transcendentals=0
        ),
    )(before, after, through)


def copy_kernel(value, after, out, sem):
    copy = pltpu.make_async_copy(value, out, sem)
    copy.start()
    copy.wait()


def copy_after(value, after):
    hbm = pl.BlockSpec(memory_space=pl.ANY)
    return pl.pallas_call(
        copy_kernel,
        out_shape=jax.ShapeDtypeStruct(value.shape, value.dtype),
        in_specs=[hbm, hbm],
        out_specs=hbm,
        scratch_shapes=[pltpu.SemaphoreType.DMA(())],
        cost_estimate=pl.CostEstimate(
            flops=0, bytes_accessed=4 * math.prod(value.shape), transcendentals=0
        ),
    )(value, after)


def finish_kernel(g_ref, e_own, e_other, l_own, l_other, stat_ref, mask_ref, ids_ref, base_ref, *outs):
    err_refs, loss_ref = outs[0:2], outs[2]
    cols, half = l_own.shape
    near = g_ref[:, 0:8, :]
    top = jnp.max(near, axis=0)
    lse = top + jnp.log(jnp.sum(jnp.exp(near - top), axis=0))
    soft = jnp.sum(
        jnp.sum(jnp.exp(near - lse) * g_ref[:, 8:16, :], axis=0), axis=0, keepdims=True
    ) / 8
    students = g_ref[:, 16, :]
    s_top = jnp.max(students, axis=0, keepdims=True)
    s_lse = s_top + jnp.log(jnp.sum(jnp.exp(students - s_top), axis=0, keepdims=True))
    hard = jnp.sum(g_ref[:, 17, :], axis=0, keepdims=True) - s_lse
    mask = mask_ref[...]
    loss_ref[...] = mask * (-mix_weight * (soft - s_lse) - (1.0 - mix_weight) * hard)
    factors = [
        jnp.exp(stat_ref[2:3, v * half : (v + 1) * half] - lse[v : v + 1]) * (mix_weight / 8)
        for v in range(8)
    ]
    scale = loss_scale * mask
    rows = lax.broadcasted_iota(jnp.int32, (cols, half), 0)
    for i, (e, l) in enumerate(((e_own, l_own), (e_other, l_other))):
        value = jnp.exp(l[...] - s_lse)
        hit = rows + base_ref[i] == ids_ref[...]
        value -= jnp.where(hit, 1.0 - mix_weight, 0.0)
        averaged = e[:, 0:half] * factors[0]
        for v in range(1, 8):
            averaged += e[:, v * half : (v + 1) * half] * factors[v]
        err_refs[i][...] = (scale * (value - averaged)).astype(jnp.bfloat16)


def finish(gathered, e, logits, stats, mask, ids, base):
    cols, half = logits[0].shape
    vmem = pl.BlockSpec(memory_space=pltpu.VMEM)
    return pl.pallas_call(
        finish_kernel,
        out_shape=[
            jax.ShapeDtypeStruct((cols, half), jnp.bfloat16),
            jax.ShapeDtypeStruct((cols, half), jnp.bfloat16),
            jax.ShapeDtypeStruct((1, half), jnp.float32),
        ],
        in_specs=[vmem] * 8 + [pl.BlockSpec(memory_space=pltpu.SMEM)],
        out_specs=[vmem] * 3,
        compiler_params=pltpu.CompilerParams(vmem_limit_bytes=24 << 20),
        cost_estimate=pl.CostEstimate(
            flops=40 * cols * half, bytes_accessed=10 * cols * 1024, transcendentals=2 * cols * half
        ),
    )(gathered, *e, *logits, stats, mask, ids, base)


def student_kernel(own_ref, other_ref, ids_ref, base_ref, l_own, l_other, stat_ref):
    half, cols = l_own.shape[1], l_own.shape[0]
    dims = (((1,), (1,)), ((), ()))
    logits = []
    for ref, out in ((own_ref, l_own), (other_ref, l_other)):
        total = jnp.zeros((cols, half), jnp.float32)
        for block in range(8):
            total += lax.dot_general(
                ref[block, half : half + cols, :],
                own_ref[block, :half, :],
                dims,
                preferred_element_type=jnp.float32,
            )
        out[...] = total
        logits.append(total)
    top = jnp.maximum(
        jnp.max(logits[0], axis=0, keepdims=True), jnp.max(logits[1], axis=0, keepdims=True)
    )
    total = jnp.zeros((1, half), jnp.float32)
    hard = jnp.zeros((1, half), jnp.float32)
    rows = lax.broadcasted_iota(jnp.int32, (cols, half), 0)
    for i in range(2):
        total += jnp.sum(jnp.exp(logits[i] - top), axis=0, keepdims=True)
        hit = rows + base_ref[i] == ids_ref[...]
        hard += jnp.sum(jnp.where(hit, logits[i], 0.0), axis=0, keepdims=True)
    stat_ref[...] = jnp.concatenate([top + jnp.log(total), hard, jnp.zeros((6, half), jnp.float32)])


def student_logits(own, other, ids, base, cols):
    half = ids.shape[1]
    vmem = pl.BlockSpec(memory_space=pltpu.VMEM)
    return pl.pallas_call(
        student_kernel,
        out_shape=[
            jax.ShapeDtypeStruct((cols, half), jnp.float32),
            jax.ShapeDtypeStruct((cols, half), jnp.float32),
            jax.ShapeDtypeStruct((8, half), jnp.float32),
        ],
        in_specs=[vmem] * 3 + [pl.BlockSpec(memory_space=pltpu.SMEM)],
        out_specs=[vmem] * 3,
        compiler_params=pltpu.CompilerParams(vmem_limit_bytes=24 << 20),
        cost_estimate=pl.CostEstimate(
            flops=2 * 2 * cols * half * 2048, bytes_accessed=12 << 20, transcendentals=2 * cols * half
        ),
    )(own, other, ids, base)


def ordered(core, own, other, axis):
    return jnp.where(
        core == 0,
        jnp.concatenate([own, other], axis=axis),
        jnp.concatenate([other, own], axis=axis),
    )


def teacher_kernel(table, inv_tau, *refs):
    groups, w_refs, l_refs = refs[0:5], refs[5:7], refs[7:9]
    e_refs, stat_ref, hidden, sem = refs[9:11], refs[11], refs[12], refs[13]

    def chunk_copy(ref, base, n):
        row = pl.multiple_of(table[base + n] * 64, 64)
        return pltpu.make_async_copy(ref.at[n], hidden.at[pl.ds(row, 64)], sem)

    blocks = []
    base = 0
    for ref in groups:
        blocks.append((ref, base))
        base += ref.shape[0]
    for ref, base in blocks:
        def start(n, _, ref=ref, base=base):
            chunk_copy(ref, base, n).start()
            return 0
        lax.fori_loop(0, ref.shape[0], start, 0)
    for ref, base in blocks:
        def wait(n, _, ref=ref, base=base):
            chunk_copy(ref, base, n).wait()
            return 0
        lax.fori_loop(0, ref.shape[0], wait, 0)

    def tile(j, _):
        lanes = pl.ds(pl.multiple_of(j * 256, 256), 256)
        scale = inv_tau[:, lanes]
        block = hidden[:, lanes]
        scores = [
            jnp.dot(w[...], block, preferred_element_type=jnp.float32) * scale for w in w_refs
        ]
        top = jnp.maximum(
            jnp.max(scores[0], axis=0, keepdims=True), jnp.max(scores[1], axis=0, keepdims=True)
        )
        total = jnp.zeros((1, 256), jnp.float32)
        cross = jnp.zeros((1, 256), jnp.float32)
        for i in range(2):
            e = jnp.exp(scores[i] - top)
            e_refs[i][:, lanes] = e
            logits = l_refs[i][...]
            total += jnp.sum(e, axis=0, keepdims=True)
            cross += jnp.sum(
                e * jnp.concatenate([logits, logits], axis=1), axis=0, keepdims=True
            )
        stat_ref[0:1, lanes] = top + jnp.log(total)
        stat_ref[1:2, lanes] = cross / total
        stat_ref[2:3, lanes] = top
        return 0

    lax.fori_loop(0, 4, tile, 0)


def teacher_scores(table, inv_tau, hidden, weights, logits):
    cols, width = weights[0].shape
    vmem = pl.BlockSpec(memory_space=pltpu.VMEM)
    hbm = pl.BlockSpec(memory_space=pl.ANY)
    return pl.pallas_call(
        teacher_kernel,
        out_shape=[
            jax.ShapeDtypeStruct((cols, 1024), jnp.float32),
            jax.ShapeDtypeStruct((cols, 1024), jnp.float32),
            jax.ShapeDtypeStruct((8, 1024), jnp.float32),
        ],
        in_specs=[pl.BlockSpec(memory_space=pltpu.SMEM), vmem] + [hbm] * 5 + [vmem] * 4,
        out_specs=[vmem] * 3,
        scratch_shapes=[
            pltpu.VMEM((width, 1024), jnp.bfloat16),
            pltpu.SemaphoreType.DMA(()),
        ],
        compiler_params=pltpu.CompilerParams(vmem_limit_bytes=44 << 20),
        cost_estimate=pl.CostEstimate(
            flops=2 * 2 * cols * width * 1024,
            bytes_accessed=2 * (2 * cols * width + width * 1024) + 8 * cols * 1024,
            transcendentals=2 * cols * 1024,
        ),
    )(table, inv_tau, *hidden, *weights, *logits)


def on_device(
    teacher_hidden,
    teacher_weight,
    variant_ids,
    temps,
    student_hidden,
    student_weight,
    token_ids,
    loss_mask,
):
    a = lax.axis_index("variant")
    b = lax.axis_index("vocab")
    core = b % 2
    x, y, z = a % 4, b // 4, (b // 2) % 2 * 2 + a // 4
    cols = teacher_weight.shape[1]
    half = 128

    halves = [
        lax.dynamic_slice_in_dim(teacher_hidden, start * half, half, axis=1)
        .transpose(2, 0, 1)
        .reshape(32, 1024)
        for start in (core, 1 - core)
    ]
    unit = ordered(core, halves[0], sibling(halves[1]), 0)
    w_own = teacher_weight.T
    w_other = sibling(copy_after(w_own, unit))
    hidden = stack(ring_gather(unit, "zx"), (w_other,))

    meta = jnp.concatenate(
        [token_ids // 256, token_ids % 256, loss_mask, jnp.zeros((32,), jnp.int32)]
    ).astype(jnp.bfloat16)
    meta = jnp.concatenate([meta, hidden[0, 0, :128]])[None, None]
    mine = lax.dynamic_slice_in_dim(student_hidden, core * half, half, axis=0)
    send = jnp.concatenate(
        [
            jnp.broadcast_to(mine[None], (8, half, 256)),
            student_weight.T.reshape(8, cols, 256),
            jnp.broadcast_to(meta, (8, ROWS - half - cols, 256)),
        ],
        axis=1,
    )
    got = lax.all_to_all(send, "variant", 0, 0, tiled=True)

    hidden = stack(ring_gather(hidden, "yy")).reshape(16, 64, 1024)
    plus, minus = ring_shift("xz", 1), ring_shift("xz", -1)
    before = lax.ppermute(hidden, AXES, plus)
    after = lax.ppermute(hidden, AXES, minus)
    lower, upper, got = forward_halves(before, after, got)
    hidden = [
        hidden,
        before,
        after,
        lax.ppermute(lower, AXES, plus),
        lax.ppermute(upper, AXES, minus),
    ]

    got_other = sibling(got)
    meta_all = got[:, half + cols]
    ids = (meta_all[:, 0:32].astype(jnp.int32) * 256 + meta_all[:, 32:64].astype(jnp.int32)).reshape(256)
    maskf = meta_all[:, 64:96].astype(jnp.float32).reshape(256)
    ids_half = lax.dynamic_slice_in_dim(ids, core * half, half)
    mask_half = lax.dynamic_slice_in_dim(maskf, core * half, half)

    offsets = jnp.array(OFFSETS, jnp.int32)
    o1, o2, o3 = (
        offsets.reshape(shape) for shape in ((1, 1, 4), (1, 4, 1), (4, 1, 1))
    )
    zero = jnp.zeros((4, 4, 4), jnp.int32)

    def place(dx, dy, dz):
        px, py, pz = (x + dx) % 4, (y + dy) % 4, (z + dz) % 4
        return ((pz % 2 * 4 + px) * 8 + py * 2 + pz // 2 + zero).reshape(64)

    table = jnp.where(core == 0, place(o3, o2, o1), place(o1, o2, o3))
    categories = jnp.arange(temps.shape[0], dtype=jnp.int32)
    taus = jnp.sum(
        jnp.where(variant_ids[:, None] == categories[None, :], temps[None, :], 0.0), axis=1
    )
    inv_tau = jnp.repeat(1.0 / taus, half)[None]

    base = jnp.stack([(b * 8 + a) * cols, ((b + 1 - 2 * core) * 8 + a) * cols])
    l_own, l_other, s_stats = student_logits(got, got_other, ids_half[None], base, cols)
    logits = (l_own, l_other)
    e_own, e_other, stats = teacher_scores(
        table, inv_tau, hidden, (w_own, w_other), logits
    )
    packed = jnp.concatenate([stats[:2].reshape(16, half), s_stats])
    groups = [
        sorted(device_index(i // 16, i // 4, i, c) for i in range(64)) for c in range(2)
    ]
    gathered = lax.all_to_all(
        jnp.broadcast_to(packed[None], (64, 24, half)),
        AXES, 0, 0, tiled=True, axis_index_groups=groups,
    )
    *errors, loss_half = finish(
        gathered, (e_own, e_other), logits, stats, mask_half[None], ids_half[None], base
    )
    loss_half = loss_half[0]
    loss_all = ordered(core, loss_half, sibling(loss_half), 0)
    token_loss = lax.dynamic_slice_in_dim(loss_all, a * 32, 32)
    error = ordered(core, errors[0], sibling(errors[1]), 1)
    error_all = lax.all_to_all(
        jnp.broadcast_to(error[None], (8, cols, 256)), "variant", 0, 0, tiled=True
    ).reshape(8 * cols, 256)
    grad_t = jnp.dot(error_all, student_hidden, preferred_element_type=jnp.float32)
    return token_loss, grad_t.T


def solution(mesh):
    in_specs = (
        P(None, None, ("variant", "vocab")),
        P(None, ("vocab", "variant")),
        P(),
        P(),
        P(None, "variant"),
        P("variant", "vocab"),
        P("variant"),
        P("variant"),
    )
    out_specs = (P("variant"), P("variant", "vocab"))
    return jax.shard_map(
        on_device, mesh=mesh, in_specs=in_specs, out_specs=out_specs, check_vma=False
    )
```

time: 208 us -> 321 us (1.54)
  Pallas kernels: 27.2 us -> 157 us
  starting transfers between devices: 53.7 us -> 38.9 us
    pallas_call x2 -> x4, Pallas kernels: 4.88 us -> 132 us  [the longest x1 126 us: copy_after(): pl.pallas_call(copy_kernel, out_shape=jax.ShapeDtypeStruct(value.shape, v...]
    ppermute x9 -> x6, waiting for transfers between devices: 27 us -> 13.7 us  [ring_gather(): lax.ppermute(value, AXES, ring_shift(axes, step))]
    all_to_all x1, waiting for transfers between devices: 0.01 us -> 12.3 us  [on_device(): got = lax.all_to_all(send, 'variant', 0, 0, tiled=True)]
    ppermute x1, waiting for transfers between devices: 0.01 us -> 6.58 us  [on_device(): lax.ppermute(lower, AXES, plus)]
    ppermute x5 -> x2, starting transfers between devices: 8.46 us -> 2.42 us  [the longest x1 2.41 us: on_device(): after = lax.ppermute(hidden, AXES, minus)]
    all_to_all x2 -> x1, starting transfers between devices: 16.3 us -> 12.1 us  [on_device(): lax.all_to_all(jnp.broadcast_to(packed[None], (64, 24, half)), AXES, 0, 0...]
    ppermute x9 -> x6, starting transfers between devices: 14.9 us -> 11.1 us  [ring_gather(): lax.ppermute(value, AXES, ring_shift(axes, step))]
    unnamed x52 -> x34, local copies, waits for them, and re-layouts: 7.37 us -> 6.22 us
  transfers between devices with their start and end apart: 25 -> 18, of which waited for: 13 -> 14; matrix products, arithmetic and copies ran while one was open for 4% -> 2% of each run, Pallas kernels for 2% -> 2%
where the time goes in v3:
time: 321 us; the launch traced here: 318 us
  Pallas kernels  157 us (49%)
  waiting for transfers between devices  99.9 us (31%)
  starting transfers between devices  38.9 us (12%)
  local copies, waits for them, and re-layouts  15.7 us (5%)
    pallas_call x1, Pallas kernels, copy_after(): pl.pallas_call(copy_kernel, out_shape=jax.ShapeDtypeStruct(value.shape, v...  126 us
    all_to_all x1, waiting for transfers between devices, on_device(): lax.all_to_all(jnp.broadcast_to(error[None], (8, cols, 256)), 'variant',...  26.4 us
    ppermute x1, waiting for transfers between devices, on_device(): after = lax.ppermute(hidden, AXES, minus)  21.5 us
    pallas_call x1, Pallas kernels, teacher_scores(): pl.pallas_call(teacher_kernel, out_shape=[jax.ShapeDtypeStruct((cols, 102...  19.8 us
    all_to_all x1, waiting for transfers between devices, on_device(): lax.all_to_all(jnp.broadcast_to(packed[None], (64, 24, half)), AXES, 0, 0...  13.7 us
    ppermute x6, waiting for transfers between devices, ring_gather(): lax.ppermute(value, AXES, ring_shift(axes, step))  13.7 us
    all_to_all x1, waiting for transfers between devices, on_device(): got = lax.all_to_all(send, 'variant', 0, 0, tiled=True)  12.3 us
    all_to_all x1, starting transfers between devices, on_device(): lax.all_to_all(jnp.broadcast_to(packed[None], (64, 24, half)), AXES, 0, 0...  12.1 us
  transfers between devices with their start and end apart: 18, of which 14 were waited for; matrix products, arithmetic and copies ran while one was open for 2% of the time, Pallas kernels for 2%

profile of v3, /device:TPU:2, one launch (start us, length us, event | category | flops | bytes accessed | tf_op | source)
XLA Modules:
  0.0 318.1 jit_solution(1777198531029463879)
XLA Ops:
  3.6 126.2 %shard_map.104 = bf16[501,4096]{1,0:T(8,128)(2,1)} custom-call(bf16[501,4096]{1,0:T(8,128)(2,1)} %bitcast.38, bf16[64,1024]{1,0:T(8,128)(2,1)} %maximum_select_fusion.1.after.refs_0_), custom_call_target="tpu_custom_call" | custom-call | bytes 8208384 | tf_op jit(solution)/shard_map/pallas_call | solution.py:103
  130.1 3.9 %collective-permute-start.3 = (bf16[64,1024]{1,0:T(8,128)(2,1)S(1)}, bf16[64,1024]{1,0:T(8,128)(2,1)S(1)}, u32[]{:S(2)}, u32[]{:S(2)}) collective-permute-start(bf16[64,1024]{1,0:T(8,128)(2,1)S(1)} %copy-done.6), channel_id=1, source_target_pairs={{0,2},{1,33},{64,66},{65,97},{2,0},{3,35},{66,64},{67,99},{4,6},{5... | collective-permute-start | bytes 393224 | tf_op jit(solution)/shard_map/ppermute | solution.py:48
  136.0 2.2 reshape.234
  141.5 1.9 shard_map.105.refs_0_
  143.4 3.2 %collective-permute-start.7 = (bf16[4,64,1024]{2,1,0:T(8,128)(2,1)}, bf16[4,64,1024]{2,1,0:T(8,128)(2,1)S(1)}, u32[]{:S(2)}, u32[]{:S(2)}) collective-permute-start(bf16[4,64,1024]{2,1,0:T(8,128)(2,1)} %shard_map.105.refs_0_), channel_id=1, source_target_pairs={{0,8},{1,9},{64,72},{65,73},{2,10},{3,11},{66,74},{67,75},{4,12},{... | collective-permute-start | bytes 1572872 | tf_op jit(solution)/shard_map/ppermute | solution.py:48
  149.5 1.7 pad_maximum_fusion
  151.2 4.8 %all-to-all-start = ((bf16[8,640,256]{2,1,0:T(8,128)(2,1)}), bf16[8,640,256]{2,1,0:T(8,128)(2,1)S(1)}, u32[]{:S(2)}, u32[]{:S(2)}) async-start(bf16[8,640,256]{2,1,0:T(8,128)(2,1)} %pad_maximum_fusion), calls=%async_computation | async-start | bytes 5242880 | tf_op jit(solution)/shard_map/all_to_all | solution.py:339
  156.0 4.0 %collective-permute-done.7.refs_3_ = bf16[4,64,1024]{2,1,0:T(8,128)(2,1)S(1)} collective-permute-done((bf16[4,64,1024]{2,1,0:T(8,128)(2,1)}, bf16[4,64,1024]{2,1,0:T(8,128)(2,1)S(1)}, u32[]{:S(2)}, u32[]{:S(2)}) %collective-permute-start.7) | collective-permute-done | bytes 524320 | tf_op jit(solution)/shard_map/ppermute | solution.py:48
  160.0 7.0 %collective-permute-done.6.refs_2_ = bf16[4,64,1024]{2,1,0:T(8,128)(2,1)} collective-permute-done((bf16[4,64,1024]{2,1,0:T(8,128)(2,1)}, bf16[4,64,1024]{2,1,0:T(8,128)(2,1)}, u32[]{:S(2)}, u32[]{:S(2)}) %collective-permute-start.6) | collective-permute-done | bytes 524320 | tf_op jit(solution)/shard_map/ppermute | solution.py:48
  167.1 3.0 shard_map.106
  170.1 2.4 collective-permute-start.9
  172.5 12.3 %all-to-all-done.through_in = bf16[8,640,256]{2,1,0:T(8,128)(2,1)S(1)} async-done(((bf16[8,640,256]{2,1,0:T(8,128)(2,1)}), bf16[8,640,256]{2,1,0:T(8,128)(2,1)S(1)}, u32[]{:S(2)}, u32[]{:S(2)}) %all-to-all-start) | async-done | bytes 2621472 | tf_op jit(solution)/shard_map/all_to_all | solution.py:339
  184.9 21.5 %collective-permute-done.9.after.refs_2_ = bf16[16,64,1024]{2,1,0:T(8,128)(2,1)} collective-permute-done((bf16[16,64,1024]{2,1,0:T(8,128)(2,1)}, bf16[16,64,1024]{2,1,0:T(8,128)(2,1)}, u32[]{:S(2)}, u32[]{:S(2)}) %collective-permute-start.9) | collective-permute-done | bytes 2097184 | tf_op jit(solution)/shard_map/ppermute | solution.py:344
  206.4 2.9 shard_map.107
  214.4 1.7 copy-done.2
  216.1 1.9 shard_map.108
  218.0 6.6 %collective-permute-done.10.refs_3_ = bf16[8,64,1024]{2,1,0:T(8,128)(2,1)} collective-permute-done((bf16[8,64,1024]{2,1,0:T(8,128)(2,1)}, bf16[8,64,1024]{2,1,0:T(8,128)(2,1)}, u32[]{:S(2)}, u32[]{:S(2)}) %collective-permute-start.10) | collective-permute-done | bytes 1048608 | tf_op jit(solution)/shard_map/ppermute | solution.py:350
  225.4 19.8 %shard_map.109 = (f32[501,1024]{1,0:T(8,128)S(1)}, f32[501,1024]{1,0:T(8,128)S(1)}, f32[8,1024]{1,0:T(8,128)S(1)}) custom-call(s32[64]{0:T(128)S(1)} %select_n.151.table, f32[1,1024]{1,0:T(1,128)S(1)} %bitcast.35, bf16[16,64,1024]{2,1,0:T(8,128)(2,1)S(1)} %bitcast.34, bf16[16,64,1024]{2,1,0:T(8,128)(2,1)} %collective-permute-done.8.before.refs_1_, ...), custom_call_target="tpu_custom_call" | custom-call | flops 8405385216 | bytes 20701184 | tf_op jit(solution)/shard_map/pallas_call | solution.py:276
  247.5 12.1 %all-to-all-start.1 = ((f32[64,24,128]{2,1,0:T(8,128)}), f32[64,24,128]{2,1,0:T(8,128)S(1)}, u32[]{:S(2)}, u32[]{:S(2)}) async-start(f32[64,24,128]{2,1,0:T(8,128)} %broadcast_in_dim.56), calls=%async_computation.1 | async-start | bytes 1572864 | tf_op jit(solution)/shard_map/all_to_all | solution.py:388
  259.8 13.7 %all-to-all-done.1.g_ref = f32[64,24,128]{2,1,0:T(8,128)S(1)} async-done(((f32[64,24,128]{2,1,0:T(8,128)}), f32[64,24,128]{2,1,0:T(8,128)S(1)}, u32[]{:S(2)}, u32[]{:S(2)}) %all-to-all-start.1) | async-done | bytes 786464 | tf_op jit(solution)/shard_map/all_to_all | solution.py:388
  279.2 5.9 %all-to-all-start.2 = ((bf16[8,501,256]{2,1,0:T(8,128)(2,1)}), bf16[8,501,256]{2,1,0:T(8,128)(2,1)}, u32[]{:S(2)}, u32[]{:S(2)}) async-start(bf16[8,501,256]{2,1,0:T(8,128)(2,1)} %broadcast_in_dim.58), calls=%async_computation.2 | async-start | bytes 4128768 | tf_op jit(solution)/shard_map/all_to_all | solution.py:399
  286.8 26.4 %all-to-all-done.2 = bf16[8,501,256]{2,1,0:T(8,128)(2,1)} async-done(((bf16[8,501,256]{2,1,0:T(8,128)(2,1)}), bf16[8,501,256]{2,1,0:T(8,128)(2,1)}, u32[]{:S(2)}, u32[]{:S(2)}) %all-to-all-start.2) | async-done | bytes 2052128 | tf_op jit(solution)/shard_map/all_to_all | solution.py:399
  313.2 2.2 reshape.239
  315.4 2.7 convolution_bitcast_fusion
  (92 shorter events, 27.1 us)
Async XLA Ops:
  0.6 137.6 %copy-start = (bf16[256,256]{1,0:T(8,128)(2,1)S(1)}, bf16[256,256]{1,0:T(8,128)(2,1)}, u32[]{:S(2)}) copy-start(bf16[256,256]{1,0:T(8,128)(2,1)} %param.13) | copy-start | bytes 393220
  1.6 1.3 collective-permute-start
  3.6 126.4 %copy-start.6 = (bf16[64,1024]{1,0:T(8,128)(2,1)S(1)}, bf16[64,1024]{1,0:T(8,128)(2,1)}, u32[]{:S(2)}) copy-start(bf16[64,1024]{1,0:T(8,128)(2,1)} %maximum_select_fusion.1.after.refs_0_) | copy-start | bytes 393220
  3.6 132.3 %copy-start.12 = (s32[32]{0:T(128)S(1)}, s32[32]{0:T(128)}, u32[]{:S(2)}) copy-start(s32[32]{0:T(128)} %param.15) | copy-start | bytes 388
  3.6 132.4 %copy-start.13 = (s32[32]{0:T(128)S(1)}, s32[32]{0:T(128)}, u32[]{:S(2)}) copy-start(s32[32]{0:T(128)} %param.16) | copy-start | bytes 388
  129.8 11.0 %collective-permute-start.4 = (bf16[501,4096]{1,0:T(8,128)(2,1)}, bf16[501,4096]{1,0:T(8,128)(2,1)}, u32[]{:S(2)}, u32[]{:S(2)}) collective-permute-start(bf16[501,4096]{1,0:T(8,128)(2,1)} %shard_map.104), channel_id=1, source_target_pairs={{0,1},{1,0},{64,65},{65,64},{2,3},{3,2},{66,67},{67,66},{4,5},{5,4... | collective-permute-start | bytes 12312584 | tf_op jit(solution)/shard_map/ppermute | solution.py:43
  130.1 8.2 %collective-permute-start.3 = (bf16[64,1024]{1,0:T(8,128)(2,1)S(1)}, bf16[64,1024]{1,0:T(8,128)(2,1)S(1)}, u32[]{:S(2)}, u32[]{:S(2)}) collective-permute-start(bf16[64,1024]{1,0:T(8,128)(2,1)S(1)} %copy-done.6), channel_id=1, source_target_pairs={{0,2},{1,33},{64,66},{65,97},{2,0},{3,35},{66,64},{67,99},{4,6},{5... | collective-permute-start | bytes 393224 | tf_op jit(solution)/shard_map/ppermute | solution.py:48
  133.9 5.4 %collective-permute-start.2 = (bf16[64,1024]{1,0:T(8,128)(2,1)S(1)}, bf16[64,1024]{1,0:T(8,128)(2,1)S(1)}, u32[]{:S(2)}, u32[]{:S(2)}) collective-permute-start(bf16[64,1024]{1,0:T(8,128)(2,1)S(1)} %copy-done.6), channel_id=1, source_target_pairs={{0,66},{1,49},{64,0},{65,113},{2,64},{3,51},{66,2},{67,115},{4,70}... | collective-permute-start | bytes 393224 | tf_op jit(solution)/shard_map/ppermute | solution.py:48
  134.7 6.2 %collective-permute-start.1 = (bf16[64,1024]{1,0:T(8,128)(2,1)S(1)}, bf16[64,1024]{1,0:T(8,128)(2,1)S(1)}, u32[]{:S(2)}, u32[]{:S(2)}) collective-permute-start(bf16[64,1024]{1,0:T(8,128)(2,1)S(1)} %copy-done.6), channel_id=1, source_target_pairs={{0,64},{1,17},{64,2},{65,81},{2,66},{3,19},{66,0},{67,83},{4,68},{... | collective-permute-start | bytes 393224 | tf_op jit(solution)/shard_map/ppermute | solution.py:48
  143.4 16.6 %collective-permute-start.7 = (bf16[4,64,1024]{2,1,0:T(8,128)(2,1)}, bf16[4,64,1024]{2,1,0:T(8,128)(2,1)S(1)}, u32[]{:S(2)}, u32[]{:S(2)}) collective-permute-start(bf16[4,64,1024]{2,1,0:T(8,128)(2,1)} %shard_map.105.refs_0_), channel_id=1, source_target_pairs={{0,8},{1,9},{64,72},{65,73},{2,10},{3,11},{66,74},{67,75},{4,12},{... | collective-permute-start | bytes 1572872 | tf_op jit(solution)/shard_map/ppermute | solution.py:48
  146.6 20.5 %collective-permute-start.6 = (bf16[4,64,1024]{2,1,0:T(8,128)(2,1)}, bf16[4,64,1024]{2,1,0:T(8,128)(2,1)}, u32[]{:S(2)}, u32[]{:S(2)}) collective-permute-start(bf16[4,64,1024]{2,1,0:T(8,128)(2,1)} %shard_map.105.refs_0_), channel_id=1, source_target_pairs={{0,12},{1,13},{64,76},{65,77},{2,14},{3,15},{66,78},{67,79},{4,0},... | collective-permute-start | bytes 1572872 | tf_op jit(solution)/shard_map/ppermute | solution.py:48
  147.7 19.4 %collective-permute-start.5 = (bf16[4,64,1024]{2,1,0:T(8,128)(2,1)}, bf16[4,64,1024]{2,1,0:T(8,128)(2,1)}, u32[]{:S(2)}, u32[]{:S(2)}) collective-permute-start(bf16[4,64,1024]{2,1,0:T(8,128)(2,1)} %shard_map.105.refs_0_), channel_id=1, source_target_pairs={{0,4},{1,5},{64,68},{65,69},{2,6},{3,7},{66,70},{67,71},{4,8},{5,9... | collective-permute-start | bytes 1572872 | tf_op jit(solution)/shard_map/ppermute | solution.py:48
  151.2 33.7 %all-to-all-start = ((bf16[8,640,256]{2,1,0:T(8,128)(2,1)}), bf16[8,640,256]{2,1,0:T(8,128)(2,1)S(1)}, u32[]{:S(2)}, u32[]{:S(2)}) async-start(bf16[8,640,256]{2,1,0:T(8,128)(2,1)} %pad_maximum_fusion), calls=%async_computation | async-start | bytes 5242880 | tf_op jit(solution)/shard_map/all_to_all | solution.py:339
  170.1 41.7 %copy-start.14 = (f32[14]{0:T(128)S(1)}, f32[14]{0:T(128)}, u32[]{:S(2)}) copy-start(f32[14]{0:T(128)} %param.12) | copy-start | bytes 172
  170.1 41.7 %copy-start.15 = (s32[8]{0:T(128)S(1)}, s32[8]{0:T(128)}, u32[]{:S(2)}) copy-start(s32[8]{0:T(128)} %param.11) | copy-start | bytes 100
  170.1 36.2 %collective-permute-start.9 = (bf16[16,64,1024]{2,1,0:T(8,128)(2,1)}, bf16[16,64,1024]{2,1,0:T(8,128)(2,1)}, u32[]{:S(2)}, u32[]{:S(2)}) collective-permute-start(bf16[16,64,1024]{2,1,0:T(8,128)(2,1)} %bitcast.32), channel_id=1, source_target_pairs={{0,48},{1,67},{64,112},{65,1},{2,50},{3,65},{66,114},{67,3},{4,52}... | collective-permute-start | bytes 6291464 | tf_op jit(solution)/shard_map/ppermute | solution.py:344
  172.5 33.8 %collective-permute-start.8 = (bf16[16,64,1024]{2,1,0:T(8,128)(2,1)}, bf16[16,64,1024]{2,1,0:T(8,128)(2,1)}, u32[]{:S(2)}, u32[]{:S(2)}) collective-permute-start(bf16[16,64,1024]{2,1,0:T(8,128)(2,1)} %bitcast.33), channel_id=1, source_target_pairs={{0,16},{1,65},{64,80},{65,3},{2,18},{3,67},{66,82},{67,1},{4,20},{... | collective-permute-start | bytes 6291464 | tf_op jit(solution)/shard_map/ppermute | solution.py:343
  209.3 5.1 %collective-permute-start.12 = (bf16[8,640,256]{2,1,0:T(8,128)(2,1)}, bf16[8,640,256]{2,1,0:T(8,128)(2,1)S(1)}, u32[]{:S(2)}, u32[]{:S(2)}) collective-permute-start(bf16[8,640,256]{2,1,0:T(8,128)(2,1)} %get-tuple-element.16.own_ref), channel_id=1, source_target_pairs={{0,1},{1,0},{64,65},{65,64},{2,3},{3,2},{66,67},{67,66},{4,5},{5,4... | collective-permute-start | bytes 7864328 | tf_op jit(solution)/shard_map/ppermute | solution.py:43
  209.5 15.1 %collective-permute-start.10 = (bf16[8,64,1024]{2,1,0:T(8,128)(2,1)}, bf16[8,64,1024]{2,1,0:T(8,128)(2,1)}, u32[]{:S(2)}, u32[]{:S(2)}) collective-permute-start(bf16[8,64,1024]{2,1,0:T(8,128)(2,1)} %get-tuple-element.14), channel_id=1, source_target_pairs={{0,16},{1,65},{64,80},{65,3},{2,18},{3,67},{66,82},{67,1},{4,20},{... | collective-permute-start | bytes 3145736 | tf_op jit(solution)/shard_map/ppermute | solution.py:350
  210.2 15.1 %collective-permute-start.11 = (bf16[8,64,1024]{2,1,0:T(8,128)(2,1)}, bf16[8,64,1024]{2,1,0:T(8,128)(2,1)}, u32[]{:S(2)}, u32[]{:S(2)}) collective-permute-start(bf16[8,64,1024]{2,1,0:T(8,128)(2,1)} %get-tuple-element.15), channel_id=1, source_target_pairs={{0,48},{1,67},{64,112},{65,1},{2,50},{3,65},{66,114},{67,3},{4,52}... | collective-permute-start | bytes 3145736 | tf_op jit(solution)/shard_map/ppermute | solution.py:351
  247.5 26.1 %all-to-all-start.1 = ((f32[64,24,128]{2,1,0:T(8,128)}), f32[64,24,128]{2,1,0:T(8,128)S(1)}, u32[]{:S(2)}, u32[]{:S(2)}) async-start(f32[64,24,128]{2,1,0:T(8,128)} %broadcast_in_dim.56), calls=%async_computation.1 | async-start | bytes 1572864 | tf_op jit(solution)/shard_map/all_to_all | solution.py:388
  276.3 1.4 collective-permute-start.14
  279.2 34.0 %all-to-all-start.2 = ((bf16[8,501,256]{2,1,0:T(8,128)(2,1)}), bf16[8,501,256]{2,1,0:T(8,128)(2,1)}, u32[]{:S(2)}, u32[]{:S(2)}) async-start(bf16[8,501,256]{2,1,0:T(8,128)(2,1)} %broadcast_in_dim.58), calls=%async_computation.2 | async-start | bytes 4128768 | tf_op jit(solution)/shard_map/all_to_all | solution.py:399
  285.1 1.1 collective-permute-start.13
  (10 other events, 86.4 us)

commit v4 on v3

--- a/solution.py
+++ b/solution.py
@@ -1,3 +1,4 @@
+import functools
 import math
 import jax
 import jax.numpy as jnp
@@ -51,12 +52,17 @@
 
 def stack_kernel(*refs):
     for i in range(4):
-        refs[-1][i] = refs[i][...]
+        if len(refs[i].shape) == 2:
+            refs[-1][i] = refs[i][...]
+        else:
+            for j in range(4):
+                refs[-1][4 * j + i] = refs[i][j]
 
 
 def stack(blocks, after=()):
     vmem = pl.BlockSpec(memory_space=pltpu.VMEM)
-    shape = (4,) + blocks[0].shape
+    old = blocks[0].shape
+    shape = (4,) + old if len(old) == 2 else (4 * old[0],) + old[1:]
     return pl.pallas_call(
         stack_kernel,
         out_shape=jax.ShapeDtypeStruct(shape, jnp.bfloat16),
@@ -92,24 +98,32 @@
     )(before, after, through)
 
 
-def copy_kernel(value, after, out, sem):
-    copy = pltpu.make_async_copy(value, out, sem)
-    copy.start()
-    copy.wait()
-
-
-def copy_after(value, after):
-    hbm = pl.BlockSpec(memory_space=pl.ANY)
-    return pl.pallas_call(
-        copy_kernel,
-        out_shape=jax.ShapeDtypeStruct(value.shape, value.dtype),
-        in_specs=[hbm, hbm],
-        out_specs=hbm,
-        scratch_shapes=[pltpu.SemaphoreType.DMA(())],
-        cost_estimate=pl.CostEstimate(
-            flops=0, bytes_accessed=4 * math.prod(value.shape), transcendentals=0
-        ),
-    )(value, after)
+def reorder_kernel(w_ref, after, out_ref):
+    step = pl.program_id(0)
+    pairs = [w_ref[:, y * 128 : (y + 1) * 128] for y in range(SIDE)]
+    for zh in range(2):
+        for i in range(2):
+            lane = pl.multiple_of(zh * 2048 + step * 256 + i * 128, 128)
+            out_ref[:, pl.ds(lane, 128)] = jnp.concatenate(
+                [pair[:, zh * 64 : (zh + 1) * 64] for pair in pairs[2 * i : 2 * i + 2]], axis=1
+            )
+
+
+def reorder(weight, after):
+    cols, width = weight.shape
+    return pl.pallas_call(
+        reorder_kernel,
+        grid=(8,),
+        out_shape=jax.ShapeDtypeStruct((cols, width), weight.dtype),
+        in_specs=[
+            pl.BlockSpec((cols, 512), lambda i: (0, i)),
+            pl.BlockSpec(memory_space=pl.ANY),
+        ],
+        out_specs=pl.BlockSpec((cols, width), lambda i: (0, 0)),
+        cost_estimate=pl.CostEstimate(
+            flops=0, bytes_accessed=4 * cols * width, transcendentals=0
+        ),
+    )(weight, after)
 
 
 def finish_kernel(g_ref, e_own, e_other, l_own, l_other, stat_ref, mask_ref, ids_ref, base_ref, *outs):
@@ -217,36 +231,73 @@
     )
 
 
-def teacher_kernel(table, inv_tau, *refs):
-    groups, w_refs, l_refs = refs[0:5], refs[5:7], refs[7:9]
-    e_refs, stat_ref, hidden, sem = refs[9:11], refs[11], refs[12], refs[13]
-
-    def chunk_copy(ref, base, n):
-        row = pl.multiple_of(table[base + n] * 64, 64)
-        return pltpu.make_async_copy(ref.at[n], hidden.at[pl.ds(row, 64)], sem)
-
-    blocks = []
-    base = 0
-    for ref in groups:
-        blocks.append((ref, base))
-        base += ref.shape[0]
-    for ref, base in blocks:
-        def start(n, _, ref=ref, base=base):
-            chunk_copy(ref, base, n).start()
-            return 0
-        lax.fori_loop(0, ref.shape[0], start, 0)
-    for ref, base in blocks:
-        def wait(n, _, ref=ref, base=base):
-            chunk_copy(ref, base, n).wait()
-            return 0
-        lax.fori_loop(0, ref.shape[0], wait, 0)
+def gather_blocks(table, sources, w_refs, hidden, weights, sems):
+    copies = []
+    run = 0
+    for ref, slot, first in sources:
+        for s1 in range(first, first + ref.shape[0] // 4):
+            at = run * 256
+            for s2 in range(4):
+                row = pl.multiple_of(at + table[16 + s2] * 64, 64)
+                copies.append(
+                    pltpu.make_async_copy(
+                        ref.at[4 * (s1 - first) + s2], hidden.at[pl.ds(row, 64)], sems.at[0]
+                    )
+                )
+            lane = pl.multiple_of(table[slot * 4 + s1] * 256, 256)
+            for w, buf in zip(w_refs, weights):
+                copies.append(
+                    pltpu.make_async_copy(
+                        w.at[:, pl.ds(lane, 256)], buf.at[:, pl.ds(at, 256)], sems.at[1]
+                    )
+                )
+            run += 1
+    for copy in copies:
+        copy.start()
+    for copy in copies:
+        copy.wait()
+
+
+def partial_kernel(sources, first, *refs):
+    n = len(sources)
+    table, w_refs = refs[0], refs[1 : 3]
+    hidden_refs, refs = refs[3 : 3 + n], refs[3 + n :]
+    olds = refs[:0] if first else refs[:2]
+    outs = refs[len(olds) : len(olds) + 2]
+    hidden, *weights, sems = refs[len(olds) + 2 :]
+    gather_blocks(
+        table, [(r,) + s for r, s in zip(hidden_refs, sources)], w_refs, hidden, weights, sems
+    )
+
+    def tile(j, _):
+        lanes = pl.ds(pl.multiple_of(j * 256, 256), 256)
+        block = hidden[:, lanes]
+        for i in range(2):
+            part = jnp.dot(weights[i][...], block, preferred_element_type=jnp.float32)
+            outs[i][:, lanes] = part if first else olds[i][:, lanes] + part
+        return 0
+
+    lax.fori_loop(0, 4, tile, 0)
+
+
+def last_kernel(sources, *refs):
+    n = len(sources)
+    table, inv_tau, w_refs = refs[0], refs[1], refs[2:4]
+    hidden_refs, refs = refs[4 : 4 + n], refs[4 + n :]
+    olds, l_refs, e_refs, stat_ref = refs[0:2], refs[2:4], refs[4:6], refs[6]
+    hidden, *weights, sems = refs[7:]
+    gather_blocks(
+        table, [(r,) + s for r, s in zip(hidden_refs, sources)], w_refs, hidden, weights, sems
+    )
 
     def tile(j, _):
         lanes = pl.ds(pl.multiple_of(j * 256, 256), 256)
         scale = inv_tau[:, lanes]
         block = hidden[:, lanes]
         scores = [
-            jnp.dot(w[...], block, preferred_element_type=jnp.float32) * scale for w in w_refs
+            (olds[i][:, lanes] + jnp.dot(weights[i][...], block, preferred_element_type=jnp.float32))
+            * scale
+            for i in range(2)
         ]
         top = jnp.maximum(
             jnp.max(scores[0], axis=0, keepdims=True), jnp.max(scores[1], axis=0, keepdims=True)
@@ -269,30 +320,41 @@
     lax.fori_loop(0, 4, tile, 0)
 
 
-def teacher_scores(table, inv_tau, hidden, weights, logits):
-    cols, width = weights[0].shape
+def teacher_step(table, weights, hidden, sources, olds=(), last=()):
+    cols = weights[0].shape[0]
+    runs = sum(h.shape[0] for h in hidden) // 4
+    smem = pl.BlockSpec(memory_space=pltpu.SMEM)
     vmem = pl.BlockSpec(memory_space=pltpu.VMEM)
     hbm = pl.BlockSpec(memory_space=pl.ANY)
-    return pl.pallas_call(
-        teacher_kernel,
-        out_shape=[
-            jax.ShapeDtypeStruct((cols, 1024), jnp.float32),
-            jax.ShapeDtypeStruct((cols, 1024), jnp.float32),
-            jax.ShapeDtypeStruct((8, 1024), jnp.float32),
+    out_shape = [jax.ShapeDtypeStruct((cols, 1024), jnp.float32)] * 2
+    if last:
+        inv_tau, *logits = last
+        body = functools.partial(last_kernel, sources)
+        out_shape = out_shape + [jax.ShapeDtypeStruct((8, 1024), jnp.float32)]
+        args = (table, inv_tau, *weights, *hidden, *olds, *logits)
+        in_specs = [smem, vmem] + [hbm] * (2 + len(hidden)) + [vmem] * 4
+    else:
+        body = functools.partial(partial_kernel, sources, not olds)
+        args = (table, *weights, *hidden, *olds)
+        in_specs = [smem] + [hbm] * (2 + len(hidden)) + [vmem] * len(olds)
+    return pl.pallas_call(
+        body,
+        out_shape=out_shape,
+        in_specs=in_specs,
+        out_specs=[vmem] * len(out_shape),
+        scratch_shapes=[
+            pltpu.VMEM((runs * 256, 1024), jnp.bfloat16),
+            pltpu.VMEM((cols, runs * 256), jnp.bfloat16),
+            pltpu.VMEM((cols, runs * 256), jnp.bfloat16),
+            pltpu.SemaphoreType.DMA((2,)),
         ],
-        in_specs=[pl.BlockSpec(memory_space=pltpu.SMEM), vmem] + [hbm] * 5 + [vmem] * 4,
-        out_specs=[vmem] * 3,
-        scratch_shapes=[
-            pltpu.VMEM((width, 1024), jnp.bfloat16),
-            pltpu.SemaphoreType.DMA(()),
-        ],
-        compiler_params=pltpu.CompilerParams(vmem_limit_bytes=44 << 20),
-        cost_estimate=pl.CostEstimate(
-            flops=2 * 2 * cols * width * 1024,
-            bytes_accessed=2 * (2 * cols * width + width * 1024) + 8 * cols * 1024,
-            transcendentals=2 * cols * 1024,
-        ),
-    )(table, inv_tau, *hidden, *weights, *logits)
+        compiler_params=pltpu.CompilerParams(vmem_limit_bytes=28 << 20),
+        cost_estimate=pl.CostEstimate(
+            flops=2 * 2 * cols * runs * 256 * 1024,
+            bytes_accessed=2 * runs * 256 * (2 * cols + 1024) + 16 * cols * 1024,
+            transcendentals=2 * cols * 1024 if last else 0,
+        ),
+    )(*args)
 
 
 def on_device(
@@ -319,14 +381,15 @@
         for start in (core, 1 - core)
     ]
     unit = ordered(core, halves[0], sibling(halves[1]), 0)
-    w_own = teacher_weight.T
-    w_other = sibling(copy_after(w_own, unit))
-    hidden = stack(ring_gather(unit, "zx"), (w_other,))
+    blocks = ring_gather(unit, "zx")
+    w_own = reorder(teacher_weight.T, unit)
+    w_other = sibling(w_own)
+    weights = (w_own, w_other)
 
     meta = jnp.concatenate(
         [token_ids // 256, token_ids % 256, loss_mask, jnp.zeros((32,), jnp.int32)]
     ).astype(jnp.bfloat16)
-    meta = jnp.concatenate([meta, hidden[0, 0, :128]])[None, None]
+    meta = jnp.concatenate([meta, unit[0, :128]])[None, None]
     mine = lax.dynamic_slice_in_dim(student_hidden, core * half, half, axis=0)
     send = jnp.concatenate(
         [
@@ -338,18 +401,23 @@
     )
     got = lax.all_to_all(send, "variant", 0, 0, tiled=True)
 
-    hidden = stack(ring_gather(hidden, "yy")).reshape(16, 64, 1024)
+    hidden = stack(blocks, (send,))
+    hidden = stack(ring_gather(hidden, "yy"))
     plus, minus = ring_shift("xz", 1), ring_shift("xz", -1)
     before = lax.ppermute(hidden, AXES, plus)
     after = lax.ppermute(hidden, AXES, minus)
+    offsets = jnp.array(OFFSETS, jnp.int32)
+    o1, o3 = offsets[None, :], offsets[:, None]
+    px = (x + jnp.where(core == 0, o3, o1)) % 4
+    pz = (z + jnp.where(core == 0, o1, o3)) % 4
+    table = jnp.concatenate(
+        [((pz // 2 * 2 + pz % 2) * 4 + px).reshape(16), (y + offsets) % 4]
+    )
     lower, upper, got = forward_halves(before, after, got)
-    hidden = [
-        hidden,
-        before,
-        after,
-        lax.ppermute(lower, AXES, plus),
-        lax.ppermute(upper, AXES, minus),
-    ]
+    partial = teacher_step(
+        table, weights, (hidden, before, after), ((0, 0), (1, 0), (2, 0))
+    )
+    far = (lax.ppermute(lower, AXES, plus), lax.ppermute(upper, AXES, minus))
 
     got_other = sibling(got)
     meta_all = got[:, half + cols]
@@ -358,17 +426,6 @@
     ids_half = lax.dynamic_slice_in_dim(ids, core * half, half)
     mask_half = lax.dynamic_slice_in_dim(maskf, core * half, half)
 
-    offsets = jnp.array(OFFSETS, jnp.int32)
-    o1, o2, o3 = (
-        offsets.reshape(shape) for shape in ((1, 1, 4), (1, 4, 1), (4, 1, 1))
-    )
-    zero = jnp.zeros((4, 4, 4), jnp.int32)
-
-    def place(dx, dy, dz):
-        px, py, pz = (x + dx) % 4, (y + dy) % 4, (z + dz) % 4
-        return ((pz % 2 * 4 + px) * 8 + py * 2 + pz // 2 + zero).reshape(64)
-
-    table = jnp.where(core == 0, place(o3, o2, o1), place(o1, o2, o3))
     categories = jnp.arange(temps.shape[0], dtype=jnp.int32)
     taus = jnp.sum(
         jnp.where(variant_ids[:, None] == categories[None, :], temps[None, :], 0.0), axis=1
@@ -378,8 +435,8 @@
     base = jnp.stack([(b * 8 + a) * cols, ((b + 1 - 2 * core) * 8 + a) * cols])
     l_own, l_other, s_stats = student_logits(got, got_other, ids_half[None], base, cols)
     logits = (l_own, l_other)
-    e_own, e_other, stats = teacher_scores(
-        table, inv_tau, hidden, (w_own, w_other), logits
+    e_own, e_other, stats = teacher_step(
+        table, weights, far, ((3, 0), (3, 2)), partial, (inv_tau, l_own, l_other)
     )
     packed = jnp.concatenate([stats[:2].reshape(16, half), s_stats])
     groups = [

time: 321 us -> 187 us (0.58)
  Pallas kernels: 157 us -> 38.6 us
  waiting for transfers between devices: 99.9 us -> 82.9 us
    pallas_call x2 -> x3, Pallas kernels: 146 us -> 27.7 us  [the longest x2 20.3 us: teacher_step(): pl.pallas_call(body, out_shape=out_shape, in_specs=in_specs, out_specs=[v...]
    all_to_all x1, waiting for transfers between devices: 12.3 us -> 0.69 us  [on_device(): got = lax.all_to_all(send, 'variant', 0, 0, tiled=True)]
    ppermute x2, waiting for transfers between devices: 7.24 us -> 0.01 us  [on_device(): far = (lax.ppermute(lower, AXES, plus), lax.ppermute(upper, AXES, minus))]
    ppermute x6, waiting for transfers between devices: 13.7 us -> 17.3 us  [ring_gather(): lax.ppermute(value, AXES, ring_shift(axes, step))]
  transfers between devices with their start and end apart: 18 -> 18, of which waited for: 14 -> 10; matrix products, arithmetic and copies ran while one was open for 2% -> 4% of each run, Pallas kernels for 2% -> 16%
where the time goes in v4:
time: 187 us; the launch traced here: 185 us
  waiting for transfers between devices  82.9 us (44%)
  Pallas kernels  38.6 us (21%)
  starting transfers between devices  38.4 us (21%)
  local copies, waits for them, and re-layouts  17.4 us (9%)
  other arithmetic  3.73 us (2%)
  matrix products  2.69 us (1%)
    all_to_all x1, waiting for transfers between devices, on_device(): lax.all_to_all(jnp.broadcast_to(error[None], (8, cols, 256)), 'variant',...  26.4 us
    ppermute x1, waiting for transfers between devices, on_device(): after = lax.ppermute(hidden, AXES, minus)  21.5 us
    pallas_call x2, Pallas kernels, teacher_step(): pl.pallas_call(body, out_shape=out_shape, in_specs=in_specs, out_specs=[v...  20.3 us
    ppermute x6, waiting for transfers between devices, ring_gather(): lax.ppermute(value, AXES, ring_shift(axes, step))  17.3 us
    all_to_all x1, waiting for transfers between devices, on_device(): lax.all_to_all(jnp.broadcast_to(packed[None], (64, 24, half)), AXES, 0, 0...  14.5 us
    ppermute x6, starting transfers between devices, ring_gather(): lax.ppermute(value, AXES, ring_shift(axes, step))  11.2 us
    all_to_all x1, starting transfers between devices, on_device(): lax.all_to_all(jnp.broadcast_to(packed[None], (64, 24, half)), AXES, 0, 0...  10.4 us
    unnamed x34, local copies, waits for them, and re-layouts  8.55 us
  transfers between devices with their start and end apart: 18, of which 10 were waited for; matrix products, arithmetic and copies ran while one was open for 4% of the time, Pallas kernels for 16%

profile of v4, /device:TPU:2, one launch (start us, length us, event | category | flops | bytes accessed | tf_op | source)
XLA Modules:
  0.0 184.6 jit_solution(5464213910108219544)
XLA Ops:
  3.1 2.2 %reshape.79 = bf16[8,501,256]{2,1,0:T(8,128)(2,1)S(1)} reshape(bf16[4008,256]{1,0:T(8,128)(2,1)} %bitcast.35) | data formatting | bytes 4104192 | tf_op jit(solution)/shard_map/reshape | solution.py:397
  5.3 4.0 %collective-permute-start.4 = (bf16[64,1024]{1,0:T(8,128)(2,1)S(1)}, bf16[64,1024]{1,0:T(8,128)(2,1)S(1)}, u32[]{:S(2)}, u32[]{:S(2)}) collective-permute-start(bf16[64,1024]{1,0:T(8,128)(2,1)S(1)} %maximum_select_fusion.1.after.refs_0_), channel_id=1, source_target_pairs={{0,2},{1,33},{64,66},{65,97},{2,0},{3,35},{66,64},{67,99},{4,6},{5... | collective-permute-start | bytes 393224 | tf_op jit(solution)/shard_map/ppermute | solution.py:49
  11.5 1.7 pad_maximum_fusion.refs_4_
  16.9 1.9 %shard_map.105.refs_0_ = bf16[4,64,1024]{2,1,0:T(8,128)(2,1)} custom-call(bf16[64,1024]{1,0:T(8,128)(2,1)} %copy-done.8, bf16[64,1024]{1,0:T(8,128)(2,1)} %copy-done.12, bf16[64,1024]{1,0:T(8,128)(2,1)} %copy-done.11, bf16[64,1024]{1,0:T(8,128)(2,1)} %copy-done.10, bf16[8,640,256]{2,1,0:T(8,128)(2,1)} %pad_maximum_fusion.refs_4_), custom_call_target="tpu_custom_call" | custom-call | bytes 1048576 | tf_op jit(solution)/shard_map/pallas_call | solution.py:66
  18.8 3.2 %collective-permute-start.7 = (bf16[4,64,1024]{2,1,0:T(8,128)(2,1)}, bf16[4,64,1024]{2,1,0:T(8,128)(2,1)S(1)}, u32[]{:S(2)}, u32[]{:S(2)}) collective-permute-start(bf16[4,64,1024]{2,1,0:T(8,128)(2,1)} %shard_map.105.refs_0_), channel_id=1, source_target_pairs={{0,8},{1,9},{64,72},{65,73},{2,10},{3,11},{66,74},{67,75},{4,12},{... | collective-permute-start | bytes 1572872 | tf_op jit(solution)/shard_map/ppermute | solution.py:49
  24.0 4.8 %all-to-all-start = ((bf16[8,640,256]{2,1,0:T(8,128)(2,1)}), bf16[8,640,256]{2,1,0:T(8,128)(2,1)S(1)}, u32[]{:S(2)}, u32[]{:S(2)}) async-start(bf16[8,640,256]{2,1,0:T(8,128)(2,1)} %pad_maximum_fusion.refs_4_), calls=%async_computation | async-start | bytes 5242880 | tf_op jit(solution)/shard_map/all_to_all | solution.py:402
  28.8 6.6 %collective-permute-done.7.refs_3_ = bf16[4,64,1024]{2,1,0:T(8,128)(2,1)S(1)} collective-permute-done((bf16[4,64,1024]{2,1,0:T(8,128)(2,1)}, bf16[4,64,1024]{2,1,0:T(8,128)(2,1)S(1)}, u32[]{:S(2)}, u32[]{:S(2)}) %collective-permute-start.7) | collective-permute-done | bytes 524320 | tf_op jit(solution)/shard_map/ppermute | solution.py:49
  35.4 7.8 %collective-permute-done.6.refs_2_ = bf16[4,64,1024]{2,1,0:T(8,128)(2,1)} collective-permute-done((bf16[4,64,1024]{2,1,0:T(8,128)(2,1)}, bf16[4,64,1024]{2,1,0:T(8,128)(2,1)}, u32[]{:S(2)}, u32[]{:S(2)}) %collective-permute-start.6) | collective-permute-done | bytes 524320 | tf_op jit(solution)/shard_map/ppermute | solution.py:49
  43.1 3.0 %shard_map.106.refs_3_ = bf16[16,64,1024]{2,1,0:T(8,128)(2,1)} custom-call(bf16[4,64,1024]{2,1,0:T(8,128)(2,1)} %shard_map.105.refs_0_, bf16[4,64,1024]{2,1,0:T(8,128)(2,1)} %collective-permute-done.5.refs_1_, bf16[4,64,1024]{2,1,0:T(8,128)(2,1)} %collective-permute-done.6.refs_2_, bf16[4,64,1024]{2,1,0:T(8,128)(2,1)} %copy-done.9), custom_call_target="tpu_custom_call" | custom-call | bytes 4194304 | tf_op jit(solution)/shard_map/pallas_call | solution.py:66
  46.2 1.8 collective-permute-start.9
  48.2 7.4 %shard_map.104.refs_1_.refs_2_ = bf16[501,4096]{1,0:T(8,128)(2,1)} custom-call(bf16[501,4096]{1,0:T(8,128)(2,1)} %bitcast.34, bf16[64,1024]{1,0:T(8,128)(2,1)} %copy-done.8), custom_call_target="tpu_custom_call" | custom-call | bytes 8208384 | tf_op jit(solution)/shard_map/pallas_call | solution.py:114
  55.6 1.7 collective-permute-start.1
  57.9 21.5 %collective-permute-done.9.after.refs_5_ = bf16[16,64,1024]{2,1,0:T(8,128)(2,1)} collective-permute-done((bf16[16,64,1024]{2,1,0:T(8,128)(2,1)}, bf16[16,64,1024]{2,1,0:T(8,128)(2,1)}, u32[]{:S(2)}, u32[]{:S(2)}) %collective-permute-start.9) | collective-permute-done | bytes 2097184 | tf_op jit(solution)/shard_map/ppermute | solution.py:408
  79.4 2.9 %shard_map.107 = (bf16[8,64,1024]{2,1,0:T(8,128)(2,1)}, bf16[8,64,1024]{2,1,0:T(8,128)(2,1)}, bf16[8,640,256]{2,1,0:T(8,128)(2,1)}) custom-call(bf16[16,64,1024]{2,1,0:T(8,128)(2,1)} %collective-permute-done.8.before.refs_4_, bf16[16,64,1024]{2,1,0:T(8,128)(2,1)} %collective-permute-done.9.after.refs_5_, ...), custom_call_target="tpu_custom_call", output_to_operand_aliasing={{2}: (2, {})} | custom-call | bytes 4194304 | tf_op jit(solution)/shard_map/pallas_call | solution.py:87
  86.2 2.3 %copy-done.3 = bf16[501,4096]{1,0:T(8,128)(2,1)S(1)} copy-done((bf16[501,4096]{1,0:T(8,128)(2,1)S(1)}, bf16[501,4096]{1,0:T(8,128)(2,1)}, u32[]{:S(2)}) %copy-start.3) | copy-done | bytes 4104216
  90.1 13.6 %shard_map.108 = (f32[501,1024]{1,0:T(8,128)S(1)}, f32[501,1024]{1,0:T(8,128)S(1)}) custom-call(s32[20]{0:T(128)S(1)} %pad_add_fusion.refs_0_, bf16[501,4096]{1,0:T(8,128)(2,1)S(1)} %copy-done.3, bf16[501,4096]{1,0:T(8,128)(2,1)} %collective-permute-done.1.refs_2_.refs_3_, bf16[16,64,1024]{2,1,0:T(8,128)(2,1)S(1)} %copy-done.5, ...), custom_call_target="tpu_custom_call" | custom-call | flops 6304038912 | bytes 20656128 | tf_op jit(solution)/shard_map/pallas_call | solution.py:340
  103.7 1.9 %shard_map.109 = (f32[501,128]{1,0:T(8,128)S(1)}, f32[501,128]{1,0:T(8,128)S(1)}, f32[8,128]{1,0:T(8,128)S(1)}) custom-call(bf16[8,640,256]{2,1,0:T(8,128)(2,1)S(1)} %copy-done.2, bf16[8,640,256]{2,1,0:T(8,128)(2,1)S(1)} %collective-permute-done.12.other_ref, s32[1,128]{1,0:T(1,128)S(1)} %dynamic-slice_bitcast_fusion.3.ids_ref, s32[2]{0:T(128)S(1)} %pad_add_fusion.1.base_ref), custom_call_target="tpu_custom_call" | custom-call | flops 525336576 | bytes 12582912 | tf_op jit(solution)/shard_map/pallas_call | solution.py:210
  105.9 6.7 %shard_map.110 = (f32[501,1024]{1,0:T(8,128)S(1)}, f32[501,1024]{1,0:T(8,128)S(1)}, f32[8,1024]{1,0:T(8,128)S(1)}) custom-call(s32[20]{0:T(128)S(1)} %pad_add_fusion.refs_0_, f32[1,1024]{1,0:T(1,128)S(1)} %bitcast.31, bf16[501,4096]{1,0:T(8,128)(2,1)S(1)} %copy-done.4, bf16[501,4096]{1,0:T(8,128)(2,1)} %collective-permute-done.1.refs_2_.refs_3_, ...), custom_call_target="tpu_custom_call" | custom-call | flops 2101346304 | bytes 12357632 | tf_op jit(solution)/shard_map/pallas_call | solution.py:340
  114.9 10.4 %all-to-all-start.1 = ((f32[64,24,128]{2,1,0:T(8,128)}), f32[64,24,128]{2,1,0:T(8,128)S(1)}, u32[]{:S(2)}, u32[]{:S(2)}) async-start(f32[64,24,128]{2,1,0:T(8,128)} %broadcast_in_dim.88), calls=%async_computation.1 | async-start | bytes 1572864 | tf_op jit(solution)/shard_map/all_to_all | solution.py:445
  125.5 14.5 %all-to-all-done.1.g_ref = f32[64,24,128]{2,1,0:T(8,128)S(1)} async-done(((f32[64,24,128]{2,1,0:T(8,128)}), f32[64,24,128]{2,1,0:T(8,128)S(1)}, u32[]{:S(2)}, u32[]{:S(2)}) %all-to-all-start.1) | async-done | bytes 786464 | tf_op jit(solution)/shard_map/all_to_all | solution.py:445
  145.8 5.9 %all-to-all-start.2 = ((bf16[8,501,256]{2,1,0:T(8,128)(2,1)}), bf16[8,501,256]{2,1,0:T(8,128)(2,1)}, u32[]{:S(2)}, u32[]{:S(2)}) async-start(bf16[8,501,256]{2,1,0:T(8,128)(2,1)} %broadcast_in_dim.90), calls=%async_computation.2 | async-start | bytes 4128768 | tf_op jit(solution)/shard_map/all_to_all | solution.py:456
  153.4 26.4 %all-to-all-done.2 = bf16[8,501,256]{2,1,0:T(8,128)(2,1)} async-done(((bf16[8,501,256]{2,1,0:T(8,128)(2,1)}), bf16[8,501,256]{2,1,0:T(8,128)(2,1)}, u32[]{:S(2)}, u32[]{:S(2)}) %all-to-all-start.2) | async-done | bytes 2052128 | tf_op jit(solution)/shard_map/all_to_all | solution.py:456
  179.7 2.2 %reshape.84 = bf16[4008,256]{1,0:T(8,128)(2,1)S(1)} reshape(bf16[8,501,256]{2,1,0:T(8,128)(2,1)} %all-to-all-done.2) | data formatting | bytes 4104192 | tf_op jit(solution)/shard_map/reshape | solution.py:458
  181.9 2.7 %convolution_bitcast_fusion = f32[256,4008]{0,1:T(8,128)} fusion(bf16[4008,256]{1,0:T(8,128)(2,1)S(1)} %reshape.84, bf16[256,256]{1,0:T(8,128)(2,1)S(1)} %copy-done), kind=kOutput, calls=%fused_computation | convolution fusion | flops 525336576 | bytes 6287360 | tf_op jit(solution)/shard_map/dot_general | solution.py:459
  (94 shorter events, 26.8 us)
Async XLA Ops:
  1.6 3.7 %collective-permute-start = (bf16[32,1024]{1,0:T(8,128)(2,1)S(1)}, bf16[32,1024]{1,0:T(8,128)(2,1)S(1)}, u32[]{:S(2)}, u32[]{:S(2)}) collective-permute-start(bf16[32,1024]{1,0:T(8,128)(2,1)S(1)} %bitcast.37), channel_id=1, source_target_pairs={{0,1},{1,0},{64,65},{65,64},{2,3},{3,2},{66,67},{67,66},{4,5},{5,4... | collective-permute-start | bytes 196616 | tf_op jit(solution)/shard_map/ppermute | solution.py:44
  5.3 7.8 %copy-start.8 = (bf16[64,1024]{1,0:T(8,128)(2,1)}, bf16[64,1024]{1,0:T(8,128)(2,1)S(1)}, u32[]{:S(2)}) copy-start(bf16[64,1024]{1,0:T(8,128)(2,1)S(1)} %maximum_select_fusion.1.after.refs_0_) | copy-start | bytes 393220
  5.3 7.8 %collective-permute-start.4 = (bf16[64,1024]{1,0:T(8,128)(2,1)S(1)}, bf16[64,1024]{1,0:T(8,128)(2,1)S(1)}, u32[]{:S(2)}, u32[]{:S(2)}) collective-permute-start(bf16[64,1024]{1,0:T(8,128)(2,1)S(1)} %maximum_select_fusion.1.after.refs_0_), channel_id=1, source_target_pairs={{0,2},{1,33},{64,66},{65,97},{2,0},{3,35},{66,64},{67,99},{4,6},{5... | collective-permute-start | bytes 393224 | tf_op jit(solution)/shard_map/ppermute | solution.py:49
  9.3 5.4 %collective-permute-start.3 = (bf16[64,1024]{1,0:T(8,128)(2,1)S(1)}, bf16[64,1024]{1,0:T(8,128)(2,1)S(1)}, u32[]{:S(2)}, u32[]{:S(2)}) collective-permute-start(bf16[64,1024]{1,0:T(8,128)(2,1)S(1)} %maximum_select_fusion.1.after.refs_0_), channel_id=1, source_target_pairs={{0,66},{1,49},{64,0},{65,113},{2,64},{3,51},{66,2},{67,115},{4,70}... | collective-permute-start | bytes 393224 | tf_op jit(solution)/shard_map/ppermute | solution.py:49
  10.0 6.2 %collective-permute-start.2 = (bf16[64,1024]{1,0:T(8,128)(2,1)S(1)}, bf16[64,1024]{1,0:T(8,128)(2,1)S(1)}, u32[]{:S(2)}, u32[]{:S(2)}) collective-permute-start(bf16[64,1024]{1,0:T(8,128)(2,1)S(1)} %maximum_select_fusion.1.after.refs_0_), channel_id=1, source_target_pairs={{0,64},{1,17},{64,2},{65,81},{2,66},{3,19},{66,0},{67,83},{4,68},{... | collective-permute-start | bytes 393224 | tf_op jit(solution)/shard_map/ppermute | solution.py:49
  18.8 16.6 %collective-permute-start.7 = (bf16[4,64,1024]{2,1,0:T(8,128)(2,1)}, bf16[4,64,1024]{2,1,0:T(8,128)(2,1)S(1)}, u32[]{:S(2)}, u32[]{:S(2)}) collective-permute-start(bf16[4,64,1024]{2,1,0:T(8,128)(2,1)} %shard_map.105.refs_0_), channel_id=1, source_target_pairs={{0,8},{1,9},{64,72},{65,73},{2,10},{3,11},{66,74},{67,75},{4,12},{... | collective-permute-start | bytes 1572872 | tf_op jit(solution)/shard_map/ppermute | solution.py:49
  22.0 21.2 %collective-permute-start.6 = (bf16[4,64,1024]{2,1,0:T(8,128)(2,1)}, bf16[4,64,1024]{2,1,0:T(8,128)(2,1)}, u32[]{:S(2)}, u32[]{:S(2)}) collective-permute-start(bf16[4,64,1024]{2,1,0:T(8,128)(2,1)} %shard_map.105.refs_0_), channel_id=1, source_target_pairs={{0,12},{1,13},{64,76},{65,77},{2,14},{3,15},{66,78},{67,79},{4,0},... | collective-permute-start | bytes 1572872 | tf_op jit(solution)/shard_map/ppermute | solution.py:49
  23.0 20.1 %collective-permute-start.5 = (bf16[4,64,1024]{2,1,0:T(8,128)(2,1)}, bf16[4,64,1024]{2,1,0:T(8,128)(2,1)}, u32[]{:S(2)}, u32[]{:S(2)}) collective-permute-start(bf16[4,64,1024]{2,1,0:T(8,128)(2,1)} %shard_map.105.refs_0_), channel_id=1, source_target_pairs={{0,4},{1,5},{64,68},{65,69},{2,6},{3,7},{66,70},{67,71},{4,8},{5,9... | collective-permute-start | bytes 1572872 | tf_op jit(solution)/shard_map/ppermute | solution.py:49
  24.0 33.9 %all-to-all-start = ((bf16[8,640,256]{2,1,0:T(8,128)(2,1)}), bf16[8,640,256]{2,1,0:T(8,128)(2,1)S(1)}, u32[]{:S(2)}, u32[]{:S(2)}) async-start(bf16[8,640,256]{2,1,0:T(8,128)(2,1)} %pad_maximum_fusion.refs_4_), calls=%async_computation | async-start | bytes 5242880 | tf_op jit(solution)/shard_map/all_to_all | solution.py:402
  46.2 33.2 %collective-permute-start.9 = (bf16[16,64,1024]{2,1,0:T(8,128)(2,1)}, bf16[16,64,1024]{2,1,0:T(8,128)(2,1)}, u32[]{:S(2)}, u32[]{:S(2)}) collective-permute-start(bf16[16,64,1024]{2,1,0:T(8,128)(2,1)} %shard_map.106.refs_3_), channel_id=1, source_target_pairs={{0,48},{1,67},{64,112},{65,1},{2,50},{3,65},{66,114},{67,3},{4,52}... | collective-permute-start | bytes 6291464 | tf_op jit(solution)/shard_map/ppermute | solution.py:408
  47.9 31.4 %collective-permute-start.8 = (bf16[16,64,1024]{2,1,0:T(8,128)(2,1)}, bf16[16,64,1024]{2,1,0:T(8,128)(2,1)}, u32[]{:S(2)}, u32[]{:S(2)}) collective-permute-start(bf16[16,64,1024]{2,1,0:T(8,128)(2,1)} %shard_map.106.refs_3_), channel_id=1, source_target_pairs={{0,16},{1,65},{64,80},{65,3},{2,18},{3,67},{66,82},{67,1},{4,20},{... | collective-permute-start | bytes 6291464 | tf_op jit(solution)/shard_map/ppermute | solution.py:407
  55.6 26.9 %copy-start.13 = (s32[4]{0:T(128)S(1)}, s32[4]{0:T(128)}, u32[]{:S(2)}) copy-start(s32[4]{0:T(128)} %constant.143.clone) | copy-start | bytes 52
  55.6 27.2 %copy-start.14 = (f32[14]{0:T(128)S(1)}, f32[14]{0:T(128)}, u32[]{:S(2)}) copy-start(f32[14]{0:T(128)} %param.12) | copy-start | bytes 172
  55.6 27.2 %copy-start.15 = (s32[8]{0:T(128)S(1)}, s32[8]{0:T(128)}, u32[]{:S(2)}) copy-start(s32[8]{0:T(128)} %param.11) | copy-start | bytes 100
  55.6 30.6 %collective-permute-start.1 = (bf16[501,4096]{1,0:T(8,128)(2,1)}, bf16[501,4096]{1,0:T(8,128)(2,1)}, u32[]{:S(2)}, u32[]{:S(2)}) collective-permute-start(bf16[501,4096]{1,0:T(8,128)(2,1)} %shard_map.104.refs_1_.refs_2_), channel_id=1, source_target_pairs={{0,1},{1,0},{64,65},{65,64},{2,3},{3,2},{66,67},{67,66},{4,5},{5,4... | collective-permute-start | bytes 12312584 | tf_op jit(solution)/shard_map/ppermute | solution.py:44
  57.9 21.5 %copy-start.1 = (bf16[8,640,256]{2,1,0:T(8,128)(2,1)}, bf16[8,640,256]{2,1,0:T(8,128)(2,1)S(1)}, u32[]{:S(2)}) copy-start(bf16[8,640,256]{2,1,0:T(8,128)(2,1)S(1)} %all-to-all-done.through_in) | copy-start | bytes 7864324
  82.3 21.4 %collective-permute-start.12 = (bf16[8,640,256]{2,1,0:T(8,128)(2,1)}, bf16[8,640,256]{2,1,0:T(8,128)(2,1)S(1)}, u32[]{:S(2)}, u32[]{:S(2)}) collective-permute-start(bf16[8,640,256]{2,1,0:T(8,128)(2,1)} %get-tuple-element.20.own_ref), channel_id=1, source_target_pairs={{0,1},{1,0},{64,65},{65,64},{2,3},{3,2},{66,67},{67,66},{4,5},{5,4... | collective-permute-start | bytes 7864328 | tf_op jit(solution)/shard_map/ppermute | solution.py:44
  83.0 22.7 %collective-permute-start.10 = (bf16[8,64,1024]{2,1,0:T(8,128)(2,1)}, bf16[8,64,1024]{2,1,0:T(8,128)(2,1)}, u32[]{:S(2)}, u32[]{:S(2)}) collective-permute-start(bf16[8,64,1024]{2,1,0:T(8,128)(2,1)} %get-tuple-element.16), channel_id=1, source_target_pairs={{0,16},{1,65},{64,80},{65,3},{2,18},{3,67},{66,82},{67,1},{4,20},{... | collective-permute-start | bytes 3145736 | tf_op jit(solution)/shard_map/ppermute | solution.py:420
  83.7 22.0 %collective-permute-start.11 = (bf16[8,64,1024]{2,1,0:T(8,128)(2,1)}, bf16[8,64,1024]{2,1,0:T(8,128)(2,1)}, u32[]{:S(2)}, u32[]{:S(2)}) collective-permute-start(bf16[8,64,1024]{2,1,0:T(8,128)(2,1)} %get-tuple-element.17), channel_id=1, source_target_pairs={{0,48},{1,67},{64,112},{65,1},{2,50},{3,65},{66,114},{67,3},{4,52}... | collective-permute-start | bytes 3145736 | tf_op jit(solution)/shard_map/ppermute | solution.py:420
  86.2 17.6 %copy-start.2 = (bf16[8,640,256]{2,1,0:T(8,128)(2,1)S(1)}, bf16[8,640,256]{2,1,0:T(8,128)(2,1)}, u32[]{:S(2)}) copy-start(bf16[8,640,256]{2,1,0:T(8,128)(2,1)} %get-tuple-element.20.own_ref) | copy-start | bytes 7864324
  114.9 25.2 %all-to-all-start.1 = ((f32[64,24,128]{2,1,0:T(8,128)}), f32[64,24,128]{2,1,0:T(8,128)S(1)}, u32[]{:S(2)}, u32[]{:S(2)}) async-start(f32[64,24,128]{2,1,0:T(8,128)} %broadcast_in_dim.88), calls=%async_computation.1 | async-start | bytes 1572864 | tf_op jit(solution)/shard_map/all_to_all | solution.py:445
  142.8 1.4 collective-permute-start.14
  145.8 34.0 %all-to-all-start.2 = ((bf16[8,501,256]{2,1,0:T(8,128)(2,1)}), bf16[8,501,256]{2,1,0:T(8,128)(2,1)}, u32[]{:S(2)}, u32[]{:S(2)}) async-start(bf16[8,501,256]{2,1,0:T(8,128)(2,1)} %broadcast_in_dim.90), calls=%async_computation.2 | async-start | bytes 4128768 | tf_op jit(solution)/shard_map/all_to_all | solution.py:456
  151.6 1.1 collective-permute-start.13
  (10 other events, 26.6 us)

commit v5 on v4

--- a/solution.py
+++ b/solution.py
@@ -126,8 +126,8 @@
     )(weight, after)
 
 
-def finish_kernel(g_ref, e_own, e_other, l_own, l_other, stat_ref, mask_ref, ids_ref, base_ref, *outs):
-    err_refs, loss_ref = outs[0:2], outs[2]
+def finish_kernel(g_ref, e_ref, l_own, l_other, top_ref, mask_ref, ids_ref, base_ref, *outs):
+    err_ref, loss_ref = outs
     cols, half = l_own.shape
     near = g_ref[:, 0:8, :]
     top = jnp.max(near, axis=0)
@@ -141,39 +141,80 @@
     hard = jnp.sum(g_ref[:, 17, :], axis=0, keepdims=True) - s_lse
     mask = mask_ref[...]
     loss_ref[...] = mask * (-mix_weight * (soft - s_lse) - (1.0 - mix_weight) * hard)
-    factors = [
-        jnp.exp(stat_ref[2:3, v * half : (v + 1) * half] - lse[v : v + 1]) * (mix_weight / 8)
-        for v in range(8)
-    ]
+    factors = jnp.exp(top_ref[...] - lse) * (mix_weight / 8)
     scale = loss_scale * mask
     rows = lax.broadcasted_iota(jnp.int32, (cols, half), 0)
-    for i, (e, l) in enumerate(((e_own, l_own), (e_other, l_other))):
+    core = base_ref[2]
+    for i, l in enumerate((l_own, l_other)):
         value = jnp.exp(l[...] - s_lse)
         hit = rows + base_ref[i] == ids_ref[...]
         value -= jnp.where(hit, 1.0 - mix_weight, 0.0)
-        averaged = e[:, 0:half] * factors[0]
+        averaged = e_ref[i, :, 0:half] * factors[0:1]
         for v in range(1, 8):
-            averaged += e[:, v * half : (v + 1) * half] * factors[v]
-        err_refs[i][...] = (scale * (value - averaged)).astype(jnp.bfloat16)
-
-
-def finish(gathered, e, logits, stats, mask, ids, base):
+            averaged += e_ref[i, :, v * half : (v + 1) * half] * factors[v : v + 1]
+        error = (scale * (value - averaged)).astype(jnp.bfloat16)
+        target = core if i == 0 else 1 - core
+
+        def spread(k, _, error=error, target=target):
+            err_ref[2 * k + target] = error
+            return 0
+
+        lax.fori_loop(0, 8, spread, 0)
+
+
+def finish(gathered, e, logits, top, mask, ids, base):
     cols, half = logits[0].shape
     vmem = pl.BlockSpec(memory_space=pltpu.VMEM)
     return pl.pallas_call(
         finish_kernel,
         out_shape=[
-            jax.ShapeDtypeStruct((cols, half), jnp.bfloat16),
-            jax.ShapeDtypeStruct((cols, half), jnp.bfloat16),
+            jax.ShapeDtypeStruct((16, cols, half), jnp.bfloat16),
             jax.ShapeDtypeStruct((1, half), jnp.float32),
         ],
-        in_specs=[vmem] * 8 + [pl.BlockSpec(memory_space=pltpu.SMEM)],
-        out_specs=[vmem] * 3,
-        compiler_params=pltpu.CompilerParams(vmem_limit_bytes=24 << 20),
-        cost_estimate=pl.CostEstimate(
-            flops=40 * cols * half, bytes_accessed=10 * cols * 1024, transcendentals=2 * cols * half
-        ),
-    )(gathered, *e, *logits, stats, mask, ids, base)
+        in_specs=[vmem] * 7 + [pl.BlockSpec(memory_space=pltpu.SMEM)],
+        out_specs=[vmem] * 2,
+        compiler_params=pltpu.CompilerParams(vmem_limit_bytes=16 << 20),
+        cost_estimate=pl.CostEstimate(
+            flops=40 * cols * half, bytes_accessed=12 * cols * 1024, transcendentals=2 * cols * half
+        ),
+    )(gathered, e, *logits, top, mask, ids, base)
+
+
+def grad_kernel(err_ref, hidden_ref, out_ref, rows_ref, sem):
+    blocks, cols = err_ref.shape[0] // 2, err_ref.shape[1]
+    copies, done = [], 0
+    for k in range(blocks):
+        error = jnp.concatenate([err_ref[2 * k], err_ref[2 * k + 1]], axis=1)
+        rows_ref[k * cols : (k + 1) * cols, :] = jnp.dot(
+            error, hidden_ref[...], preferred_element_type=jnp.float32
+        )
+        ready = (k + 1) * cols // 8 * 8
+        here = pl.ds(done, ready - done)
+        copies.append(pltpu.make_async_copy(rows_ref.at[here], out_ref.at[here], sem.at[k]))
+        copies[-1].start()
+        done = ready
+    for copy in copies:
+        copy.wait()
+
+
+def student_gradient(errors, hidden):
+    blocks, cols = errors.shape[0] // 2, errors.shape[1]
+    vmem = pl.BlockSpec(memory_space=pltpu.VMEM)
+    width = hidden.shape[1]
+    return pl.pallas_call(
+        grad_kernel,
+        out_shape=jax.ShapeDtypeStruct((blocks * cols, width), jnp.float32),
+        in_specs=[vmem, vmem],
+        out_specs=pl.BlockSpec(memory_space=pltpu.HBM),
+        scratch_shapes=[
+            pltpu.VMEM((blocks * cols, width), jnp.float32),
+            pltpu.SemaphoreType.DMA((blocks,)),
+        ],
+        compiler_params=pltpu.CompilerParams(vmem_limit_bytes=16 << 20),
+        cost_estimate=pl.CostEstimate(
+            flops=2 * blocks * cols * 256 * width, bytes_accessed=7 << 20, transcendentals=0
+        ),
+    )(errors, hidden)
 
 
 def student_kernel(own_ref, other_ref, ids_ref, base_ref, l_own, l_other, stat_ref):
@@ -284,14 +325,14 @@
     n = len(sources)
     table, inv_tau, w_refs = refs[0], refs[1], refs[2:4]
     hidden_refs, refs = refs[4 : 4 + n], refs[4 + n :]
-    olds, l_refs, e_refs, stat_ref = refs[0:2], refs[2:4], refs[4:6], refs[6]
-    hidden, *weights, sems = refs[7:]
+    olds, l_refs, student = refs[0:2], refs[2:4], refs[4]
+    e_ref, top_ref, stat_ref = refs[5:8]
+    hidden, *weights, sems = refs[8:]
     gather_blocks(
         table, [(r,) + s for r, s in zip(hidden_refs, sources)], w_refs, hidden, weights, sems
     )
-
-    def tile(j, _):
-        lanes = pl.ds(pl.multiple_of(j * 256, 256), 256)
+    for j in range(4):
+        lanes = slice(j * 256, j * 256 + 256)
         scale = inv_tau[:, lanes]
         block = hidden[:, lanes]
         scores = [
@@ -306,18 +347,26 @@
         cross = jnp.zeros((1, 256), jnp.float32)
         for i in range(2):
             e = jnp.exp(scores[i] - top)
-            e_refs[i][:, lanes] = e
+            e_ref[i, :, lanes] = e
             logits = l_refs[i][...]
             total += jnp.sum(e, axis=0, keepdims=True)
             cross += jnp.sum(
                 e * jnp.concatenate([logits, logits], axis=1), axis=0, keepdims=True
             )
-        stat_ref[0:1, lanes] = top + jnp.log(total)
-        stat_ref[1:2, lanes] = cross / total
-        stat_ref[2:3, lanes] = top
+        lse, mean = top + jnp.log(total), cross / total
+        for k in range(2):
+            part, v = slice(k * 128, k * 128 + 128), 2 * j + k
+            top_ref[v : v + 1, :] = top[:, part]
+            stat_ref[0, v : v + 1, :] = lse[:, part]
+            stat_ref[0, 8 + v : 9 + v, :] = mean[:, part]
+    stat_ref[0, 16:24, :] = student[...]
+    rows = stat_ref[0]
+
+    def spread(k, _):
+        stat_ref[k] = rows
         return 0
 
-    lax.fori_loop(0, 4, tile, 0)
+    lax.fori_loop(1, stat_ref.shape[0], spread, 0)
 
 
 def teacher_step(table, weights, hidden, sources, olds=(), last=()):
@@ -326,14 +375,18 @@
     smem = pl.BlockSpec(memory_space=pltpu.SMEM)
     vmem = pl.BlockSpec(memory_space=pltpu.VMEM)
     hbm = pl.BlockSpec(memory_space=pl.ANY)
-    out_shape = [jax.ShapeDtypeStruct((cols, 1024), jnp.float32)] * 2
     if last:
         inv_tau, *logits = last
         body = functools.partial(last_kernel, sources)
-        out_shape = out_shape + [jax.ShapeDtypeStruct((8, 1024), jnp.float32)]
+        out_shape = [
+            jax.ShapeDtypeStruct((2, cols, 1024), jnp.float32),
+            jax.ShapeDtypeStruct((8, 128), jnp.float32),
+            jax.ShapeDtypeStruct((64, 24, 128), jnp.float32),
+        ]
         args = (table, inv_tau, *weights, *hidden, *olds, *logits)
-        in_specs = [smem, vmem] + [hbm] * (2 + len(hidden)) + [vmem] * 4
+        in_specs = [smem, vmem] + [hbm] * (2 + len(hidden)) + [vmem] * 5
     else:
+        out_shape = [jax.ShapeDtypeStruct((cols, 1024), jnp.float32)] * 2
         body = functools.partial(partial_kernel, sources, not olds)
         args = (table, *weights, *hidden, *olds)
         in_specs = [smem] + [hbm] * (2 + len(hidden)) + [vmem] * len(olds)
@@ -348,7 +401,7 @@
             pltpu.VMEM((cols, runs * 256), jnp.bfloat16),
             pltpu.SemaphoreType.DMA((2,)),
         ],
-        compiler_params=pltpu.CompilerParams(vmem_limit_bytes=28 << 20),
+        compiler_params=pltpu.CompilerParams(vmem_limit_bytes=(50 if last else 56) << 20),
         cost_estimate=pl.CostEstimate(
             flops=2 * 2 * cols * runs * 256 * 1024,
             bytes_accessed=2 * runs * 256 * (2 * cols + 1024) + 16 * cols * 1024,
@@ -435,29 +488,23 @@
     base = jnp.stack([(b * 8 + a) * cols, ((b + 1 - 2 * core) * 8 + a) * cols])
     l_own, l_other, s_stats = student_logits(got, got_other, ids_half[None], base, cols)
     logits = (l_own, l_other)
-    e_own, e_other, stats = teacher_step(
-        table, weights, far, ((3, 0), (3, 2)), partial, (inv_tau, l_own, l_other)
-    )
-    packed = jnp.concatenate([stats[:2].reshape(16, half), s_stats])
+    e, local_top, packed = teacher_step(
+        table, weights, far, ((3, 0), (3, 2)), partial, (inv_tau, l_own, l_other, s_stats)
+    )
     groups = [
         sorted(device_index(i // 16, i // 4, i, c) for i in range(64)) for c in range(2)
     ]
-    gathered = lax.all_to_all(
-        jnp.broadcast_to(packed[None], (64, 24, half)),
-        AXES, 0, 0, tiled=True, axis_index_groups=groups,
-    )
-    *errors, loss_half = finish(
-        gathered, (e_own, e_other), logits, stats, mask_half[None], ids_half[None], base
+    gathered = lax.all_to_all(packed, AXES, 0, 0, tiled=True, axis_index_groups=groups)
+    errors, loss_half = finish(
+        gathered, e, logits, local_top, mask_half[None], ids_half[None],
+        jnp.concatenate([base, core[None]]),
     )
     loss_half = loss_half[0]
     loss_all = ordered(core, loss_half, sibling(loss_half), 0)
     token_loss = lax.dynamic_slice_in_dim(loss_all, a * 32, 32)
-    error = ordered(core, errors[0], sibling(errors[1]), 1)
-    error_all = lax.all_to_all(
-        jnp.broadcast_to(error[None], (8, cols, 256)), "variant", 0, 0, tiled=True
-    ).reshape(8 * cols, 256)
-    grad_t = jnp.dot(error_all, student_hidden, preferred_element_type=jnp.float32)
-    return token_loss, grad_t.T
+    pairs = [[v * 16 + 2 * k + c for v in range(8) for c in range(2)] for k in range(8)]
+    errors = lax.all_to_all(errors, AXES, 0, 0, tiled=True, axis_index_groups=pairs)
+    return token_loss, student_gradient(errors, student_hidden).T
 
 
 def solution(mesh):

time: 187 us -> 181 us (0.968); the launches traced: 185 us -> 181 us
  local copies, waits for them, and re-layouts: 17.4 us -> 9.37 us
  Pallas kernels: 38.6 us -> 46.6 us
  matrix products: 2.69 us -> 0 us
    pallas_call x2, Pallas kernels: 20.3 us -> 25.3 us  [teacher_step(): pl.pallas_call(body, out_shape=out_shape, in_specs=in_specs, out_specs=[v...]
    unnamed x34 -> x30, local copies, waits for them, and re-layouts: 8.55 us -> 5.09 us
    pallas_call x1 -> x2, Pallas kernels: 1.16 us -> 4.16 us  [the longest x1 2.34 us: student_gradient(): pl.pallas_call(grad_kernel, out_shape=jax.ShapeDtypeStruct((blocks * cols...]
    dot_general x1 -> x0, matrix products: 2.69 us -> none  [on_device(): jnp.dot(error_all, student_hidden, preferred_element_type=jnp.float32)]
    broadcast_in_dim x2 -> x0, local copies, waits for them, and re-layouts: 2.4 us -> none  [the longest x1 1.44 us: on_device(): jnp.broadcast_to(error[None], (8, cols, 256))]
    reshape x2 -> x0, local copies, waits for them, and re-layouts: 2.2 us -> none  [the longest x1 2.19 us: on_device(): error_all = lax.all_to_all(jnp.broadcast_to(error[None], (8, cols, 256)),...]
  transfers between devices with their start and end apart: 18 -> 17, of which waited for: 10 -> 9; matrix products, arithmetic and copies ran while one was open for 4% -> 5% of each run, Pallas kernels for 16% -> 17%
where the time goes in v5:
time: 181 us
  waiting for transfers between devices  81.4 us (45%)
  Pallas kernels  46.6 us (26%)
  starting transfers between devices  37.9 us (21%)
  local copies, waits for them, and re-layouts  9.37 us (5%)
  other arithmetic  4.22 us (2%)
    all_to_all x1, waiting for transfers between devices, on_device(): lax.all_to_all(errors, AXES, 0, 0, tiled=True, axis_index_groups=pairs)  26.5 us
    pallas_call x2, Pallas kernels, teacher_step(): pl.pallas_call(body, out_shape=out_shape, in_specs=in_specs, out_specs=[v...  25.3 us
    ppermute x1, waiting for transfers between devices, on_device(): after = lax.ppermute(hidden, AXES, minus)  21.5 us
    ppermute x6, waiting for transfers between devices, ring_gather(): lax.ppermute(value, AXES, ring_shift(axes, step))  17.3 us
    all_to_all x1, waiting for transfers between devices, on_device(): lax.all_to_all(packed, AXES, 0, 0, tiled=True, axis_index_groups=groups)  14.5 us
    ppermute x6, starting transfers between devices, ring_gather(): lax.ppermute(value, AXES, ring_shift(axes, step))  11.2 us
    all_to_all x1, starting transfers between devices, on_device(): lax.all_to_all(packed, AXES, 0, 0, tiled=True, axis_index_groups=groups)  10.6 us
    pallas_call x1, Pallas kernels, reorder(): pl.pallas_call(reorder_kernel, grid=(8,), out_shape=jax.ShapeDtypeStruct(...  7.37 us
  transfers between devices with their start and end apart: 17, of which 9 were waited for; matrix products, arithmetic and copies ran while one was open for 5% of the time, Pallas kernels for 17%

profile of v5, /device:TPU:2, one launch (start us, length us, event | category | flops | bytes accessed | tf_op | source)
XLA Modules:
  0.0 180.6 jit_solution(17065390760696342576)
XLA Ops:
  3.0 2.2 %reshape.43 = bf16[8,501,256]{2,1,0:T(8,128)(2,1)S(1)} reshape(bf16[4008,256]{1,0:T(8,128)(2,1)} %bitcast.34) | data formatting | bytes 4104192 | tf_op jit(solution)/shard_map/reshape | solution.py:450
  5.3 4.0 %collective-permute-start.4 = (bf16[64,1024]{1,0:T(8,128)(2,1)S(1)}, bf16[64,1024]{1,0:T(8,128)(2,1)S(1)}, u32[]{:S(2)}, u32[]{:S(2)}) collective-permute-start(bf16[64,1024]{1,0:T(8,128)(2,1)S(1)} %maximum_select_fusion.after.refs_0_), channel_id=1, source_target_pairs={{0,2},{1,33},{64,66},{65,97},{2,0},{3,35},{66,64},{67,99},{4,6},{5... | collective-permute-start | bytes 393224 | tf_op jit(solution)/shard_map/ppermute | solution.py:49
  11.5 1.7 pad_maximum_fusion.refs_4_
  16.8 1.9 %shard_map.105.refs_0_ = bf16[4,64,1024]{2,1,0:T(8,128)(2,1)} custom-call(bf16[64,1024]{1,0:T(8,128)(2,1)} %copy-done.6, bf16[64,1024]{1,0:T(8,128)(2,1)} %copy-done.10, bf16[64,1024]{1,0:T(8,128)(2,1)} %copy-done.9, bf16[64,1024]{1,0:T(8,128)(2,1)} %copy-done.8, bf16[8,640,256]{2,1,0:T(8,128)(2,1)} %pad_maximum_fusion.refs_4_), custom_call_target="tpu_custom_call" | custom-call | bytes 1048576 | tf_op jit(solution)/shard_map/pallas_call | solution.py:66
  18.8 3.2 %collective-permute-start.7 = (bf16[4,64,1024]{2,1,0:T(8,128)(2,1)}, bf16[4,64,1024]{2,1,0:T(8,128)(2,1)S(1)}, u32[]{:S(2)}, u32[]{:S(2)}) collective-permute-start(bf16[4,64,1024]{2,1,0:T(8,128)(2,1)} %shard_map.105.refs_0_), channel_id=1, source_target_pairs={{0,8},{1,9},{64,72},{65,73},{2,10},{3,11},{66,74},{67,75},{4,12},{... | collective-permute-start | bytes 1572872 | tf_op jit(solution)/shard_map/ppermute | solution.py:49
  24.0 4.8 %all-to-all-start = ((bf16[8,640,256]{2,1,0:T(8,128)(2,1)}), bf16[8,640,256]{2,1,0:T(8,128)(2,1)S(1)}, u32[]{:S(2)}, u32[]{:S(2)}) async-start(bf16[8,640,256]{2,1,0:T(8,128)(2,1)} %pad_maximum_fusion.refs_4_), calls=%async_computation | async-start | bytes 5242880 | tf_op jit(solution)/shard_map/all_to_all | solution.py:455
  28.8 6.6 %collective-permute-done.7.refs_3_ = bf16[4,64,1024]{2,1,0:T(8,128)(2,1)S(1)} collective-permute-done((bf16[4,64,1024]{2,1,0:T(8,128)(2,1)}, bf16[4,64,1024]{2,1,0:T(8,128)(2,1)S(1)}, u32[]{:S(2)}, u32[]{:S(2)}) %collective-permute-start.7) | collective-permute-done | bytes 524320 | tf_op jit(solution)/shard_map/ppermute | solution.py:49
  35.4 7.7 %collective-permute-done.6.refs_2_ = bf16[4,64,1024]{2,1,0:T(8,128)(2,1)} collective-permute-done((bf16[4,64,1024]{2,1,0:T(8,128)(2,1)}, bf16[4,64,1024]{2,1,0:T(8,128)(2,1)}, u32[]{:S(2)}, u32[]{:S(2)}) %collective-permute-start.6) | collective-permute-done | bytes 524320 | tf_op jit(solution)/shard_map/ppermute | solution.py:49
  43.1 3.0 %shard_map.106.refs_3_ = bf16[16,64,1024]{2,1,0:T(8,128)(2,1)} custom-call(bf16[4,64,1024]{2,1,0:T(8,128)(2,1)} %shard_map.105.refs_0_, bf16[4,64,1024]{2,1,0:T(8,128)(2,1)} %collective-permute-done.5.refs_1_, bf16[4,64,1024]{2,1,0:T(8,128)(2,1)} %collective-permute-done.6.refs_2_, bf16[4,64,1024]{2,1,0:T(8,128)(2,1)} %copy-done.7), custom_call_target="tpu_custom_call" | custom-call | bytes 4194304 | tf_op jit(solution)/shard_map/pallas_call | solution.py:66
  46.1 1.8 collective-permute-start.9
  48.2 7.4 %shard_map.104.refs_1_.refs_2_ = bf16[501,4096]{1,0:T(8,128)(2,1)} custom-call(bf16[501,4096]{1,0:T(8,128)(2,1)} %bitcast.32, bf16[64,1024]{1,0:T(8,128)(2,1)} %copy-done.6), custom_call_target="tpu_custom_call" | custom-call | bytes 8208384 | tf_op jit(solution)/shard_map/pallas_call | solution.py:114
  55.5 1.7 collective-permute-start.1
  57.9 21.5 %collective-permute-done.9.after.refs_5_ = bf16[16,64,1024]{2,1,0:T(8,128)(2,1)} collective-permute-done((bf16[16,64,1024]{2,1,0:T(8,128)(2,1)}, bf16[16,64,1024]{2,1,0:T(8,128)(2,1)}, u32[]{:S(2)}, u32[]{:S(2)}) %collective-permute-start.9) | collective-permute-done | bytes 2097184 | tf_op jit(solution)/shard_map/ppermute | solution.py:461
  79.4 3.0 %shard_map.107 = (bf16[8,64,1024]{2,1,0:T(8,128)(2,1)}, bf16[8,64,1024]{2,1,0:T(8,128)(2,1)}, bf16[8,640,256]{2,1,0:T(8,128)(2,1)}) custom-call(bf16[16,64,1024]{2,1,0:T(8,128)(2,1)} %collective-permute-done.8.before.refs_4_, bf16[16,64,1024]{2,1,0:T(8,128)(2,1)} %collective-permute-done.9.after.refs_5_, ...), custom_call_target="tpu_custom_call", output_to_operand_aliasing={{2}: (2, {})} | custom-call | bytes 4194304 | tf_op jit(solution)/shard_map/pallas_call | solution.py:87
  86.7 14.7 %shard_map.108 = (f32[501,1024]{1,0:T(8,128)}, f32[501,1024]{1,0:T(8,128)}) custom-call(s32[20]{0:T(128)} %pad_add_fusion.refs_0_, bf16[501,4096]{1,0:T(8,128)(2,1)} %shard_map.104.refs_1_.refs_2_, bf16[501,4096]{1,0:T(8,128)(2,1)} %collective-permute-done.1.refs_2_.refs_3_, bf16[16,64,1024]{2,1,0:T(8,128)(2,1)} %shard_map.106.refs_3_, ...), custom_call_target="tpu_custom_call" | custom-call | flops 6304038912 | bytes 20656128 | tf_op jit(solution)/shard_map/pallas_call | solution.py:393
  101.4 1.9 %shard_map.109 = (f32[501,128]{1,0:T(8,128)S(1)}, f32[501,128]{1,0:T(8,128)S(1)}, f32[8,128]{1,0:T(8,128)S(1)}) custom-call(bf16[8,640,256]{2,1,0:T(8,128)(2,1)S(1)} %copy-done.1, bf16[8,640,256]{2,1,0:T(8,128)(2,1)S(1)} %collective-permute-done.12.other_ref, s32[1,128]{1,0:T(1,128)S(1)} %dynamic-slice_bitcast_fusion.3.ids_ref, s32[2]{0:T(128)S(1)} %pad_add_fusion.1.base_ref), custom_call_target="tpu_custom_call" | custom-call | flops 525336576 | bytes 12582912 | tf_op jit(solution)/shard_map/pallas_call | solution.py:251
  103.4 10.6 %shard_map.110 = (f32[2,501,1024]{2,1,0:T(8,128)}, f32[8,128]{1,0:T(8,128)S(1)}, f32[64,24,128]{2,1,0:T(8,128)}) custom-call(s32[20]{0:T(128)S(1)} %copy-done.5, f32[1,1024]{1,0:T(1,128)S(1)} %bitcast.29, bf16[501,4096]{1,0:T(8,128)(2,1)} %shard_map.104.refs_1_.refs_2_, bf16[501,4096]{1,0:T(8,128)(2,1)} %collective-permute-done.1.refs_2_.refs_3_, ...), custom_call_target="tpu_custom_call" | custom-call | flops 2101346304 | bytes 12357632 | tf_op jit(solution)/shard_map/pallas_call | solution.py:393
  114.1 10.6 %all-to-all-start.1 = ((f32[64,24,128]{2,1,0:T(8,128)}), f32[64,24,128]{2,1,0:T(8,128)S(1)}, u32[]{:S(2)}, u32[]{:S(2)}) async-start(f32[64,24,128]{2,1,0:T(8,128)} %get-tuple-element.23), calls=%async_computation.1 | async-start | bytes 1572864 | tf_op jit(solution)/shard_map/all_to_all | solution.py:497
  124.9 14.5 %all-to-all-done.1.g_ref = f32[64,24,128]{2,1,0:T(8,128)S(1)} async-done(((f32[64,24,128]{2,1,0:T(8,128)}), f32[64,24,128]{2,1,0:T(8,128)S(1)}, u32[]{:S(2)}, u32[]{:S(2)}) %all-to-all-start.1) | async-done | bytes 786464 | tf_op jit(solution)/shard_map/all_to_all | solution.py:497
  139.4 2.2 %copy-done.2 = f32[2,501,1024]{2,1,0:T(8,128)S(1)} copy-done((f32[2,501,1024]{2,1,0:T(8,128)S(1)}, f32[2,501,1024]{2,1,0:T(8,128)}, u32[]{:S(2)}) %copy-start.2) | copy-done | bytes 4104216
  141.6 1.8 %shard_map.111 = (bf16[16,501,128]{2,1,0:T(8,128)(2,1)S(1)}, f32[1,128]{1,0:T(1,128)S(1)}) custom-call(f32[64,24,128]{2,1,0:T(8,128)S(1)} %all-to-all-done.1.g_ref, f32[2,501,1024]{2,1,0:T(8,128)S(1)} %copy-done.2, f32[501,128]{1,0:T(8,128)S(1)} %get-tuple-element.20.refs_8_.l_own, f32[501,128]{1,0:T(8,128)S(1)} %get-tuple-element.21.refs_9_.l_other, ...), custom_call_target="tpu_custom_call" | custom-call | flops 2565120 | bytes 6156288 | tf_op jit(solution)/shard_map/pallas_call | solution.py:168
  144.7 5.2 %all-to-all-start.2 = ((bf16[16,501,128]{2,1,0:T(8,128)(2,1)}), bf16[16,501,128]{2,1,0:T(8,128)(2,1)S(1)}, u32[]{:S(2)}, u32[]{:S(2)}) async-start(bf16[16,501,128]{2,1,0:T(8,128)(2,1)} %copy-done.3), calls=%async_computation.2 | async-start | bytes 4128768 | tf_op jit(solution)/shard_map/all_to_all | solution.py:506
  151.6 26.5 %all-to-all-done.2.err_ref = bf16[16,501,128]{2,1,0:T(8,128)(2,1)S(1)} async-done(((bf16[16,501,128]{2,1,0:T(8,128)(2,1)}), bf16[16,501,128]{2,1,0:T(8,128)(2,1)S(1)}, u32[]{:S(2)}, u32[]{:S(2)}) %all-to-all-start.2) | async-done | bytes 2052128 | tf_op jit(solution)/shard_map/all_to_all | solution.py:506
  178.1 2.3 %shard_map.112 = f32[4008,256]{1,0:T(8,128)} custom-call(bf16[16,501,128]{2,1,0:T(8,128)(2,1)S(1)} %all-to-all-done.2.err_ref, bf16[256,256]{1,0:T(8,128)(2,1)S(1)} %copy-done.4), custom_call_target="tpu_custom_call" | custom-call | flops 525336576 | bytes 7340032 | tf_op jit(solution)/shard_map/pallas_call | solution.py:204
  (82 shorter events, 19.0 us)
Async XLA Ops:
  1.6 3.7 %collective-permute-start = (bf16[32,1024]{1,0:T(8,128)(2,1)S(1)}, bf16[32,1024]{1,0:T(8,128)(2,1)S(1)}, u32[]{:S(2)}, u32[]{:S(2)}) collective-permute-start(bf16[32,1024]{1,0:T(8,128)(2,1)S(1)} %bitcast.36), channel_id=1, source_target_pairs={{0,1},{1,0},{64,65},{65,64},{2,3},{3,2},{66,67},{67,66},{4,5},{5,4... | collective-permute-start | bytes 196616 | tf_op jit(solution)/shard_map/ppermute | solution.py:44
  5.3 7.8 %copy-start.6 = (bf16[64,1024]{1,0:T(8,128)(2,1)}, bf16[64,1024]{1,0:T(8,128)(2,1)S(1)}, u32[]{:S(2)}) copy-start(bf16[64,1024]{1,0:T(8,128)(2,1)S(1)} %maximum_select_fusion.after.refs_0_) | copy-start | bytes 393220
  5.3 7.8 %collective-permute-start.4 = (bf16[64,1024]{1,0:T(8,128)(2,1)S(1)}, bf16[64,1024]{1,0:T(8,128)(2,1)S(1)}, u32[]{:S(2)}, u32[]{:S(2)}) collective-permute-start(bf16[64,1024]{1,0:T(8,128)(2,1)S(1)} %maximum_select_fusion.after.refs_0_), channel_id=1, source_target_pairs={{0,2},{1,33},{64,66},{65,97},{2,0},{3,35},{66,64},{67,99},{4,6},{5... | collective-permute-start | bytes 393224 | tf_op jit(solution)/shard_map/ppermute | solution.py:49
  9.3 5.4 %collective-permute-start.3 = (bf16[64,1024]{1,0:T(8,128)(2,1)S(1)}, bf16[64,1024]{1,0:T(8,128)(2,1)S(1)}, u32[]{:S(2)}, u32[]{:S(2)}) collective-permute-start(bf16[64,1024]{1,0:T(8,128)(2,1)S(1)} %maximum_select_fusion.after.refs_0_), channel_id=1, source_target_pairs={{0,66},{1,49},{64,0},{65,113},{2,64},{3,51},{66,2},{67,115},{4,70}... | collective-permute-start | bytes 393224 | tf_op jit(solution)/shard_map/ppermute | solution.py:49
  10.0 6.2 %collective-permute-start.2 = (bf16[64,1024]{1,0:T(8,128)(2,1)S(1)}, bf16[64,1024]{1,0:T(8,128)(2,1)S(1)}, u32[]{:S(2)}, u32[]{:S(2)}) collective-permute-start(bf16[64,1024]{1,0:T(8,128)(2,1)S(1)} %maximum_select_fusion.after.refs_0_), channel_id=1, source_target_pairs={{0,64},{1,17},{64,2},{65,81},{2,66},{3,19},{66,0},{67,83},{4,68},{... | collective-permute-start | bytes 393224 | tf_op jit(solution)/shard_map/ppermute | solution.py:49
  18.8 16.6 %collective-permute-start.7 = (bf16[4,64,1024]{2,1,0:T(8,128)(2,1)}, bf16[4,64,1024]{2,1,0:T(8,128)(2,1)S(1)}, u32[]{:S(2)}, u32[]{:S(2)}) collective-permute-start(bf16[4,64,1024]{2,1,0:T(8,128)(2,1)} %shard_map.105.refs_0_), channel_id=1, source_target_pairs={{0,8},{1,9},{64,72},{65,73},{2,10},{3,11},{66,74},{67,75},{4,12},{... | collective-permute-start | bytes 1572872 | tf_op jit(solution)/shard_map/ppermute | solution.py:49
  22.0 21.2 %collective-permute-start.6 = (bf16[4,64,1024]{2,1,0:T(8,128)(2,1)}, bf16[4,64,1024]{2,1,0:T(8,128)(2,1)}, u32[]{:S(2)}, u32[]{:S(2)}) collective-permute-start(bf16[4,64,1024]{2,1,0:T(8,128)(2,1)} %shard_map.105.refs_0_), channel_id=1, source_target_pairs={{0,12},{1,13},{64,76},{65,77},{2,14},{3,15},{66,78},{67,79},{4,0},... | collective-permute-start | bytes 1572872 | tf_op jit(solution)/shard_map/ppermute | solution.py:49
  23.0 20.1 %collective-permute-start.5 = (bf16[4,64,1024]{2,1,0:T(8,128)(2,1)}, bf16[4,64,1024]{2,1,0:T(8,128)(2,1)}, u32[]{:S(2)}, u32[]{:S(2)}) collective-permute-start(bf16[4,64,1024]{2,1,0:T(8,128)(2,1)} %shard_map.105.refs_0_), channel_id=1, source_target_pairs={{0,4},{1,5},{64,68},{65,69},{2,6},{3,7},{66,70},{67,71},{4,8},{5,9... | collective-permute-start | bytes 1572872 | tf_op jit(solution)/shard_map/ppermute | solution.py:49
  24.0 33.9 %all-to-all-start = ((bf16[8,640,256]{2,1,0:T(8,128)(2,1)}), bf16[8,640,256]{2,1,0:T(8,128)(2,1)S(1)}, u32[]{:S(2)}, u32[]{:S(2)}) async-start(bf16[8,640,256]{2,1,0:T(8,128)(2,1)} %pad_maximum_fusion.refs_4_), calls=%async_computation | async-start | bytes 5242880 | tf_op jit(solution)/shard_map/all_to_all | solution.py:455
  35.4 7.7 %copy-start.7 = (bf16[4,64,1024]{2,1,0:T(8,128)(2,1)}, bf16[4,64,1024]{2,1,0:T(8,128)(2,1)S(1)}, u32[]{:S(2)}) copy-start(bf16[4,64,1024]{2,1,0:T(8,128)(2,1)S(1)} %collective-permute-done.7.refs_3_) | copy-start | bytes 1572868
  46.1 33.2 %collective-permute-start.9 = (bf16[16,64,1024]{2,1,0:T(8,128)(2,1)}, bf16[16,64,1024]{2,1,0:T(8,128)(2,1)}, u32[]{:S(2)}, u32[]{:S(2)}) collective-permute-start(bf16[16,64,1024]{2,1,0:T(8,128)(2,1)} %shard_map.106.refs_3_), channel_id=1, source_target_pairs={{0,48},{1,67},{64,112},{65,1},{2,50},{3,65},{66,114},{67,3},{4,52}... | collective-permute-start | bytes 6291464 | tf_op jit(solution)/shard_map/ppermute | solution.py:461
  47.9 31.4 %collective-permute-start.8 = (bf16[16,64,1024]{2,1,0:T(8,128)(2,1)}, bf16[16,64,1024]{2,1,0:T(8,128)(2,1)}, u32[]{:S(2)}, u32[]{:S(2)}) collective-permute-start(bf16[16,64,1024]{2,1,0:T(8,128)(2,1)} %shard_map.106.refs_3_), channel_id=1, source_target_pairs={{0,16},{1,65},{64,80},{65,3},{2,18},{3,67},{66,82},{67,1},{4,20},{... | collective-permute-start | bytes 6291464 | tf_op jit(solution)/shard_map/ppermute | solution.py:460
  55.5 26.9 %copy-start.11 = (s32[4]{0:T(128)S(1)}, s32[4]{0:T(128)}, u32[]{:S(2)}) copy-start(s32[4]{0:T(128)} %constant.143.clone) | copy-start | bytes 52
  55.5 27.2 %copy-start.12 = (f32[14]{0:T(128)S(1)}, f32[14]{0:T(128)}, u32[]{:S(2)}) copy-start(f32[14]{0:T(128)} %param.12) | copy-start | bytes 172
  55.5 27.2 %copy-start.13 = (s32[8]{0:T(128)S(1)}, s32[8]{0:T(128)}, u32[]{:S(2)}) copy-start(s32[8]{0:T(128)} %param.11) | copy-start | bytes 100
  55.5 31.2 %collective-permute-start.1 = (bf16[501,4096]{1,0:T(8,128)(2,1)}, bf16[501,4096]{1,0:T(8,128)(2,1)}, u32[]{:S(2)}, u32[]{:S(2)}) collective-permute-start(bf16[501,4096]{1,0:T(8,128)(2,1)} %shard_map.104.refs_1_.refs_2_), channel_id=1, source_target_pairs={{0,1},{1,0},{64,65},{65,64},{2,3},{3,2},{66,67},{67,66},{4,5},{5,4... | collective-permute-start | bytes 12312584 | tf_op jit(solution)/shard_map/ppermute | solution.py:44
  57.9 21.5 %copy-start = (bf16[8,640,256]{2,1,0:T(8,128)(2,1)}, bf16[8,640,256]{2,1,0:T(8,128)(2,1)S(1)}, u32[]{:S(2)}) copy-start(bf16[8,640,256]{2,1,0:T(8,128)(2,1)S(1)} %all-to-all-done.through_in) | copy-start | bytes 7864324
  82.3 19.1 %collective-permute-start.12 = (bf16[8,640,256]{2,1,0:T(8,128)(2,1)}, bf16[8,640,256]{2,1,0:T(8,128)(2,1)S(1)}, u32[]{:S(2)}, u32[]{:S(2)}) collective-permute-start(bf16[8,640,256]{2,1,0:T(8,128)(2,1)} %get-tuple-element.19.own_ref), channel_id=1, source_target_pairs={{0,1},{1,0},{64,65},{65,64},{2,3},{3,2},{66,67},{67,66},{4,5},{5,4... | collective-permute-start | bytes 7864328 | tf_op jit(solution)/shard_map/ppermute | solution.py:44
  83.0 20.3 %collective-permute-start.10 = (bf16[8,64,1024]{2,1,0:T(8,128)(2,1)}, bf16[8,64,1024]{2,1,0:T(8,128)(2,1)}, u32[]{:S(2)}, u32[]{:S(2)}) collective-permute-start(bf16[8,64,1024]{2,1,0:T(8,128)(2,1)} %get-tuple-element.15), channel_id=1, source_target_pairs={{0,16},{1,65},{64,80},{65,3},{2,18},{3,67},{66,82},{67,1},{4,20},{... | collective-permute-start | bytes 3145736 | tf_op jit(solution)/shard_map/ppermute | solution.py:473
  83.7 19.6 %collective-permute-start.11 = (bf16[8,64,1024]{2,1,0:T(8,128)(2,1)}, bf16[8,64,1024]{2,1,0:T(8,128)(2,1)}, u32[]{:S(2)}, u32[]{:S(2)}) collective-permute-start(bf16[8,64,1024]{2,1,0:T(8,128)(2,1)} %get-tuple-element.16), channel_id=1, source_target_pairs={{0,48},{1,67},{64,112},{65,1},{2,50},{3,65},{66,114},{67,3},{4,52}... | collective-permute-start | bytes 3145736 | tf_op jit(solution)/shard_map/ppermute | solution.py:473
  86.7 14.7 %copy-start.1 = (bf16[8,640,256]{2,1,0:T(8,128)(2,1)S(1)}, bf16[8,640,256]{2,1,0:T(8,128)(2,1)}, u32[]{:S(2)}) copy-start(bf16[8,640,256]{2,1,0:T(8,128)(2,1)} %get-tuple-element.19.own_ref) | copy-start | bytes 7864324
  114.1 25.4 %all-to-all-start.1 = ((f32[64,24,128]{2,1,0:T(8,128)}), f32[64,24,128]{2,1,0:T(8,128)S(1)}, u32[]{:S(2)}, u32[]{:S(2)}) async-start(f32[64,24,128]{2,1,0:T(8,128)} %get-tuple-element.23), calls=%async_computation.1 | async-start | bytes 1572864 | tf_op jit(solution)/shard_map/all_to_all | solution.py:497
  144.7 33.4 %all-to-all-start.2 = ((bf16[16,501,128]{2,1,0:T(8,128)(2,1)}), bf16[16,501,128]{2,1,0:T(8,128)(2,1)S(1)}, u32[]{:S(2)}, u32[]{:S(2)}) async-start(bf16[16,501,128]{2,1,0:T(8,128)(2,1)} %copy-done.3), calls=%async_computation.2 | async-start | bytes 4128768 | tf_op jit(solution)/shard_map/all_to_all | solution.py:506
  149.9 1.1 collective-permute-start.13
  (7 other events, 15.3 us)

commit v6 on v5

--- a/solution.py
+++ b/solution.py
@@ -74,12 +74,12 @@
     )(*blocks, *after)
 
 
-def halves_kernel(before, after, through_in, before_half, after_half, through_out):
+def halves_kernel(before, after, through_in, other, before_half, after_half, through_out):
     before_half[...] = before[...]
     after_half[...] = after[...]
 
 
-def forward_halves(before, after, through):
+def forward_halves(before, after, through, other):
     n, rows, lanes = before.shape
     block = (n // 2, rows, lanes)
     hbm = pl.BlockSpec(memory_space=pl.ANY)
@@ -89,24 +89,28 @@
         grid=(1,),
         out_shape=[jax.ShapeDtypeStruct(block, before.dtype)] * 2
         + [jax.ShapeDtypeStruct(through.shape, through.dtype)],
-        in_specs=[lower, pl.BlockSpec(block, lambda i: (1, 0, 0)), hbm],
+        in_specs=[lower, pl.BlockSpec(block, lambda i: (1, 0, 0)), hbm, hbm],
         out_specs=[lower, lower, hbm],
         input_output_aliases={2: 2},
         cost_estimate=pl.CostEstimate(
             flops=0, bytes_accessed=4 * n * rows * lanes, transcendentals=0
         ),
-    )(before, after, through)
-
-
-def reorder_kernel(w_ref, after, out_ref):
+    )(before, after, through, other)
+
+
+def reorder_kernel(w_ref, after, *out_refs):
     step = pl.program_id(0)
+    cols = w_ref.shape[0]
     pairs = [w_ref[:, y * 128 : (y + 1) * 128] for y in range(SIDE)]
     for zh in range(2):
         for i in range(2):
             lane = pl.multiple_of(zh * 2048 + step * 256 + i * 128, 128)
-            out_ref[:, pl.ds(lane, 128)] = jnp.concatenate(
+            piece = jnp.concatenate(
                 [pair[:, zh * 64 : (zh + 1) * 64] for pair in pairs[2 * i : 2 * i + 2]], axis=1
             )
+            for k, out_ref in enumerate(out_refs):
+                here = piece[128 * k : min(128 * (k + 1), cols)]
+                out_ref[: here.shape[0], pl.ds(lane, 128)] = here
 
 
 def reorder(weight, after):
@@ -114,12 +118,12 @@
     return pl.pallas_call(
         reorder_kernel,
         grid=(8,),
-        out_shape=jax.ShapeDtypeStruct((cols, width), weight.dtype),
+        out_shape=[jax.ShapeDtypeStruct((128, width), weight.dtype)] * 4,
         in_specs=[
             pl.BlockSpec((cols, 512), lambda i: (0, i)),
             pl.BlockSpec(memory_space=pl.ANY),
         ],
-        out_specs=pl.BlockSpec((cols, width), lambda i: (0, 0)),
+        out_specs=[pl.BlockSpec((128, width), lambda i: (0, 0))] * 4,
         cost_estimate=pl.CostEstimate(
             flops=0, bytes_accessed=4 * cols * width, transcendentals=0
         ),
@@ -286,10 +290,12 @@
                     )
                 )
             lane = pl.multiple_of(table[slot * 4 + s1] * 256, 256)
-            for w, buf in zip(w_refs, weights):
+            for k, w in enumerate(w_refs):
                 copies.append(
                     pltpu.make_async_copy(
-                        w.at[:, pl.ds(lane, 256)], buf.at[:, pl.ds(at, 256)], sems.at[1]
+                        w.at[:, pl.ds(lane, 256)],
+                        weights.at[pl.ds(128 * k, 128), pl.ds(at, 256)],
+                        sems.at[1],
                     )
                 )
             run += 1
@@ -301,21 +307,19 @@
 
 def partial_kernel(sources, first, *refs):
     n = len(sources)
-    table, w_refs = refs[0], refs[1 : 3]
-    hidden_refs, refs = refs[3 : 3 + n], refs[3 + n :]
-    olds = refs[:0] if first else refs[:2]
-    outs = refs[len(olds) : len(olds) + 2]
-    hidden, *weights, sems = refs[len(olds) + 2 :]
+    table, w_refs, hidden_refs, refs = refs[0], refs[1:9], refs[9 : 9 + n], refs[9 + n :]
+    old = None if first else refs[0]
+    hidden, weights, sems = refs[-3:]
+    out, done = refs[0 if first else 1], refs[1 if first else 2]
     gather_blocks(
         table, [(r,) + s for r, s in zip(hidden_refs, sources)], w_refs, hidden, weights, sems
     )
+    done[...] = jnp.zeros_like(done)
 
     def tile(j, _):
         lanes = pl.ds(pl.multiple_of(j * 256, 256), 256)
-        block = hidden[:, lanes]
-        for i in range(2):
-            part = jnp.dot(weights[i][...], block, preferred_element_type=jnp.float32)
-            outs[i][:, lanes] = part if first else olds[i][:, lanes] + part
+        part = jnp.dot(weights[...], hidden[:, lanes], preferred_element_type=jnp.float32)
+        out[:, lanes] = part if first else old[:, lanes] + part
         return 0
 
     lax.fori_loop(0, 4, tile, 0)
@@ -323,21 +327,21 @@
 
 def last_kernel(sources, *refs):
     n = len(sources)
-    table, inv_tau, w_refs = refs[0], refs[1], refs[2:4]
-    hidden_refs, refs = refs[4 : 4 + n], refs[4 + n :]
-    olds, l_refs, student = refs[0:2], refs[2:4], refs[4]
-    e_ref, top_ref, stat_ref = refs[5:8]
-    hidden, *weights, sems = refs[8:]
+    table, inv_tau, w_refs = refs[0], refs[1], refs[2:10]
+    hidden_refs, refs = refs[10 : 10 + n], refs[10 + n :]
+    old, l_refs, student = refs[0], refs[1:3], refs[3]
+    e_ref, top_ref, stat_ref = refs[4:7]
+    hidden, weights, sems = refs[7:]
+    cols = e_ref.shape[1]
     gather_blocks(
         table, [(r,) + s for r, s in zip(hidden_refs, sources)], w_refs, hidden, weights, sems
     )
     for j in range(4):
         lanes = slice(j * 256, j * 256 + 256)
         scale = inv_tau[:, lanes]
-        block = hidden[:, lanes]
+        part = jnp.dot(weights[...], hidden[:, lanes], preferred_element_type=jnp.float32)
         scores = [
-            (olds[i][:, lanes] + jnp.dot(weights[i][...], block, preferred_element_type=jnp.float32))
-            * scale
+            (old[i * 512 : i * 512 + cols, lanes] + part[i * 512 : i * 512 + cols]) * scale
             for i in range(2)
         ]
         top = jnp.maximum(
@@ -369,42 +373,46 @@
     lax.fori_loop(1, stat_ref.shape[0], spread, 0)
 
 
-def teacher_step(table, weights, hidden, sources, olds=(), last=()):
-    cols = weights[0].shape[0]
+def teacher_step(table, weights, hidden, sources, cols, old=(), last=()):
+    width = weights[0].shape[1]
     runs = sum(h.shape[0] for h in hidden) // 4
     smem = pl.BlockSpec(memory_space=pltpu.SMEM)
     vmem = pl.BlockSpec(memory_space=pltpu.VMEM)
-    hbm = pl.BlockSpec(memory_space=pl.ANY)
+    hbm = pl.BlockSpec(memory_space=pltpu.HBM)
     if last:
-        inv_tau, *logits = last
+        inv_tau, *student = last
         body = functools.partial(last_kernel, sources)
         out_shape = [
             jax.ShapeDtypeStruct((2, cols, 1024), jnp.float32),
             jax.ShapeDtypeStruct((8, 128), jnp.float32),
             jax.ShapeDtypeStruct((64, 24, 128), jnp.float32),
         ]
-        args = (table, inv_tau, *weights, *hidden, *olds, *logits)
-        in_specs = [smem, vmem] + [hbm] * (2 + len(hidden)) + [vmem] * 5
+        args = (table, inv_tau, *weights, *hidden, *old, *student)
+        in_specs = [smem, vmem] + [hbm] * (8 + len(hidden)) + [vmem] * 4
+        out_specs = [vmem] * 3
     else:
-        out_shape = [jax.ShapeDtypeStruct((cols, 1024), jnp.float32)] * 2
-        body = functools.partial(partial_kernel, sources, not olds)
-        args = (table, *weights, *hidden, *olds)
-        in_specs = [smem] + [hbm] * (2 + len(hidden)) + [vmem] * len(olds)
+        body = functools.partial(partial_kernel, sources, not old)
+        out_shape = [
+            jax.ShapeDtypeStruct((1024, 1024), jnp.float32),
+            jax.ShapeDtypeStruct((8, 128), jnp.float32),
+        ]
+        args = (table, *weights, *hidden, *old)
+        in_specs = [smem] + [hbm] * (8 + len(hidden)) + [vmem] * len(old)
+        out_specs = [vmem] * 2
     return pl.pallas_call(
         body,
         out_shape=out_shape,
         in_specs=in_specs,
-        out_specs=[vmem] * len(out_shape),
+        out_specs=out_specs,
         scratch_shapes=[
             pltpu.VMEM((runs * 256, 1024), jnp.bfloat16),
-            pltpu.VMEM((cols, runs * 256), jnp.bfloat16),
-            pltpu.VMEM((cols, runs * 256), jnp.bfloat16),
+            pltpu.VMEM((1024, runs * 256), jnp.bfloat16),
             pltpu.SemaphoreType.DMA((2,)),
         ],
-        compiler_params=pltpu.CompilerParams(vmem_limit_bytes=(50 if last else 56) << 20),
-        cost_estimate=pl.CostEstimate(
-            flops=2 * 2 * cols * runs * 256 * 1024,
-            bytes_accessed=2 * runs * 256 * (2 * cols + 1024) + 16 * cols * 1024,
+        compiler_params=pltpu.CompilerParams(vmem_limit_bytes=(52 if last else 56) << 20),
+        cost_estimate=pl.CostEstimate(
+            flops=2 * 1024 * runs * 256 * 1024 if last else 100 << 20,
+            bytes_accessed=8 << 20 if last else 100 << 10,
             transcendentals=2 * cols * 1024 if last else 0,
         ),
     )(*args)
@@ -435,9 +443,6 @@
     ]
     unit = ordered(core, halves[0], sibling(halves[1]), 0)
     blocks = ring_gather(unit, "zx")
-    w_own = reorder(teacher_weight.T, unit)
-    w_other = sibling(w_own)
-    weights = (w_own, w_other)
 
     meta = jnp.concatenate(
         [token_ids // 256, token_ids % 256, loss_mask, jnp.zeros((32,), jnp.int32)]
@@ -456,6 +461,8 @@
 
     hidden = stack(blocks, (send,))
     hidden = stack(ring_gather(hidden, "yy"))
+    w_own = reorder(teacher_weight.T, unit)
+    weights = (*w_own, *(sibling(w) for w in w_own))
     plus, minus = ring_shift("xz", 1), ring_shift("xz", -1)
     before = lax.ppermute(hidden, AXES, plus)
     after = lax.ppermute(hidden, AXES, minus)
@@ -466,9 +473,10 @@
     table = jnp.concatenate(
         [((pz // 2 * 2 + pz % 2) * 4 + px).reshape(16), (y + offsets) % 4]
     )
-    lower, upper, got = forward_halves(before, after, got)
-    partial = teacher_step(
-        table, weights, (hidden, before, after), ((0, 0), (1, 0), (2, 0))
+    partial, done = teacher_step(table, weights, (hidden,), ((0, 0),), cols)
+    lower, upper, got = forward_halves(before, after, got, done)
+    partial, done = teacher_step(
+        table, weights, (before, after), ((1, 0), (2, 0)), cols, (partial,)
     )
     far = (lax.ppermute(lower, AXES, plus), lax.ppermute(upper, AXES, minus))
 
@@ -489,7 +497,7 @@
     l_own, l_other, s_stats = student_logits(got, got_other, ids_half[None], base, cols)
     logits = (l_own, l_other)
     e, local_top, packed = teacher_step(
-        table, weights, far, ((3, 0), (3, 2)), partial, (inv_tau, l_own, l_other, s_stats)
+        table, weights, far, ((3, 0), (3, 2)), cols, (partial,), (inv_tau, l_own, l_other, s_stats)
     )
     groups = [
         sorted(device_index(i // 16, i // 4, i, c) for i in range(64)) for c in range(2)

time: 181 us -> 177 us (0.978)
  waiting for transfers between devices: 81.4 us -> 71.7 us
  Pallas kernels: 46.6 us -> 52.7 us
    ppermute x1, waiting for transfers between devices: 21.5 us -> 1.65 us  [on_device(): after = lax.ppermute(hidden, AXES, minus)]
    ppermute x1, waiting for transfers between devices: 0.01 us -> 15.7 us  [on_device(): before = lax.ppermute(hidden, AXES, plus)]
    ppermute x6, waiting for transfers between devices: 17.3 us -> 8.3 us  [ring_gather(): lax.ppermute(value, AXES, ring_shift(axes, step))]
    pallas_call x3 -> x4, Pallas kernels: 32.7 us -> 38.6 us  [the longest x3 31.3 us: teacher_step(): pl.pallas_call(body, out_shape=out_shape, in_specs=in_specs, out_specs=ou...]
    ppermute x4 -> x7, waiting for transfers between devices: 0.98 us -> 5.2 us  [sibling(): lax.ppermute(value, AXES, permutation(lambda x, y, z, c: (x, y, z, 1 - c)))]
    all_to_all x1, starting transfers between devices: 10.6 us -> 8.43 us  [on_device(): lax.all_to_all(packed, AXES, 0, 0, tiled=True, axis_index_groups=groups)]
  transfers between devices with their start and end apart: 17 -> 20, of which waited for: 9 -> 11; matrix products, arithmetic and copies ran while one was open for 5% -> 5% of each run, Pallas kernels for 17% -> 19%
where the time goes in v6:
time: 177 us
  waiting for transfers between devices  71.7 us (41%)
  Pallas kernels  52.7 us (30%)
  starting transfers between devices  37.5 us (21%)
  local copies, waits for them, and re-layouts  9.37 us (5%)
  other arithmetic  4.25 us (2%)
    pallas_call x3, Pallas kernels, teacher_step(): pl.pallas_call(body, out_shape=out_shape, in_specs=in_specs, out_specs=ou...  31.3 us
    all_to_all x1, waiting for transfers between devices, on_device(): lax.all_to_all(errors, AXES, 0, 0, tiled=True, axis_index_groups=pairs)  26.5 us
    ppermute x1, waiting for transfers between devices, on_device(): before = lax.ppermute(hidden, AXES, plus)  15.7 us
    all_to_all x1, waiting for transfers between devices, on_device(): lax.all_to_all(packed, AXES, 0, 0, tiled=True, axis_index_groups=groups)  14.4 us
    ppermute x6, starting transfers between devices, ring_gather(): lax.ppermute(value, AXES, ring_shift(axes, step))  12.4 us
    all_to_all x1, starting transfers between devices, on_device(): lax.all_to_all(packed, AXES, 0, 0, tiled=True, axis_index_groups=groups)  8.43 us
    ppermute x6, waiting for transfers between devices, ring_gather(): lax.ppermute(value, AXES, ring_shift(axes, step))  8.3 us
    pallas_call x1, Pallas kernels, reorder(): pl.pallas_call(reorder_kernel, grid=(8,), out_shape=[jax.ShapeDtypeStruct...  7.37 us
  transfers between devices with their start and end apart: 20, of which 11 were waited for; matrix products, arithmetic and copies ran while one was open for 5% of the time, Pallas kernels for 19%

profile of v6, /device:TPU:2, one launch (start us, length us, event | category | flops | bytes accessed | tf_op | source)
XLA Modules:
  0.0 176.6 jit_solution(4965805042201139759)
XLA Ops:
  3.1 2.2 %reshape.43 = bf16[8,501,256]{2,1,0:T(8,128)(2,1)S(1)} reshape(bf16[4008,256]{1,0:T(8,128)(2,1)} %bitcast.34) | data formatting | bytes 4104192 | tf_op jit(solution)/shard_map/reshape | solution.py:455
  5.3 2.0 %collective-permute-start.5 = (bf16[64,1024]{1,0:T(8,128)(2,1)S(1)}, bf16[64,1024]{1,0:T(8,128)(2,1)S(1)}, u32[]{:S(2)}, u32[]{:S(2)}) collective-permute-start(bf16[64,1024]{1,0:T(8,128)(2,1)S(1)} %maximum_select_fusion.after.refs_0_), channel_id=1, source_target_pairs={{0,64},{1,17},{64,2},{65,81},{2,66},{3,19},{66,0},{67,83},{4,68},{... | collective-permute-start | bytes 393224 | tf_op jit(solution)/shard_map/ppermute | solution.py:49
  7.3 2.2 %collective-permute-start.6 = (bf16[64,1024]{1,0:T(8,128)(2,1)S(1)}, bf16[64,1024]{1,0:T(8,128)(2,1)S(1)}, u32[]{:S(2)}, u32[]{:S(2)}) collective-permute-start(bf16[64,1024]{1,0:T(8,128)(2,1)S(1)} %maximum_select_fusion.after.refs_0_), channel_id=1, source_target_pairs={{0,66},{1,49},{64,0},{65,113},{2,64},{3,51},{66,2},{67,115},{4,70}... | collective-permute-start | bytes 393224 | tf_op jit(solution)/shard_map/ppermute | solution.py:49
  13.2 2.8 %collective-permute-done.7.refs_3_ = bf16[64,1024]{1,0:T(8,128)(2,1)S(1)} collective-permute-done((bf16[64,1024]{1,0:T(8,128)(2,1)S(1)}, bf16[64,1024]{1,0:T(8,128)(2,1)S(1)}, u32[]{:S(2)}, u32[]{:S(2)}) %collective-permute-start.7) | collective-permute-done | bytes 131104 | tf_op jit(solution)/shard_map/ppermute | solution.py:49
  16.7 1.9 %shard_map.105.refs_0_ = bf16[4,64,1024]{2,1,0:T(8,128)(2,1)} custom-call(bf16[64,1024]{1,0:T(8,128)(2,1)} %copy-done.6, bf16[64,1024]{1,0:T(8,128)(2,1)} %copy-done.8, bf16[64,1024]{1,0:T(8,128)(2,1)} %copy-done.9, bf16[64,1024]{1,0:T(8,128)(2,1)} %copy-done.10, bf16[8,640,256]{2,1,0:T(8,128)(2,1)} %pad_maximum_fusion.refs_4_), custom_call_target="tpu_custom_call" | custom-call | bytes 1048576 | tf_op jit(solution)/shard_map/pallas_call | solution.py:66
  18.6 3.2 %collective-permute-start.10 = (bf16[4,64,1024]{2,1,0:T(8,128)(2,1)}, bf16[4,64,1024]{2,1,0:T(8,128)(2,1)S(1)}, u32[]{:S(2)}, u32[]{:S(2)}) collective-permute-start(bf16[4,64,1024]{2,1,0:T(8,128)(2,1)} %shard_map.105.refs_0_), channel_id=1, source_target_pairs={{0,8},{1,9},{64,72},{65,73},{2,10},{3,11},{66,74},{67,75},{4,12},{... | collective-permute-start | bytes 1572872 | tf_op jit(solution)/shard_map/ppermute | solution.py:49
  22.5 2.6 %collective-permute-start.9 = (bf16[4,64,1024]{2,1,0:T(8,128)(2,1)}, bf16[4,64,1024]{2,1,0:T(8,128)(2,1)}, u32[]{:S(2)}, u32[]{:S(2)}) collective-permute-start(bf16[4,64,1024]{2,1,0:T(8,128)(2,1)} %shard_map.105.refs_0_), channel_id=1, source_target_pairs={{0,12},{1,13},{64,76},{65,77},{2,14},{3,15},{66,78},{67,79},{4,0},... | collective-permute-start | bytes 1572872 | tf_op jit(solution)/shard_map/ppermute | solution.py:49
  25.0 4.9 %all-to-all-start = ((bf16[8,640,256]{2,1,0:T(8,128)(2,1)}), bf16[8,640,256]{2,1,0:T(8,128)(2,1)S(1)}, u32[]{:S(2)}, u32[]{:S(2)}) async-start(bf16[8,640,256]{2,1,0:T(8,128)(2,1)} %pad_maximum_fusion.refs_4_), calls=%async_computation | async-start | bytes 5242880 | tf_op jit(solution)/shard_map/all_to_all | solution.py:460
  30.0 7.4 %shard_map.104 = (bf16[128,4096]{1,0:T(8,128)(2,1)}, bf16[128,4096]{1,0:T(8,128)(2,1)}, bf16[128,4096]{1,0:T(8,128)(2,1)}, bf16[128,4096]{1,0:T(8,128)(2,1)}) custom-call(bf16[501,4096]{1,0:T(8,128)(2,1)} %bitcast.32, bf16[64,1024]{1,0:T(8,128)(2,1)} %copy-done.6), custom_call_target="tpu_custom_call" | custom-call | bytes 8208384 | tf_op jit(solution)/shard_map/pallas_call | solution.py:118
  37.4 5.1 %collective-permute-done.8.refs_1_ = bf16[4,64,1024]{2,1,0:T(8,128)(2,1)} collective-permute-done((bf16[4,64,1024]{2,1,0:T(8,128)(2,1)}, bf16[4,64,1024]{2,1,0:T(8,128)(2,1)}, u32[]{:S(2)}, u32[]{:S(2)}) %collective-permute-start.8) | collective-permute-done | bytes 524320 | tf_op jit(solution)/shard_map/ppermute | solution.py:49
  42.8 3.0 %shard_map.106.refs_9_ = bf16[16,64,1024]{2,1,0:T(8,128)(2,1)} custom-call(bf16[4,64,1024]{2,1,0:T(8,128)(2,1)} %shard_map.105.refs_0_, bf16[4,64,1024]{2,1,0:T(8,128)(2,1)} %collective-permute-done.8.refs_1_, bf16[4,64,1024]{2,1,0:T(8,128)(2,1)} %collective-permute-done.9.refs_2_, bf16[4,64,1024]{2,1,0:T(8,128)(2,1)} %copy-done.7), custom_call_target="tpu_custom_call" | custom-call | bytes 4194304 | tf_op jit(solution)/shard_map/pallas_call | solution.py:66
  55.2 7.8 %shard_map.107 = (f32[1024,1024]{1,0:T(8,128)}, f32[8,128]{1,0:T(8,128)}) custom-call(s32[20]{0:T(128)} %pad_add_fusion.refs_0_, bf16[128,4096]{1,0:T(8,128)(2,1)} %get-tuple-element.20.refs_1_.refs_2_, bf16[128,4096]{1,0:T(8,128)(2,1)} %get-tuple-element.21.refs_2_.refs_3_, bf16[128,4096]{1,0:T(8,128)(2,1)} %get-tuple-element.22.refs_3_.refs_4_, ...), custom_call_target="tpu_custom_call" | custom-call | flops 104857600 | bytes 102400 | tf_op jit(solution)/shard_map/pallas_call | solution.py:402
  63.0 15.7 %collective-permute-done.11.before.refs_9_ = bf16[16,64,1024]{2,1,0:T(8,128)(2,1)} collective-permute-done((bf16[16,64,1024]{2,1,0:T(8,128)(2,1)}, bf16[16,64,1024]{2,1,0:T(8,128)(2,1)}, u32[]{:S(2)}, u32[]{:S(2)}) %collective-permute-start.11) | collective-permute-done | bytes 2097184 | tf_op jit(solution)/shard_map/ppermute | solution.py:467
  80.3 3.0 %shard_map.108 = (bf16[8,64,1024]{2,1,0:T(8,128)(2,1)}, bf16[8,64,1024]{2,1,0:T(8,128)(2,1)}, bf16[8,640,256]{2,1,0:T(8,128)(2,1)}) custom-call(bf16[16,64,1024]{2,1,0:T(8,128)(2,1)} %collective-permute-done.11.before.refs_9_, bf16[16,64,1024]{2,1,0:T(8,128)(2,1)} %collective-permute-done.12.after.refs_10_, ...), custom_call_target="tpu_custom_call", output_to_operand_aliasing={{2}: (2, {})} | custom-call | bytes 4194304 | tf_op jit(solution)/shard_map/pallas_call | solution.py:87
  86.7 12.9 %shard_map.109 = (f32[1024,1024]{1,0:T(8,128)}, f32[8,128]{1,0:T(8,128)}) custom-call(s32[20]{0:T(128)} %pad_add_fusion.refs_0_, bf16[128,4096]{1,0:T(8,128)(2,1)} %get-tuple-element.20.refs_1_.refs_2_, bf16[128,4096]{1,0:T(8,128)(2,1)} %get-tuple-element.21.refs_2_.refs_3_, bf16[128,4096]{1,0:T(8,128)(2,1)} %get-tuple-element.22.refs_3_.refs_4_, ...), custom_call_target="tpu_custom_call" | custom-call | flops 104857600 | bytes 102400 | tf_op jit(solution)/shard_map/pallas_call | solution.py:402
  99.7 1.9 %shard_map.110 = (f32[501,128]{1,0:T(8,128)S(1)}, f32[501,128]{1,0:T(8,128)S(1)}, f32[8,128]{1,0:T(8,128)S(1)}) custom-call(bf16[8,640,256]{2,1,0:T(8,128)(2,1)S(1)} %copy-done.1, bf16[8,640,256]{2,1,0:T(8,128)(2,1)S(1)} %collective-permute-done.15.other_ref, s32[1,128]{1,0:T(1,128)S(1)} %dynamic-slice_bitcast_fusion.3.ids_ref, s32[2]{0:T(128)S(1)} %pad_add_fusion.1.base_ref), custom_call_target="tpu_custom_call" | custom-call | flops 525336576 | bytes 12582912 | tf_op jit(solution)/shard_map/pallas_call | solution.py:255
  101.7 10.6 %shard_map.111 = (f32[2,501,1024]{2,1,0:T(8,128)}, f32[8,128]{1,0:T(8,128)S(1)}, f32[64,24,128]{2,1,0:T(8,128)}) custom-call(s32[20]{0:T(128)S(1)} %copy-done.5, f32[1,1024]{1,0:T(1,128)S(1)} %bitcast.29, bf16[128,4096]{1,0:T(8,128)(2,1)} %get-tuple-element.20.refs_1_.refs_2_, bf16[128,4096]{1,0:T(8,128)(2,1)} %get-tuple-element.21.refs_2_.refs_3_, ...), custom_call_target="tpu_custom_call" | custom-call | flops 2147483648 | bytes 8388608 | tf_op jit(solution)/shard_map/pallas_call | solution.py:402
  112.3 8.4 %all-to-all-start.1 = ((f32[64,24,128]{2,1,0:T(8,128)}), f32[64,24,128]{2,1,0:T(8,128)S(1)}, u32[]{:S(2)}, u32[]{:S(2)}) async-start(f32[64,24,128]{2,1,0:T(8,128)} %get-tuple-element.33), calls=%async_computation.1 | async-start | bytes 1572864 | tf_op jit(solution)/shard_map/all_to_all | solution.py:505
  121.0 14.4 %all-to-all-done.1.g_ref = f32[64,24,128]{2,1,0:T(8,128)S(1)} async-done(((f32[64,24,128]{2,1,0:T(8,128)}), f32[64,24,128]{2,1,0:T(8,128)S(1)}, u32[]{:S(2)}, u32[]{:S(2)}) %all-to-all-start.1) | async-done | bytes 786464 | tf_op jit(solution)/shard_map/all_to_all | solution.py:505
  135.4 2.2 %copy-done.2 = f32[2,501,1024]{2,1,0:T(8,128)S(1)} copy-done((f32[2,501,1024]{2,1,0:T(8,128)S(1)}, f32[2,501,1024]{2,1,0:T(8,128)}, u32[]{:S(2)}) %copy-start.2) | copy-done | bytes 4104216
  137.6 1.8 %shard_map.112 = (bf16[16,501,128]{2,1,0:T(8,128)(2,1)S(1)}, f32[1,128]{1,0:T(1,128)S(1)}) custom-call(f32[64,24,128]{2,1,0:T(8,128)S(1)} %all-to-all-done.1.g_ref, f32[2,501,1024]{2,1,0:T(8,128)S(1)} %copy-done.2, f32[501,128]{1,0:T(8,128)S(1)} %get-tuple-element.30.refs_13_.l_own, f32[501,128]{1,0:T(8,128)S(1)} %get-tuple-element.31.refs_14_.l_other, ...), custom_call_target="tpu_custom_call" | custom-call | flops 2565120 | bytes 6156288 | tf_op jit(solution)/shard_map/pallas_call | solution.py:172
  140.7 5.2 %all-to-all-start.2 = ((bf16[16,501,128]{2,1,0:T(8,128)(2,1)}), bf16[16,501,128]{2,1,0:T(8,128)(2,1)S(1)}, u32[]{:S(2)}, u32[]{:S(2)}) async-start(bf16[16,501,128]{2,1,0:T(8,128)(2,1)} %copy-done.3), calls=%async_computation.2 | async-start | bytes 4128768 | tf_op jit(solution)/shard_map/all_to_all | solution.py:514
  147.6 26.5 %all-to-all-done.2.err_ref = bf16[16,501,128]{2,1,0:T(8,128)(2,1)S(1)} async-done(((bf16[16,501,128]{2,1,0:T(8,128)(2,1)}), bf16[16,501,128]{2,1,0:T(8,128)(2,1)S(1)}, u32[]{:S(2)}, u32[]{:S(2)}) %all-to-all-start.2) | async-done | bytes 2052128 | tf_op jit(solution)/shard_map/all_to_all | solution.py:514
  174.1 2.3 %shard_map.113 = f32[4008,256]{1,0:T(8,128)} custom-call(bf16[16,501,128]{2,1,0:T(8,128)(2,1)S(1)} %all-to-all-done.2.err_ref, bf16[256,256]{1,0:T(8,128)(2,1)S(1)} %copy-done.4), custom_call_target="tpu_custom_call" | custom-call | flops 525336576 | bytes 7340032 | tf_op jit(solution)/shard_map/pallas_call | solution.py:208
  (89 shorter events, 25.6 us)
Async XLA Ops:
  1.6 3.7 %collective-permute-start = (bf16[32,1024]{1,0:T(8,128)(2,1)S(1)}, bf16[32,1024]{1,0:T(8,128)(2,1)S(1)}, u32[]{:S(2)}, u32[]{:S(2)}) collective-permute-start(bf16[32,1024]{1,0:T(8,128)(2,1)S(1)} %bitcast.36), channel_id=1, source_target_pairs={{0,1},{1,0},{64,65},{65,64},{2,3},{3,2},{66,67},{67,66},{4,5},{5,4... | collective-permute-start | bytes 196616 | tf_op jit(solution)/shard_map/ppermute | solution.py:44
  5.3 7.8 %copy-start.6 = (bf16[64,1024]{1,0:T(8,128)(2,1)}, bf16[64,1024]{1,0:T(8,128)(2,1)S(1)}, u32[]{:S(2)}) copy-start(bf16[64,1024]{1,0:T(8,128)(2,1)S(1)} %maximum_select_fusion.after.refs_0_) | copy-start | bytes 393220
  5.3 7.8 %collective-permute-start.5 = (bf16[64,1024]{1,0:T(8,128)(2,1)S(1)}, bf16[64,1024]{1,0:T(8,128)(2,1)S(1)}, u32[]{:S(2)}, u32[]{:S(2)}) collective-permute-start(bf16[64,1024]{1,0:T(8,128)(2,1)S(1)} %maximum_select_fusion.after.refs_0_), channel_id=1, source_target_pairs={{0,64},{1,17},{64,2},{65,81},{2,66},{3,19},{66,0},{67,83},{4,68},{... | collective-permute-start | bytes 393224 | tf_op jit(solution)/shard_map/ppermute | solution.py:49
  7.3 5.8 %collective-permute-start.6 = (bf16[64,1024]{1,0:T(8,128)(2,1)S(1)}, bf16[64,1024]{1,0:T(8,128)(2,1)S(1)}, u32[]{:S(2)}, u32[]{:S(2)}) collective-permute-start(bf16[64,1024]{1,0:T(8,128)(2,1)S(1)} %maximum_select_fusion.after.refs_0_), channel_id=1, source_target_pairs={{0,66},{1,49},{64,0},{65,113},{2,64},{3,51},{66,2},{67,115},{4,70}... | collective-permute-start | bytes 393224 | tf_op jit(solution)/shard_map/ppermute | solution.py:49
  9.5 6.5 %collective-permute-start.7 = (bf16[64,1024]{1,0:T(8,128)(2,1)S(1)}, bf16[64,1024]{1,0:T(8,128)(2,1)S(1)}, u32[]{:S(2)}, u32[]{:S(2)}) collective-permute-start(bf16[64,1024]{1,0:T(8,128)(2,1)S(1)} %maximum_select_fusion.after.refs_0_), channel_id=1, source_target_pairs={{0,2},{1,33},{64,66},{65,97},{2,0},{3,35},{66,64},{67,99},{4,6},{5... | collective-permute-start | bytes 393224 | tf_op jit(solution)/shard_map/ppermute | solution.py:49
  18.6 18.8 %collective-permute-start.10 = (bf16[4,64,1024]{2,1,0:T(8,128)(2,1)}, bf16[4,64,1024]{2,1,0:T(8,128)(2,1)S(1)}, u32[]{:S(2)}, u32[]{:S(2)}) collective-permute-start(bf16[4,64,1024]{2,1,0:T(8,128)(2,1)} %shard_map.105.refs_0_), channel_id=1, source_target_pairs={{0,8},{1,9},{64,72},{65,73},{2,10},{3,11},{66,74},{67,75},{4,12},{... | collective-permute-start | bytes 1572872 | tf_op jit(solution)/shard_map/ppermute | solution.py:49
  21.8 20.7 %collective-permute-start.8 = (bf16[4,64,1024]{2,1,0:T(8,128)(2,1)}, bf16[4,64,1024]{2,1,0:T(8,128)(2,1)}, u32[]{:S(2)}, u32[]{:S(2)}) collective-permute-start(bf16[4,64,1024]{2,1,0:T(8,128)(2,1)} %shard_map.105.refs_0_), channel_id=1, source_target_pairs={{0,4},{1,5},{64,68},{65,69},{2,6},{3,7},{66,70},{67,71},{4,8},{5,9... | collective-permute-start | bytes 1572872 | tf_op jit(solution)/shard_map/ppermute | solution.py:49
  22.5 20.4 %collective-permute-start.9 = (bf16[4,64,1024]{2,1,0:T(8,128)(2,1)}, bf16[4,64,1024]{2,1,0:T(8,128)(2,1)}, u32[]{:S(2)}, u32[]{:S(2)}) collective-permute-start(bf16[4,64,1024]{2,1,0:T(8,128)(2,1)} %shard_map.105.refs_0_), channel_id=1, source_target_pairs={{0,12},{1,13},{64,76},{65,77},{2,14},{3,15},{66,78},{67,79},{4,0},... | collective-permute-start | bytes 1572872 | tf_op jit(solution)/shard_map/ppermute | solution.py:49
  25.0 37.9 %all-to-all-start = ((bf16[8,640,256]{2,1,0:T(8,128)(2,1)}), bf16[8,640,256]{2,1,0:T(8,128)(2,1)S(1)}, u32[]{:S(2)}, u32[]{:S(2)}) async-start(bf16[8,640,256]{2,1,0:T(8,128)(2,1)} %pad_maximum_fusion.refs_4_), calls=%async_computation | async-start | bytes 5242880 | tf_op jit(solution)/shard_map/all_to_all | solution.py:460
  37.3 12.7 %copy-start.11 = (s32[4]{0:T(128)S(1)}, s32[4]{0:T(128)}, u32[]{:S(2)}) copy-start(s32[4]{0:T(128)} %constant.143.clone) | copy-start | bytes 52
  37.3 12.2 %collective-permute-start.1 = (bf16[128,4096]{1,0:T(8,128)(2,1)}, bf16[128,4096]{1,0:T(8,128)(2,1)}, u32[]{:S(2)}, u32[]{:S(2)}) collective-permute-start(bf16[128,4096]{1,0:T(8,128)(2,1)} %get-tuple-element.20.refs_1_.refs_2_), channel_id=1, source_target_pairs={{0,1},{1,0},{64,65},{65,64},{2,3},{3,2},{66,67},{67,66},{4,5},{5,4... | collective-permute-start | bytes 3145736 | tf_op jit(solution)/shard_map/ppermute | solution.py:44
  45.8 32.8 %collective-permute-start.11 = (bf16[16,64,1024]{2,1,0:T(8,128)(2,1)}, bf16[16,64,1024]{2,1,0:T(8,128)(2,1)}, u32[]{:S(2)}, u32[]{:S(2)}) collective-permute-start(bf16[16,64,1024]{2,1,0:T(8,128)(2,1)} %shard_map.106.refs_9_), channel_id=1, source_target_pairs={{0,16},{1,65},{64,80},{65,3},{2,18},{3,67},{66,82},{67,1},{4,20},{... | collective-permute-start | bytes 6291464 | tf_op jit(solution)/shard_map/ppermute | solution.py:467
  47.0 33.2 %collective-permute-start.12 = (bf16[16,64,1024]{2,1,0:T(8,128)(2,1)}, bf16[16,64,1024]{2,1,0:T(8,128)(2,1)}, u32[]{:S(2)}, u32[]{:S(2)}) collective-permute-start(bf16[16,64,1024]{2,1,0:T(8,128)(2,1)} %shard_map.106.refs_9_), channel_id=1, source_target_pairs={{0,48},{1,67},{64,112},{65,1},{2,50},{3,65},{66,114},{67,3},{4,52}... | collective-permute-start | bytes 6291464 | tf_op jit(solution)/shard_map/ppermute | solution.py:468
  47.9 4.3 %collective-permute-start.2 = (bf16[128,4096]{1,0:T(8,128)(2,1)}, bf16[128,4096]{1,0:T(8,128)(2,1)}, u32[]{:S(2)}, u32[]{:S(2)}) collective-permute-start(bf16[128,4096]{1,0:T(8,128)(2,1)} %get-tuple-element.21.refs_2_.refs_3_), channel_id=1, source_target_pairs={{0,1},{1,0},{64,65},{65,64},{2,3},{3,2},{66,67},{67,66},{4,5},{5,4... | collective-permute-start | bytes 3145736 | tf_op jit(solution)/shard_map/ppermute | solution.py:44
  49.5 4.1 %collective-permute-start.3 = (bf16[128,4096]{1,0:T(8,128)(2,1)}, bf16[128,4096]{1,0:T(8,128)(2,1)}, u32[]{:S(2)}, u32[]{:S(2)}) collective-permute-start(bf16[128,4096]{1,0:T(8,128)(2,1)} %get-tuple-element.22.refs_3_.refs_4_), channel_id=1, source_target_pairs={{0,1},{1,0},{64,65},{65,64},{2,3},{3,2},{66,67},{67,66},{4,5},{5,4... | collective-permute-start | bytes 3145736 | tf_op jit(solution)/shard_map/ppermute | solution.py:44
  49.5 5.6 %collective-permute-start.4 = (bf16[128,4096]{1,0:T(8,128)(2,1)}, bf16[128,4096]{1,0:T(8,128)(2,1)}, u32[]{:S(2)}, u32[]{:S(2)}) collective-permute-start(bf16[128,4096]{1,0:T(8,128)(2,1)} %get-tuple-element.23.refs_4_.refs_5_), channel_id=1, source_target_pairs={{0,1},{1,0},{64,65},{65,64},{2,3},{3,2},{66,67},{67,66},{4,5},{5,4... | collective-permute-start | bytes 3145736 | tf_op jit(solution)/shard_map/ppermute | solution.py:44
  63.0 17.3 %copy-start = (bf16[8,640,256]{2,1,0:T(8,128)(2,1)}, bf16[8,640,256]{2,1,0:T(8,128)(2,1)S(1)}, u32[]{:S(2)}) copy-start(bf16[8,640,256]{2,1,0:T(8,128)(2,1)S(1)} %all-to-all-done.through_in) | copy-start | bytes 7864324
  83.3 16.4 %collective-permute-start.15 = (bf16[8,640,256]{2,1,0:T(8,128)(2,1)}, bf16[8,640,256]{2,1,0:T(8,128)(2,1)S(1)}, u32[]{:S(2)}, u32[]{:S(2)}) collective-permute-start(bf16[8,640,256]{2,1,0:T(8,128)(2,1)} %get-tuple-element.29.own_ref), channel_id=1, source_target_pairs={{0,1},{1,0},{64,65},{65,64},{2,3},{3,2},{66,67},{67,66},{4,5},{5,4... | collective-permute-start | bytes 7864328 | tf_op jit(solution)/shard_map/ppermute | solution.py:44
  83.4 18.2 %collective-permute-start.13 = (bf16[8,64,1024]{2,1,0:T(8,128)(2,1)}, bf16[8,64,1024]{2,1,0:T(8,128)(2,1)}, u32[]{:S(2)}, u32[]{:S(2)}) collective-permute-start(bf16[8,64,1024]{2,1,0:T(8,128)(2,1)} %get-tuple-element.25), channel_id=1, source_target_pairs={{0,16},{1,65},{64,80},{65,3},{2,18},{3,67},{66,82},{67,1},{4,20},{... | collective-permute-start | bytes 3145736 | tf_op jit(solution)/shard_map/ppermute | solution.py:481
  84.1 17.5 %collective-permute-start.14 = (bf16[8,64,1024]{2,1,0:T(8,128)(2,1)}, bf16[8,64,1024]{2,1,0:T(8,128)(2,1)}, u32[]{:S(2)}, u32[]{:S(2)}) collective-permute-start(bf16[8,64,1024]{2,1,0:T(8,128)(2,1)} %get-tuple-element.26), channel_id=1, source_target_pairs={{0,48},{1,67},{64,112},{65,1},{2,50},{3,65},{66,114},{67,3},{4,52}... | collective-permute-start | bytes 3145736 | tf_op jit(solution)/shard_map/ppermute | solution.py:481
  86.7 13.0 %copy-start.1 = (bf16[8,640,256]{2,1,0:T(8,128)(2,1)S(1)}, bf16[8,640,256]{2,1,0:T(8,128)(2,1)}, u32[]{:S(2)}) copy-start(bf16[8,640,256]{2,1,0:T(8,128)(2,1)} %get-tuple-element.29.own_ref) | copy-start | bytes 7864324
  112.3 23.2 %all-to-all-start.1 = ((f32[64,24,128]{2,1,0:T(8,128)}), f32[64,24,128]{2,1,0:T(8,128)S(1)}, u32[]{:S(2)}, u32[]{:S(2)}) async-start(f32[64,24,128]{2,1,0:T(8,128)} %get-tuple-element.33), calls=%async_computation.1 | async-start | bytes 1572864 | tf_op jit(solution)/shard_map/all_to_all | solution.py:505
  140.7 33.4 %all-to-all-start.2 = ((bf16[16,501,128]{2,1,0:T(8,128)(2,1)}), bf16[16,501,128]{2,1,0:T(8,128)(2,1)S(1)}, u32[]{:S(2)}, u32[]{:S(2)}) async-start(bf16[16,501,128]{2,1,0:T(8,128)(2,1)} %copy-done.3), calls=%async_computation.2 | async-start | bytes 4128768 | tf_op jit(solution)/shard_map/all_to_all | solution.py:514
  145.9 1.1 collective-permute-start.16
  (10 other events, 32.4 us)

commit v7 on v6

--- a/solution.py
+++ b/solution.py
@@ -219,6 +219,29 @@
             flops=2 * blocks * cols * 256 * width, bytes_accessed=7 << 20, transcendentals=0
         ),
     )(errors, hidden)
+
+
+def send_kernel(mine_ref, weight_ref, meta_ref, out_ref):
+    blocks, half = out_ref.shape[0], mine_ref.shape[0]
+    cols = weight_ref.shape[0] // blocks
+    for k in range(blocks):
+        out_ref[k, :half, :] = mine_ref[...]
+        out_ref[k, half : half + cols, :] = weight_ref[k * cols : (k + 1) * cols, :]
+        out_ref[k, half + cols :, :] = jnp.broadcast_to(
+            meta_ref[...], (ROWS - half - cols, meta_ref.shape[1])
+        )
+
+
+def send_blocks(mine, weight, meta):
+    vmem = pl.BlockSpec(memory_space=pltpu.VMEM)
+    return pl.pallas_call(
+        send_kernel,
+        out_shape=jax.ShapeDtypeStruct((8, ROWS, mine.shape[1]), mine.dtype),
+        in_specs=[vmem] * 3,
+        out_specs=vmem,
+        compiler_params=pltpu.CompilerParams(vmem_limit_bytes=16 << 20),
+        cost_estimate=pl.CostEstimate(flops=0, bytes_accessed=9 << 20, transcendentals=0),
+    )(mine, weight, meta)
 
 
 def student_kernel(own_ref, other_ref, ids_ref, base_ref, l_own, l_other, stat_ref):
@@ -447,16 +470,9 @@
     meta = jnp.concatenate(
         [token_ids // 256, token_ids % 256, loss_mask, jnp.zeros((32,), jnp.int32)]
     ).astype(jnp.bfloat16)
-    meta = jnp.concatenate([meta, unit[0, :128]])[None, None]
+    meta = jnp.concatenate([meta, unit[0, :128]])[None]
     mine = lax.dynamic_slice_in_dim(student_hidden, core * half, half, axis=0)
-    send = jnp.concatenate(
-        [
-            jnp.broadcast_to(mine[None], (8, half, 256)),
-            student_weight.T.reshape(8, cols, 256),
-            jnp.broadcast_to(meta, (8, ROWS - half - cols, 256)),
-        ],
-        axis=1,
-    )
+    send = send_blocks(mine, student_weight.T, meta)
     got = lax.all_to_all(send, "variant", 0, 0, tiled=True)
 
     hidden = stack(blocks, (send,))

time: 177 us -> 177 us (level)
    unnamed x30 -> x34, local copies, waits for them, and re-layouts: 5.08 us -> 8.11 us
    reshape x1 -> x0, local copies, waits for them, and re-layouts: 2.18 us -> none  [on_device(): student_weight.T.reshape(8, cols, 256)]
  transfers between devices with their start and end apart: 20 -> 20, of which waited for: 11 -> 11; matrix products, arithmetic and copies ran while one was open for 5% -> 3% of each run, Pallas kernels for 19% -> 19%
where the time goes in v7:
time: 177 us; the launch traced here: 176 us
  waiting for transfers between devices  70.7 us (40%)
  Pallas kernels  53 us (30%)
  starting transfers between devices  37.3 us (21%)
  local copies, waits for them, and re-layouts  11 us (6%)
  other arithmetic  2.54 us (1%)
    pallas_call x3, Pallas kernels, teacher_step(): pl.pallas_call(body, out_shape=out_shape, in_specs=in_specs, out_specs=ou...  31.3 us
    all_to_all x1, waiting for transfers between devices, on_device(): lax.all_to_all(errors, AXES, 0, 0, tiled=True, axis_index_groups=pairs)  26.5 us
    ppermute x1, waiting for transfers between devices, on_device(): before = lax.ppermute(hidden, AXES, plus)  15.8 us
    all_to_all x1, waiting for transfers between devices, on_device(): lax.all_to_all(packed, AXES, 0, 0, tiled=True, axis_index_groups=groups)  14.5 us
    ppermute x6, starting transfers between devices, ring_gather(): lax.ppermute(value, AXES, ring_shift(axes, step))  12.4 us
    all_to_all x1, starting transfers between devices, on_device(): lax.all_to_all(packed, AXES, 0, 0, tiled=True, axis_index_groups=groups)  8.39 us
    unnamed x34, local copies, waits for them, and re-layouts  8.11 us
    pallas_call x1, Pallas kernels, reorder(): pl.pallas_call(reorder_kernel, grid=(8,), out_shape=[jax.ShapeDtypeStruct...  7.34 us
  transfers between devices with their start and end apart: 20, of which 11 were waited for; matrix products, arithmetic and copies ran while one was open for 3% of the time, Pallas kernels for 19%

profile of v7, /device:TPU:2, one launch (start us, length us, event | category | flops | bytes accessed | tf_op | source)
XLA Modules:
  0.0 175.7 jit_solution(12256235757210266042)
XLA Ops:
  3.9 2.0 %collective-permute-start.5 = (bf16[64,1024]{1,0:T(8,128)(2,1)S(1)}, bf16[64,1024]{1,0:T(8,128)(2,1)S(1)}, u32[]{:S(2)}, u32[]{:S(2)}) collective-permute-start(bf16[64,1024]{1,0:T(8,128)(2,1)S(1)} %maximum_select_fusion.after.refs_0_), channel_id=1, source_target_pairs={{0,64},{1,17},{64,2},{65,81},{2,66},{3,19},{66,0},{67,83},{4,68},{... | collective-permute-start | bytes 393224 | tf_op jit(solution)/shard_map/ppermute | solution.py:49
  5.9 2.2 %collective-permute-start.6 = (bf16[64,1024]{1,0:T(8,128)(2,1)S(1)}, bf16[64,1024]{1,0:T(8,128)(2,1)S(1)}, u32[]{:S(2)}, u32[]{:S(2)}) collective-permute-start(bf16[64,1024]{1,0:T(8,128)(2,1)S(1)} %maximum_select_fusion.after.refs_0_), channel_id=1, source_target_pairs={{0,66},{1,49},{64,0},{65,113},{2,64},{3,51},{66,2},{67,115},{4,70}... | collective-permute-start | bytes 393224 | tf_op jit(solution)/shard_map/ppermute | solution.py:49
  8.1 1.8 %collective-permute-start.7 = (bf16[64,1024]{1,0:T(8,128)(2,1)S(1)}, bf16[64,1024]{1,0:T(8,128)(2,1)S(1)}, u32[]{:S(2)}, u32[]{:S(2)}) collective-permute-start(bf16[64,1024]{1,0:T(8,128)(2,1)S(1)} %maximum_select_fusion.after.refs_0_), channel_id=1, source_target_pairs={{0,2},{1,33},{64,66},{65,97},{2,0},{3,35},{66,64},{67,99},{4,6},{5... | collective-permute-start | bytes 393224 | tf_op jit(solution)/shard_map/ppermute | solution.py:49
  15.2 1.9 %shard_map.106.refs_0_ = bf16[4,64,1024]{2,1,0:T(8,128)(2,1)} custom-call(bf16[64,1024]{1,0:T(8,128)(2,1)} %copy-done.8, bf16[64,1024]{1,0:T(8,128)(2,1)} %copy-done.10, bf16[64,1024]{1,0:T(8,128)(2,1)} %copy-done.11, bf16[64,1024]{1,0:T(8,128)(2,1)} %copy-done.12, bf16[8,640,256]{2,1,0:T(8,128)(2,1)} %copy-done.2), custom_call_target="tpu_custom_call" | custom-call | bytes 1048576 | tf_op jit(solution)/shard_map/pallas_call | solution.py:66
  17.2 3.2 %collective-permute-start.10 = (bf16[4,64,1024]{2,1,0:T(8,128)(2,1)}, bf16[4,64,1024]{2,1,0:T(8,128)(2,1)S(1)}, u32[]{:S(2)}, u32[]{:S(2)}) collective-permute-start(bf16[4,64,1024]{2,1,0:T(8,128)(2,1)} %shard_map.106.refs_0_), channel_id=1, source_target_pairs={{0,8},{1,9},{64,72},{65,73},{2,10},{3,11},{66,74},{67,75},{4,12},{... | collective-permute-start | bytes 1572872 | tf_op jit(solution)/shard_map/ppermute | solution.py:49
  21.0 2.6 %collective-permute-start.9 = (bf16[4,64,1024]{2,1,0:T(8,128)(2,1)}, bf16[4,64,1024]{2,1,0:T(8,128)(2,1)}, u32[]{:S(2)}, u32[]{:S(2)}) collective-permute-start(bf16[4,64,1024]{2,1,0:T(8,128)(2,1)} %shard_map.106.refs_0_), channel_id=1, source_target_pairs={{0,12},{1,13},{64,76},{65,77},{2,14},{3,15},{66,78},{67,79},{4,0},... | collective-permute-start | bytes 1572872 | tf_op jit(solution)/shard_map/ppermute | solution.py:49
  23.6 4.9 %all-to-all-start = ((bf16[8,640,256]{2,1,0:T(8,128)(2,1)}), bf16[8,640,256]{2,1,0:T(8,128)(2,1)S(1)}, u32[]{:S(2)}, u32[]{:S(2)}) async-start(bf16[8,640,256]{2,1,0:T(8,128)(2,1)} %copy-done.2), calls=%async_computation | async-start | bytes 5242880 | tf_op jit(solution)/shard_map/all_to_all | solution.py:476
  28.5 7.3 %shard_map.104 = (bf16[128,4096]{1,0:T(8,128)(2,1)}, bf16[128,4096]{1,0:T(8,128)(2,1)}, bf16[128,4096]{1,0:T(8,128)(2,1)}, bf16[128,4096]{1,0:T(8,128)(2,1)}) custom-call(bf16[501,4096]{1,0:T(8,128)(2,1)} %bitcast.33, bf16[64,1024]{1,0:T(8,128)(2,1)} %copy-done.8), custom_call_target="tpu_custom_call" | custom-call | bytes 8208384 | tf_op jit(solution)/shard_map/pallas_call | solution.py:118
  35.9 5.6 %collective-permute-done.8.refs_1_ = bf16[4,64,1024]{2,1,0:T(8,128)(2,1)} collective-permute-done((bf16[4,64,1024]{2,1,0:T(8,128)(2,1)}, bf16[4,64,1024]{2,1,0:T(8,128)(2,1)}, u32[]{:S(2)}, u32[]{:S(2)}) %collective-permute-start.8) | collective-permute-done | bytes 524320 | tf_op jit(solution)/shard_map/ppermute | solution.py:49
  41.9 3.0 %shard_map.107.refs_9_ = bf16[16,64,1024]{2,1,0:T(8,128)(2,1)} custom-call(bf16[4,64,1024]{2,1,0:T(8,128)(2,1)} %shard_map.106.refs_0_, bf16[4,64,1024]{2,1,0:T(8,128)(2,1)} %collective-permute-done.8.refs_1_, bf16[4,64,1024]{2,1,0:T(8,128)(2,1)} %collective-permute-done.9.refs_2_, bf16[4,64,1024]{2,1,0:T(8,128)(2,1)} %copy-done.9), custom_call_target="tpu_custom_call" | custom-call | bytes 4194304 | tf_op jit(solution)/shard_map/pallas_call | solution.py:66
  53.9 7.8 %shard_map.108 = (f32[1024,1024]{1,0:T(8,128)}, f32[8,128]{1,0:T(8,128)}) custom-call(s32[20]{0:T(128)} %pad_add_fusion.refs_0_, bf16[128,4096]{1,0:T(8,128)(2,1)} %get-tuple-element.20.refs_1_.refs_2_, bf16[128,4096]{1,0:T(8,128)(2,1)} %get-tuple-element.21.refs_2_.refs_3_, bf16[128,4096]{1,0:T(8,128)(2,1)} %get-tuple-element.22.refs_3_.refs_4_, ...), custom_call_target="tpu_custom_call" | custom-call | flops 104857600 | bytes 102400 | tf_op jit(solution)/shard_map/pallas_call | solution.py:425
  61.8 15.8 %collective-permute-done.11.before.refs_9_ = bf16[16,64,1024]{2,1,0:T(8,128)(2,1)} collective-permute-done((bf16[16,64,1024]{2,1,0:T(8,128)(2,1)}, bf16[16,64,1024]{2,1,0:T(8,128)(2,1)}, u32[]{:S(2)}, u32[]{:S(2)}) %collective-permute-start.11) | collective-permute-done | bytes 2097184 | tf_op jit(solution)/shard_map/ppermute | solution.py:483
  77.6 1.7 collective-permute-done.12.after.refs_10_
  79.2 3.0 %shard_map.109 = (bf16[8,64,1024]{2,1,0:T(8,128)(2,1)}, bf16[8,64,1024]{2,1,0:T(8,128)(2,1)}, bf16[8,640,256]{2,1,0:T(8,128)(2,1)}) custom-call(bf16[16,64,1024]{2,1,0:T(8,128)(2,1)} %collective-permute-done.11.before.refs_9_, bf16[16,64,1024]{2,1,0:T(8,128)(2,1)} %collective-permute-done.12.after.refs_10_, ...), custom_call_target="tpu_custom_call", output_to_operand_aliasing={{2}: (2, {})} | custom-call | bytes 4194304 | tf_op jit(solution)/shard_map/pallas_call | solution.py:87
  85.6 12.9 %shard_map.110 = (f32[1024,1024]{1,0:T(8,128)}, f32[8,128]{1,0:T(8,128)}) custom-call(s32[20]{0:T(128)} %pad_add_fusion.refs_0_, bf16[128,4096]{1,0:T(8,128)(2,1)} %get-tuple-element.20.refs_1_.refs_2_, bf16[128,4096]{1,0:T(8,128)(2,1)} %get-tuple-element.21.refs_2_.refs_3_, bf16[128,4096]{1,0:T(8,128)(2,1)} %get-tuple-element.22.refs_3_.refs_4_, ...), custom_call_target="tpu_custom_call" | custom-call | flops 104857600 | bytes 102400 | tf_op jit(solution)/shard_map/pallas_call | solution.py:425
  98.6 1.9 %shard_map.111 = (f32[501,128]{1,0:T(8,128)S(1)}, f32[501,128]{1,0:T(8,128)S(1)}, f32[8,128]{1,0:T(8,128)S(1)}) custom-call(bf16[8,640,256]{2,1,0:T(8,128)(2,1)S(1)} %copy-done.1, bf16[8,640,256]{2,1,0:T(8,128)(2,1)S(1)} %collective-permute-done.15.other_ref, s32[1,128]{1,0:T(1,128)S(1)} %dynamic-slice_bitcast_fusion.3.ids_ref, s32[2]{0:T(128)S(1)} %pad_add_fusion.1.base_ref), custom_call_target="tpu_custom_call" | custom-call | flops 525336576 | bytes 12582912 | tf_op jit(solution)/shard_map/pallas_call | solution.py:278
  100.6 10.6 %shard_map.112 = (f32[2,501,1024]{2,1,0:T(8,128)}, f32[8,128]{1,0:T(8,128)S(1)}, f32[64,24,128]{2,1,0:T(8,128)}) custom-call(s32[20]{0:T(128)S(1)} %copy-done.7, f32[1,1024]{1,0:T(1,128)S(1)} %bitcast.30, bf16[128,4096]{1,0:T(8,128)(2,1)} %get-tuple-element.20.refs_1_.refs_2_, bf16[128,4096]{1,0:T(8,128)(2,1)} %get-tuple-element.21.refs_2_.refs_3_, ...), custom_call_target="tpu_custom_call" | custom-call | flops 2147483648 | bytes 8388608 | tf_op jit(solution)/shard_map/pallas_call | solution.py:425
  111.2 8.4 %all-to-all-start.1 = ((f32[64,24,128]{2,1,0:T(8,128)}), f32[64,24,128]{2,1,0:T(8,128)S(1)}, u32[]{:S(2)}, u32[]{:S(2)}) async-start(f32[64,24,128]{2,1,0:T(8,128)} %get-tuple-element.33), calls=%async_computation.1 | async-start | bytes 1572864 | tf_op jit(solution)/shard_map/all_to_all | solution.py:521
  119.9 14.5 %all-to-all-done.1.g_ref = f32[64,24,128]{2,1,0:T(8,128)S(1)} async-done(((f32[64,24,128]{2,1,0:T(8,128)}), f32[64,24,128]{2,1,0:T(8,128)S(1)}, u32[]{:S(2)}, u32[]{:S(2)}) %all-to-all-start.1) | async-done | bytes 786464 | tf_op jit(solution)/shard_map/all_to_all | solution.py:521
  134.4 2.2 %copy-done.3 = f32[2,501,1024]{2,1,0:T(8,128)S(1)} copy-done((f32[2,501,1024]{2,1,0:T(8,128)S(1)}, f32[2,501,1024]{2,1,0:T(8,128)}, u32[]{:S(2)}) %copy-start.3) | copy-done | bytes 4104216
  136.6 1.8 %shard_map.113 = (bf16[16,501,128]{2,1,0:T(8,128)(2,1)S(1)}, f32[1,128]{1,0:T(1,128)S(1)}) custom-call(f32[64,24,128]{2,1,0:T(8,128)S(1)} %all-to-all-done.1.g_ref, f32[2,501,1024]{2,1,0:T(8,128)S(1)} %copy-done.3, f32[501,128]{1,0:T(8,128)S(1)} %get-tuple-element.30.refs_13_.l_own, f32[501,128]{1,0:T(8,128)S(1)} %get-tuple-element.31.refs_14_.l_other, ...), custom_call_target="tpu_custom_call" | custom-call | flops 2565120 | bytes 6156288 | tf_op jit(solution)/shard_map/pallas_call | solution.py:172
  139.7 5.3 %all-to-all-start.2 = ((bf16[16,501,128]{2,1,0:T(8,128)(2,1)}), bf16[16,501,128]{2,1,0:T(8,128)(2,1)S(1)}, u32[]{:S(2)}, u32[]{:S(2)}) async-start(bf16[16,501,128]{2,1,0:T(8,128)(2,1)} %copy-done.4), calls=%async_computation.2 | async-start | bytes 4128768 | tf_op jit(solution)/shard_map/all_to_all | solution.py:530
  146.7 26.5 %all-to-all-done.2.err_ref = bf16[16,501,128]{2,1,0:T(8,128)(2,1)S(1)} async-done(((bf16[16,501,128]{2,1,0:T(8,128)(2,1)}), bf16[16,501,128]{2,1,0:T(8,128)(2,1)S(1)}, u32[]{:S(2)}, u32[]{:S(2)}) %all-to-all-start.2) | async-done | bytes 2052128 | tf_op jit(solution)/shard_map/all_to_all | solution.py:530
  173.2 2.3 %shard_map.114 = f32[4008,256]{1,0:T(8,128)} custom-call(bf16[16,501,128]{2,1,0:T(8,128)(2,1)S(1)} %all-to-all-done.2.err_ref, bf16[256,256]{1,0:T(8,128)(2,1)S(1)} %copy-done.6), custom_call_target="tpu_custom_call" | custom-call | flops 525336576 | bytes 7340032 | tf_op jit(solution)/shard_map/pallas_call | solution.py:208
  (91 shorter events, 25.4 us)
Async XLA Ops:
  1.6 2.3 %collective-permute-start = (bf16[32,1024]{1,0:T(8,128)(2,1)S(1)}, bf16[32,1024]{1,0:T(8,128)(2,1)S(1)}, u32[]{:S(2)}, u32[]{:S(2)}) collective-permute-start(bf16[32,1024]{1,0:T(8,128)(2,1)S(1)} %bitcast.36), channel_id=1, source_target_pairs={{0,1},{1,0},{64,65},{65,64},{2,3},{3,2},{66,67},{67,66},{4,5},{5,4... | collective-permute-start | bytes 196616 | tf_op jit(solution)/shard_map/ppermute | solution.py:44
  3.9 9.6 %collective-permute-start.5 = (bf16[64,1024]{1,0:T(8,128)(2,1)S(1)}, bf16[64,1024]{1,0:T(8,128)(2,1)S(1)}, u32[]{:S(2)}, u32[]{:S(2)}) collective-permute-start(bf16[64,1024]{1,0:T(8,128)(2,1)S(1)} %maximum_select_fusion.after.refs_0_), channel_id=1, source_target_pairs={{0,64},{1,17},{64,2},{65,81},{2,66},{3,19},{66,0},{67,83},{4,68},{... | collective-permute-start | bytes 393224 | tf_op jit(solution)/shard_map/ppermute | solution.py:49
  5.9 7.6 %collective-permute-start.6 = (bf16[64,1024]{1,0:T(8,128)(2,1)S(1)}, bf16[64,1024]{1,0:T(8,128)(2,1)S(1)}, u32[]{:S(2)}, u32[]{:S(2)}) collective-permute-start(bf16[64,1024]{1,0:T(8,128)(2,1)S(1)} %maximum_select_fusion.after.refs_0_), channel_id=1, source_target_pairs={{0,66},{1,49},{64,0},{65,113},{2,64},{3,51},{66,2},{67,115},{4,70}... | collective-permute-start | bytes 393224 | tf_op jit(solution)/shard_map/ppermute | solution.py:49
  8.1 6.5 %collective-permute-start.7 = (bf16[64,1024]{1,0:T(8,128)(2,1)S(1)}, bf16[64,1024]{1,0:T(8,128)(2,1)S(1)}, u32[]{:S(2)}, u32[]{:S(2)}) collective-permute-start(bf16[64,1024]{1,0:T(8,128)(2,1)S(1)} %maximum_select_fusion.after.refs_0_), channel_id=1, source_target_pairs={{0,2},{1,33},{64,66},{65,97},{2,0},{3,35},{66,64},{67,99},{4,6},{5... | collective-permute-start | bytes 393224 | tf_op jit(solution)/shard_map/ppermute | solution.py:49
  17.2 18.7 %collective-permute-start.10 = (bf16[4,64,1024]{2,1,0:T(8,128)(2,1)}, bf16[4,64,1024]{2,1,0:T(8,128)(2,1)S(1)}, u32[]{:S(2)}, u32[]{:S(2)}) collective-permute-start(bf16[4,64,1024]{2,1,0:T(8,128)(2,1)} %shard_map.106.refs_0_), channel_id=1, source_target_pairs={{0,8},{1,9},{64,72},{65,73},{2,10},{3,11},{66,74},{67,75},{4,12},{... | collective-permute-start | bytes 1572872 | tf_op jit(solution)/shard_map/ppermute | solution.py:49
  20.3 21.2 %collective-permute-start.8 = (bf16[4,64,1024]{2,1,0:T(8,128)(2,1)}, bf16[4,64,1024]{2,1,0:T(8,128)(2,1)}, u32[]{:S(2)}, u32[]{:S(2)}) collective-permute-start(bf16[4,64,1024]{2,1,0:T(8,128)(2,1)} %shard_map.106.refs_0_), channel_id=1, source_target_pairs={{0,4},{1,5},{64,68},{65,69},{2,6},{3,7},{66,70},{67,71},{4,8},{5,9... | collective-permute-start | bytes 1572872 | tf_op jit(solution)/shard_map/ppermute | solution.py:49
  21.0 20.9 %collective-permute-start.9 = (bf16[4,64,1024]{2,1,0:T(8,128)(2,1)}, bf16[4,64,1024]{2,1,0:T(8,128)(2,1)}, u32[]{:S(2)}, u32[]{:S(2)}) collective-permute-start(bf16[4,64,1024]{2,1,0:T(8,128)(2,1)} %shard_map.106.refs_0_), channel_id=1, source_target_pairs={{0,12},{1,13},{64,76},{65,77},{2,14},{3,15},{66,78},{67,79},{4,0},... | collective-permute-start | bytes 1572872 | tf_op jit(solution)/shard_map/ppermute | solution.py:49
  23.6 38.2 %all-to-all-start = ((bf16[8,640,256]{2,1,0:T(8,128)(2,1)}), bf16[8,640,256]{2,1,0:T(8,128)(2,1)S(1)}, u32[]{:S(2)}, u32[]{:S(2)}) async-start(bf16[8,640,256]{2,1,0:T(8,128)(2,1)} %copy-done.2), calls=%async_computation | async-start | bytes 5242880 | tf_op jit(solution)/shard_map/all_to_all | solution.py:476
  35.9 13.0 %copy-start.13 = (s32[4]{0:T(128)S(1)}, s32[4]{0:T(128)}, u32[]{:S(2)}) copy-start(s32[4]{0:T(128)} %constant.143.clone) | copy-start | bytes 52
  35.9 12.4 %collective-permute-start.1 = (bf16[128,4096]{1,0:T(8,128)(2,1)}, bf16[128,4096]{1,0:T(8,128)(2,1)}, u32[]{:S(2)}, u32[]{:S(2)}) collective-permute-start(bf16[128,4096]{1,0:T(8,128)(2,1)} %get-tuple-element.20.refs_1_.refs_2_), channel_id=1, source_target_pairs={{0,1},{1,0},{64,65},{65,64},{2,3},{3,2},{66,67},{67,66},{4,5},{5,4... | collective-permute-start | bytes 3145736 | tf_op jit(solution)/shard_map/ppermute | solution.py:44
  44.9 32.7 %collective-permute-start.11 = (bf16[16,64,1024]{2,1,0:T(8,128)(2,1)}, bf16[16,64,1024]{2,1,0:T(8,128)(2,1)}, u32[]{:S(2)}, u32[]{:S(2)}) collective-permute-start(bf16[16,64,1024]{2,1,0:T(8,128)(2,1)} %shard_map.107.refs_9_), channel_id=1, source_target_pairs={{0,16},{1,65},{64,80},{65,3},{2,18},{3,67},{66,82},{67,1},{4,20},{... | collective-permute-start | bytes 6291464 | tf_op jit(solution)/shard_map/ppermute | solution.py:483
  46.0 33.2 %collective-permute-start.12 = (bf16[16,64,1024]{2,1,0:T(8,128)(2,1)}, bf16[16,64,1024]{2,1,0:T(8,128)(2,1)}, u32[]{:S(2)}, u32[]{:S(2)}) collective-permute-start(bf16[16,64,1024]{2,1,0:T(8,128)(2,1)} %shard_map.107.refs_9_), channel_id=1, source_target_pairs={{0,48},{1,67},{64,112},{65,1},{2,50},{3,65},{66,114},{67,3},{4,52}... | collective-permute-start | bytes 6291464 | tf_op jit(solution)/shard_map/ppermute | solution.py:484
  46.9 4.0 %collective-permute-start.2 = (bf16[128,4096]{1,0:T(8,128)(2,1)}, bf16[128,4096]{1,0:T(8,128)(2,1)}, u32[]{:S(2)}, u32[]{:S(2)}) collective-permute-start(bf16[128,4096]{1,0:T(8,128)(2,1)} %get-tuple-element.21.refs_2_.refs_3_), channel_id=1, source_target_pairs={{0,1},{1,0},{64,65},{65,64},{2,3},{3,2},{66,67},{67,66},{4,5},{5,4... | collective-permute-start | bytes 3145736 | tf_op jit(solution)/shard_map/ppermute | solution.py:44
  48.3 4.1 %collective-permute-start.3 = (bf16[128,4096]{1,0:T(8,128)(2,1)}, bf16[128,4096]{1,0:T(8,128)(2,1)}, u32[]{:S(2)}, u32[]{:S(2)}) collective-permute-start(bf16[128,4096]{1,0:T(8,128)(2,1)} %get-tuple-element.22.refs_3_.refs_4_), channel_id=1, source_target_pairs={{0,1},{1,0},{64,65},{65,64},{2,3},{3,2},{66,67},{67,66},{4,5},{5,4... | collective-permute-start | bytes 3145736 | tf_op jit(solution)/shard_map/ppermute | solution.py:44
  48.3 5.6 %collective-permute-start.4 = (bf16[128,4096]{1,0:T(8,128)(2,1)}, bf16[128,4096]{1,0:T(8,128)(2,1)}, u32[]{:S(2)}, u32[]{:S(2)}) collective-permute-start(bf16[128,4096]{1,0:T(8,128)(2,1)} %get-tuple-element.23.refs_4_.refs_5_), channel_id=1, source_target_pairs={{0,1},{1,0},{64,65},{65,64},{2,3},{3,2},{66,67},{67,66},{4,5},{5,4... | collective-permute-start | bytes 3145736 | tf_op jit(solution)/shard_map/ppermute | solution.py:44
  61.8 17.5 %copy-start = (bf16[8,640,256]{2,1,0:T(8,128)(2,1)}, bf16[8,640,256]{2,1,0:T(8,128)(2,1)S(1)}, u32[]{:S(2)}) copy-start(bf16[8,640,256]{2,1,0:T(8,128)(2,1)S(1)} %all-to-all-done.through_in) | copy-start | bytes 7864324
  82.3 16.4 %collective-permute-start.15 = (bf16[8,640,256]{2,1,0:T(8,128)(2,1)}, bf16[8,640,256]{2,1,0:T(8,128)(2,1)S(1)}, u32[]{:S(2)}, u32[]{:S(2)}) collective-permute-start(bf16[8,640,256]{2,1,0:T(8,128)(2,1)} %get-tuple-element.29.own_ref), channel_id=1, source_target_pairs={{0,1},{1,0},{64,65},{65,64},{2,3},{3,2},{66,67},{67,66},{4,5},{5,4... | collective-permute-start | bytes 7864328 | tf_op jit(solution)/shard_map/ppermute | solution.py:44
  82.4 18.1 %collective-permute-start.13 = (bf16[8,64,1024]{2,1,0:T(8,128)(2,1)}, bf16[8,64,1024]{2,1,0:T(8,128)(2,1)}, u32[]{:S(2)}, u32[]{:S(2)}) collective-permute-start(bf16[8,64,1024]{2,1,0:T(8,128)(2,1)} %get-tuple-element.25), channel_id=1, source_target_pairs={{0,16},{1,65},{64,80},{65,3},{2,18},{3,67},{66,82},{67,1},{4,20},{... | collective-permute-start | bytes 3145736 | tf_op jit(solution)/shard_map/ppermute | solution.py:497
  83.0 17.6 %collective-permute-start.14 = (bf16[8,64,1024]{2,1,0:T(8,128)(2,1)}, bf16[8,64,1024]{2,1,0:T(8,128)(2,1)}, u32[]{:S(2)}, u32[]{:S(2)}) collective-permute-start(bf16[8,64,1024]{2,1,0:T(8,128)(2,1)} %get-tuple-element.26), channel_id=1, source_target_pairs={{0,48},{1,67},{64,112},{65,1},{2,50},{3,65},{66,114},{67,3},{4,52}... | collective-permute-start | bytes 3145736 | tf_op jit(solution)/shard_map/ppermute | solution.py:497
  85.6 13.0 %copy-start.1 = (bf16[8,640,256]{2,1,0:T(8,128)(2,1)S(1)}, bf16[8,640,256]{2,1,0:T(8,128)(2,1)}, u32[]{:S(2)}) copy-start(bf16[8,640,256]{2,1,0:T(8,128)(2,1)} %get-tuple-element.29.own_ref) | copy-start | bytes 7864324
  111.2 23.2 %all-to-all-start.1 = ((f32[64,24,128]{2,1,0:T(8,128)}), f32[64,24,128]{2,1,0:T(8,128)S(1)}, u32[]{:S(2)}, u32[]{:S(2)}) async-start(f32[64,24,128]{2,1,0:T(8,128)} %get-tuple-element.33), calls=%async_computation.1 | async-start | bytes 1572864 | tf_op jit(solution)/shard_map/all_to_all | solution.py:521
  139.7 33.5 %copy-start.6 = (bf16[256,256]{1,0:T(8,128)(2,1)S(1)}, bf16[256,256]{1,0:T(8,128)(2,1)}, u32[]{:S(2)}) copy-start(bf16[256,256]{1,0:T(8,128)(2,1)} %hidden_ref.1) | copy-start | bytes 393220
  139.7 33.5 %all-to-all-start.2 = ((bf16[16,501,128]{2,1,0:T(8,128)(2,1)}), bf16[16,501,128]{2,1,0:T(8,128)(2,1)S(1)}, u32[]{:S(2)}, u32[]{:S(2)}) async-start(bf16[16,501,128]{2,1,0:T(8,128)(2,1)} %copy-done.4), calls=%async_computation.2 | async-start | bytes 4128768 | tf_op jit(solution)/shard_map/all_to_all | solution.py:530
  145.0 1.1 collective-permute-start.16
  (12 other events, 38.6 us)

commit v8 on v7

--- a/solution.py
+++ b/solution.py
@@ -12,7 +12,7 @@
 
 AXES = ("variant", "vocab")
 SIDE = 4
-ROWS = 640
+ROWS = 632
 OFFSETS = (0, -1, 1, 2)
 
 

time: 177 us -> 176 us (level)
  no operation moved by 1% of the time
where the time goes in v8:
time: 176 us; the launch traced here: 175 us
  waiting for transfers between devices  70.4 us (40%)
  Pallas kernels  53 us (30%)
  starting transfers between devices  37.2 us (21%)
  local copies, waits for them, and re-layouts  11 us (6%)
  other arithmetic  2.54 us (1%)
    pallas_call x3, Pallas kernels, teacher_step(): pl.pallas_call(body, out_shape=out_shape, in_specs=in_specs, out_specs=ou...  31.2 us
    all_to_all x1, waiting for transfers between devices, on_device(): lax.all_to_all(errors, AXES, 0, 0, tiled=True, axis_index_groups=pairs)  26.5 us
    ppermute x1, waiting for transfers between devices, on_device(): before = lax.ppermute(hidden, AXES, plus)  15.5 us
    all_to_all x1, waiting for transfers between devices, on_device(): lax.all_to_all(packed, AXES, 0, 0, tiled=True, axis_index_groups=groups)  14.5 us
    ppermute x6, starting transfers between devices, ring_gather(): lax.ppermute(value, AXES, ring_shift(axes, step))  12.4 us
    all_to_all x1, starting transfers between devices, on_device(): lax.all_to_all(packed, AXES, 0, 0, tiled=True, axis_index_groups=groups)  8.22 us
    unnamed x34, local copies, waits for them, and re-layouts  8.1 us
    pallas_call x1, Pallas kernels, reorder(): pl.pallas_call(reorder_kernel, grid=(8,), out_shape=[jax.ShapeDtypeStruct...  7.34 us
  transfers between devices with their start and end apart: 20, of which 11 were waited for; matrix products, arithmetic and copies ran while one was open for 3% of the time, Pallas kernels for 19%

profile of v8, /device:TPU:2, one launch (start us, length us, event | category | flops | bytes accessed | tf_op | source)
XLA Modules:
  0.0 175.2 jit_solution(13389427172888000400)
XLA Ops:
  3.9 2.0 %collective-permute-start.5 = (bf16[64,1024]{1,0:T(8,128)(2,1)S(1)}, bf16[64,1024]{1,0:T(8,128)(2,1)S(1)}, u32[]{:S(2)}, u32[]{:S(2)}) collective-permute-start(bf16[64,1024]{1,0:T(8,128)(2,1)S(1)} %maximum_select_fusion.after.refs_0_), channel_id=1, source_target_pairs={{0,64},{1,17},{64,2},{65,81},{2,66},{3,19},{66,0},{67,83},{4,68},{... | collective-permute-start | bytes 393224 | tf_op jit(solution)/shard_map/ppermute | solution.py:49
  5.9 2.2 %collective-permute-start.6 = (bf16[64,1024]{1,0:T(8,128)(2,1)S(1)}, bf16[64,1024]{1,0:T(8,128)(2,1)S(1)}, u32[]{:S(2)}, u32[]{:S(2)}) collective-permute-start(bf16[64,1024]{1,0:T(8,128)(2,1)S(1)} %maximum_select_fusion.after.refs_0_), channel_id=1, source_target_pairs={{0,66},{1,49},{64,0},{65,113},{2,64},{3,51},{66,2},{67,115},{4,70}... | collective-permute-start | bytes 393224 | tf_op jit(solution)/shard_map/ppermute | solution.py:49
  8.1 1.8 %collective-permute-start.7 = (bf16[64,1024]{1,0:T(8,128)(2,1)S(1)}, bf16[64,1024]{1,0:T(8,128)(2,1)S(1)}, u32[]{:S(2)}, u32[]{:S(2)}) collective-permute-start(bf16[64,1024]{1,0:T(8,128)(2,1)S(1)} %maximum_select_fusion.after.refs_0_), channel_id=1, source_target_pairs={{0,2},{1,33},{64,66},{65,97},{2,0},{3,35},{66,64},{67,99},{4,6},{5... | collective-permute-start | bytes 393224 | tf_op jit(solution)/shard_map/ppermute | solution.py:49
  15.2 1.9 %shard_map.106.refs_0_ = bf16[4,64,1024]{2,1,0:T(8,128)(2,1)} custom-call(bf16[64,1024]{1,0:T(8,128)(2,1)} %copy-done.8, bf16[64,1024]{1,0:T(8,128)(2,1)} %copy-done.10, bf16[64,1024]{1,0:T(8,128)(2,1)} %copy-done.11, bf16[64,1024]{1,0:T(8,128)(2,1)} %copy-done.12, bf16[8,632,256]{2,1,0:T(8,128)(2,1)} %copy-done.2), custom_call_target="tpu_custom_call" | custom-call | bytes 1048576 | tf_op jit(solution)/shard_map/pallas_call | solution.py:66
  17.2 3.2 %collective-permute-start.10 = (bf16[4,64,1024]{2,1,0:T(8,128)(2,1)}, bf16[4,64,1024]{2,1,0:T(8,128)(2,1)S(1)}, u32[]{:S(2)}, u32[]{:S(2)}) collective-permute-start(bf16[4,64,1024]{2,1,0:T(8,128)(2,1)} %shard_map.106.refs_0_), channel_id=1, source_target_pairs={{0,8},{1,9},{64,72},{65,73},{2,10},{3,11},{66,74},{67,75},{4,12},{... | collective-permute-start | bytes 1572872 | tf_op jit(solution)/shard_map/ppermute | solution.py:49
  21.0 2.6 %collective-permute-start.9 = (bf16[4,64,1024]{2,1,0:T(8,128)(2,1)}, bf16[4,64,1024]{2,1,0:T(8,128)(2,1)}, u32[]{:S(2)}, u32[]{:S(2)}) collective-permute-start(bf16[4,64,1024]{2,1,0:T(8,128)(2,1)} %shard_map.106.refs_0_), channel_id=1, source_target_pairs={{0,12},{1,13},{64,76},{65,77},{2,14},{3,15},{66,78},{67,79},{4,0},... | collective-permute-start | bytes 1572872 | tf_op jit(solution)/shard_map/ppermute | solution.py:49
  23.6 4.9 %all-to-all-start = ((bf16[8,632,256]{2,1,0:T(8,128)(2,1)}), bf16[8,632,256]{2,1,0:T(8,128)(2,1)S(1)}, u32[]{:S(2)}, u32[]{:S(2)}) async-start(bf16[8,632,256]{2,1,0:T(8,128)(2,1)} %copy-done.2), calls=%async_computation | async-start | bytes 5177344 | tf_op jit(solution)/shard_map/all_to_all | solution.py:476
  28.5 7.3 %shard_map.104 = (bf16[128,4096]{1,0:T(8,128)(2,1)}, bf16[128,4096]{1,0:T(8,128)(2,1)}, bf16[128,4096]{1,0:T(8,128)(2,1)}, bf16[128,4096]{1,0:T(8,128)(2,1)}) custom-call(bf16[501,4096]{1,0:T(8,128)(2,1)} %bitcast.33, bf16[64,1024]{1,0:T(8,128)(2,1)} %copy-done.8), custom_call_target="tpu_custom_call" | custom-call | bytes 8208384 | tf_op jit(solution)/shard_map/pallas_call | solution.py:118
  35.9 5.6 %collective-permute-done.8.refs_1_ = bf16[4,64,1024]{2,1,0:T(8,128)(2,1)} collective-permute-done((bf16[4,64,1024]{2,1,0:T(8,128)(2,1)}, bf16[4,64,1024]{2,1,0:T(8,128)(2,1)}, u32[]{:S(2)}, u32[]{:S(2)}) %collective-permute-start.8) | collective-permute-done | bytes 524320 | tf_op jit(solution)/shard_map/ppermute | solution.py:49
  41.9 3.0 %shard_map.107.refs_9_ = bf16[16,64,1024]{2,1,0:T(8,128)(2,1)} custom-call(bf16[4,64,1024]{2,1,0:T(8,128)(2,1)} %shard_map.106.refs_0_, bf16[4,64,1024]{2,1,0:T(8,128)(2,1)} %collective-permute-done.8.refs_1_, bf16[4,64,1024]{2,1,0:T(8,128)(2,1)} %collective-permute-done.9.refs_2_, bf16[4,64,1024]{2,1,0:T(8,128)(2,1)} %copy-done.9), custom_call_target="tpu_custom_call" | custom-call | bytes 4194304 | tf_op jit(solution)/shard_map/pallas_call | solution.py:66
  53.9 7.8 %shard_map.108 = (f32[1024,1024]{1,0:T(8,128)}, f32[8,128]{1,0:T(8,128)}) custom-call(s32[20]{0:T(128)} %pad_add_fusion.refs_0_, bf16[128,4096]{1,0:T(8,128)(2,1)} %get-tuple-element.20.refs_1_.refs_2_, bf16[128,4096]{1,0:T(8,128)(2,1)} %get-tuple-element.21.refs_2_.refs_3_, bf16[128,4096]{1,0:T(8,128)(2,1)} %get-tuple-element.22.refs_3_.refs_4_, ...), custom_call_target="tpu_custom_call" | custom-call | flops 104857600 | bytes 102400 | tf_op jit(solution)/shard_map/pallas_call | solution.py:425
  61.7 15.5 %collective-permute-done.11.before.refs_9_ = bf16[16,64,1024]{2,1,0:T(8,128)(2,1)} collective-permute-done((bf16[16,64,1024]{2,1,0:T(8,128)(2,1)}, bf16[16,64,1024]{2,1,0:T(8,128)(2,1)}, u32[]{:S(2)}, u32[]{:S(2)}) %collective-permute-start.11) | collective-permute-done | bytes 2097184 | tf_op jit(solution)/shard_map/ppermute | solution.py:483
  77.2 1.7 collective-permute-done.12.after.refs_10_
  78.9 3.0 %shard_map.109 = (bf16[8,64,1024]{2,1,0:T(8,128)(2,1)}, bf16[8,64,1024]{2,1,0:T(8,128)(2,1)}, bf16[8,632,256]{2,1,0:T(8,128)(2,1)}) custom-call(bf16[16,64,1024]{2,1,0:T(8,128)(2,1)} %collective-permute-done.11.before.refs_9_, bf16[16,64,1024]{2,1,0:T(8,128)(2,1)} %collective-permute-done.12.after.refs_10_, ...), custom_call_target="tpu_custom_call", output_to_operand_aliasing={{2}: (2, {})} | custom-call | bytes 4194304 | tf_op jit(solution)/shard_map/pallas_call | solution.py:87
  85.3 12.9 %shard_map.110 = (f32[1024,1024]{1,0:T(8,128)}, f32[8,128]{1,0:T(8,128)}) custom-call(s32[20]{0:T(128)} %pad_add_fusion.refs_0_, bf16[128,4096]{1,0:T(8,128)(2,1)} %get-tuple-element.20.refs_1_.refs_2_, bf16[128,4096]{1,0:T(8,128)(2,1)} %get-tuple-element.21.refs_2_.refs_3_, bf16[128,4096]{1,0:T(8,128)(2,1)} %get-tuple-element.22.refs_3_.refs_4_, ...), custom_call_target="tpu_custom_call" | custom-call | flops 104857600 | bytes 102400 | tf_op jit(solution)/shard_map/pallas_call | solution.py:425
  98.3 1.9 %shard_map.111 = (f32[501,128]{1,0:T(8,128)S(1)}, f32[501,128]{1,0:T(8,128)S(1)}, f32[8,128]{1,0:T(8,128)S(1)}) custom-call(bf16[8,632,256]{2,1,0:T(8,128)(2,1)S(1)} %copy-done.1, bf16[8,632,256]{2,1,0:T(8,128)(2,1)S(1)} %collective-permute-done.15.other_ref, s32[1,128]{1,0:T(1,128)S(1)} %dynamic-slice_bitcast_fusion.3.ids_ref, s32[2]{0:T(128)S(1)} %pad_add_fusion.1.base_ref), custom_call_target="tpu_custom_call" | custom-call | flops 525336576 | bytes 12582912 | tf_op jit(solution)/shard_map/pallas_call | solution.py:278
  100.3 10.6 %shard_map.112 = (f32[2,501,1024]{2,1,0:T(8,128)}, f32[8,128]{1,0:T(8,128)S(1)}, f32[64,24,128]{2,1,0:T(8,128)}) custom-call(s32[20]{0:T(128)S(1)} %copy-done.7, f32[1,1024]{1,0:T(1,128)S(1)} %bitcast.30, bf16[128,4096]{1,0:T(8,128)(2,1)} %get-tuple-element.20.refs_1_.refs_2_, bf16[128,4096]{1,0:T(8,128)(2,1)} %get-tuple-element.21.refs_2_.refs_3_, ...), custom_call_target="tpu_custom_call" | custom-call | flops 2147483648 | bytes 8388608 | tf_op jit(solution)/shard_map/pallas_call | solution.py:425
  110.8 8.2 %all-to-all-start.1 = ((f32[64,24,128]{2,1,0:T(8,128)}), f32[64,24,128]{2,1,0:T(8,128)S(1)}, u32[]{:S(2)}, u32[]{:S(2)}) async-start(f32[64,24,128]{2,1,0:T(8,128)} %get-tuple-element.33), calls=%async_computation.1 | async-start | bytes 1572864 | tf_op jit(solution)/shard_map/all_to_all | solution.py:521
  119.4 14.5 %all-to-all-done.1.g_ref = f32[64,24,128]{2,1,0:T(8,128)S(1)} async-done(((f32[64,24,128]{2,1,0:T(8,128)}), f32[64,24,128]{2,1,0:T(8,128)S(1)}, u32[]{:S(2)}, u32[]{:S(2)}) %all-to-all-start.1) | async-done | bytes 786464 | tf_op jit(solution)/shard_map/all_to_all | solution.py:521
  133.9 2.2 %copy-done.3 = f32[2,501,1024]{2,1,0:T(8,128)S(1)} copy-done((f32[2,501,1024]{2,1,0:T(8,128)S(1)}, f32[2,501,1024]{2,1,0:T(8,128)}, u32[]{:S(2)}) %copy-start.3) | copy-done | bytes 4104216
  136.0 1.8 %shard_map.113 = (bf16[16,501,128]{2,1,0:T(8,128)(2,1)S(1)}, f32[1,128]{1,0:T(1,128)S(1)}) custom-call(f32[64,24,128]{2,1,0:T(8,128)S(1)} %all-to-all-done.1.g_ref, f32[2,501,1024]{2,1,0:T(8,128)S(1)} %copy-done.3, f32[501,128]{1,0:T(8,128)S(1)} %get-tuple-element.30.refs_13_.l_own, f32[501,128]{1,0:T(8,128)S(1)} %get-tuple-element.31.refs_14_.l_other, ...), custom_call_target="tpu_custom_call" | custom-call | flops 2565120 | bytes 6156288 | tf_op jit(solution)/shard_map/pallas_call | solution.py:172
  139.2 5.3 %all-to-all-start.2 = ((bf16[16,501,128]{2,1,0:T(8,128)(2,1)}), bf16[16,501,128]{2,1,0:T(8,128)(2,1)S(1)}, u32[]{:S(2)}, u32[]{:S(2)}) async-start(bf16[16,501,128]{2,1,0:T(8,128)(2,1)} %copy-done.4), calls=%async_computation.2 | async-start | bytes 4128768 | tf_op jit(solution)/shard_map/all_to_all | solution.py:530
  146.2 26.5 %all-to-all-done.2.err_ref = bf16[16,501,128]{2,1,0:T(8,128)(2,1)S(1)} async-done(((bf16[16,501,128]{2,1,0:T(8,128)(2,1)}), bf16[16,501,128]{2,1,0:T(8,128)(2,1)S(1)}, u32[]{:S(2)}, u32[]{:S(2)}) %all-to-all-start.2) | async-done | bytes 2052128 | tf_op jit(solution)/shard_map/all_to_all | solution.py:530
  172.7 2.3 %shard_map.114 = f32[4008,256]{1,0:T(8,128)} custom-call(bf16[16,501,128]{2,1,0:T(8,128)(2,1)S(1)} %all-to-all-done.2.err_ref, bf16[256,256]{1,0:T(8,128)(2,1)S(1)} %copy-done.6), custom_call_target="tpu_custom_call" | custom-call | flops 525336576 | bytes 7340032 | tf_op jit(solution)/shard_map/pallas_call | solution.py:208
  (91 shorter events, 25.4 us)
Async XLA Ops:
  1.6 2.3 %collective-permute-start = (bf16[32,1024]{1,0:T(8,128)(2,1)S(1)}, bf16[32,1024]{1,0:T(8,128)(2,1)S(1)}, u32[]{:S(2)}, u32[]{:S(2)}) collective-permute-start(bf16[32,1024]{1,0:T(8,128)(2,1)S(1)} %bitcast.36), channel_id=1, source_target_pairs={{0,1},{1,0},{64,65},{65,64},{2,3},{3,2},{66,67},{67,66},{4,5},{5,4... | collective-permute-start | bytes 196616 | tf_op jit(solution)/shard_map/ppermute | solution.py:44
  3.9 9.6 %collective-permute-start.5 = (bf16[64,1024]{1,0:T(8,128)(2,1)S(1)}, bf16[64,1024]{1,0:T(8,128)(2,1)S(1)}, u32[]{:S(2)}, u32[]{:S(2)}) collective-permute-start(bf16[64,1024]{1,0:T(8,128)(2,1)S(1)} %maximum_select_fusion.after.refs_0_), channel_id=1, source_target_pairs={{0,64},{1,17},{64,2},{65,81},{2,66},{3,19},{66,0},{67,83},{4,68},{... | collective-permute-start | bytes 393224 | tf_op jit(solution)/shard_map/ppermute | solution.py:49
  5.9 7.6 %collective-permute-start.6 = (bf16[64,1024]{1,0:T(8,128)(2,1)S(1)}, bf16[64,1024]{1,0:T(8,128)(2,1)S(1)}, u32[]{:S(2)}, u32[]{:S(2)}) collective-permute-start(bf16[64,1024]{1,0:T(8,128)(2,1)S(1)} %maximum_select_fusion.after.refs_0_), channel_id=1, source_target_pairs={{0,66},{1,49},{64,0},{65,113},{2,64},{3,51},{66,2},{67,115},{4,70}... | collective-permute-start | bytes 393224 | tf_op jit(solution)/shard_map/ppermute | solution.py:49
  8.1 6.5 %collective-permute-start.7 = (bf16[64,1024]{1,0:T(8,128)(2,1)S(1)}, bf16[64,1024]{1,0:T(8,128)(2,1)S(1)}, u32[]{:S(2)}, u32[]{:S(2)}) collective-permute-start(bf16[64,1024]{1,0:T(8,128)(2,1)S(1)} %maximum_select_fusion.after.refs_0_), channel_id=1, source_target_pairs={{0,2},{1,33},{64,66},{65,97},{2,0},{3,35},{66,64},{67,99},{4,6},{5... | collective-permute-start | bytes 393224 | tf_op jit(solution)/shard_map/ppermute | solution.py:49
  17.2 18.7 %collective-permute-start.10 = (bf16[4,64,1024]{2,1,0:T(8,128)(2,1)}, bf16[4,64,1024]{2,1,0:T(8,128)(2,1)S(1)}, u32[]{:S(2)}, u32[]{:S(2)}) collective-permute-start(bf16[4,64,1024]{2,1,0:T(8,128)(2,1)} %shard_map.106.refs_0_), channel_id=1, source_target_pairs={{0,8},{1,9},{64,72},{65,73},{2,10},{3,11},{66,74},{67,75},{4,12},{... | collective-permute-start | bytes 1572872 | tf_op jit(solution)/shard_map/ppermute | solution.py:49
  20.3 21.2 %collective-permute-start.8 = (bf16[4,64,1024]{2,1,0:T(8,128)(2,1)}, bf16[4,64,1024]{2,1,0:T(8,128)(2,1)}, u32[]{:S(2)}, u32[]{:S(2)}) collective-permute-start(bf16[4,64,1024]{2,1,0:T(8,128)(2,1)} %shard_map.106.refs_0_), channel_id=1, source_target_pairs={{0,4},{1,5},{64,68},{65,69},{2,6},{3,7},{66,70},{67,71},{4,8},{5,9... | collective-permute-start | bytes 1572872 | tf_op jit(solution)/shard_map/ppermute | solution.py:49
  21.0 20.9 %collective-permute-start.9 = (bf16[4,64,1024]{2,1,0:T(8,128)(2,1)}, bf16[4,64,1024]{2,1,0:T(8,128)(2,1)}, u32[]{:S(2)}, u32[]{:S(2)}) collective-permute-start(bf16[4,64,1024]{2,1,0:T(8,128)(2,1)} %shard_map.106.refs_0_), channel_id=1, source_target_pairs={{0,12},{1,13},{64,76},{65,77},{2,14},{3,15},{66,78},{67,79},{4,0},... | collective-permute-start | bytes 1572872 | tf_op jit(solution)/shard_map/ppermute | solution.py:49
  23.6 38.1 %all-to-all-start = ((bf16[8,632,256]{2,1,0:T(8,128)(2,1)}), bf16[8,632,256]{2,1,0:T(8,128)(2,1)S(1)}, u32[]{:S(2)}, u32[]{:S(2)}) async-start(bf16[8,632,256]{2,1,0:T(8,128)(2,1)} %copy-done.2), calls=%async_computation | async-start | bytes 5177344 | tf_op jit(solution)/shard_map/all_to_all | solution.py:476
  35.9 12.9 %copy-start.13 = (s32[4]{0:T(128)S(1)}, s32[4]{0:T(128)}, u32[]{:S(2)}) copy-start(s32[4]{0:T(128)} %constant.143.clone) | copy-start | bytes 52
  35.9 12.4 %collective-permute-start.1 = (bf16[128,4096]{1,0:T(8,128)(2,1)}, bf16[128,4096]{1,0:T(8,128)(2,1)}, u32[]{:S(2)}, u32[]{:S(2)}) collective-permute-start(bf16[128,4096]{1,0:T(8,128)(2,1)} %get-tuple-element.20.refs_1_.refs_2_), channel_id=1, source_target_pairs={{0,1},{1,0},{64,65},{65,64},{2,3},{3,2},{66,67},{67,66},{4,5},{5,4... | collective-permute-start | bytes 3145736 | tf_op jit(solution)/shard_map/ppermute | solution.py:44
  44.9 32.3 %collective-permute-start.11 = (bf16[16,64,1024]{2,1,0:T(8,128)(2,1)}, bf16[16,64,1024]{2,1,0:T(8,128)(2,1)}, u32[]{:S(2)}, u32[]{:S(2)}) collective-permute-start(bf16[16,64,1024]{2,1,0:T(8,128)(2,1)} %shard_map.107.refs_9_), channel_id=1, source_target_pairs={{0,16},{1,65},{64,80},{65,3},{2,18},{3,67},{66,82},{67,1},{4,20},{... | collective-permute-start | bytes 6291464 | tf_op jit(solution)/shard_map/ppermute | solution.py:483
  46.0 32.9 %collective-permute-start.12 = (bf16[16,64,1024]{2,1,0:T(8,128)(2,1)}, bf16[16,64,1024]{2,1,0:T(8,128)(2,1)}, u32[]{:S(2)}, u32[]{:S(2)}) collective-permute-start(bf16[16,64,1024]{2,1,0:T(8,128)(2,1)} %shard_map.107.refs_9_), channel_id=1, source_target_pairs={{0,48},{1,67},{64,112},{65,1},{2,50},{3,65},{66,114},{67,3},{4,52}... | collective-permute-start | bytes 6291464 | tf_op jit(solution)/shard_map/ppermute | solution.py:484
  46.9 4.0 %collective-permute-start.2 = (bf16[128,4096]{1,0:T(8,128)(2,1)}, bf16[128,4096]{1,0:T(8,128)(2,1)}, u32[]{:S(2)}, u32[]{:S(2)}) collective-permute-start(bf16[128,4096]{1,0:T(8,128)(2,1)} %get-tuple-element.21.refs_2_.refs_3_), channel_id=1, source_target_pairs={{0,1},{1,0},{64,65},{65,64},{2,3},{3,2},{66,67},{67,66},{4,5},{5,4... | collective-permute-start | bytes 3145736 | tf_op jit(solution)/shard_map/ppermute | solution.py:44
  48.3 4.1 %collective-permute-start.3 = (bf16[128,4096]{1,0:T(8,128)(2,1)}, bf16[128,4096]{1,0:T(8,128)(2,1)}, u32[]{:S(2)}, u32[]{:S(2)}) collective-permute-start(bf16[128,4096]{1,0:T(8,128)(2,1)} %get-tuple-element.22.refs_3_.refs_4_), channel_id=1, source_target_pairs={{0,1},{1,0},{64,65},{65,64},{2,3},{3,2},{66,67},{67,66},{4,5},{5,4... | collective-permute-start | bytes 3145736 | tf_op jit(solution)/shard_map/ppermute | solution.py:44
  48.3 5.6 %collective-permute-start.4 = (bf16[128,4096]{1,0:T(8,128)(2,1)}, bf16[128,4096]{1,0:T(8,128)(2,1)}, u32[]{:S(2)}, u32[]{:S(2)}) collective-permute-start(bf16[128,4096]{1,0:T(8,128)(2,1)} %get-tuple-element.23.refs_4_.refs_5_), channel_id=1, source_target_pairs={{0,1},{1,0},{64,65},{65,64},{2,3},{3,2},{66,67},{67,66},{4,5},{5,4... | collective-permute-start | bytes 3145736 | tf_op jit(solution)/shard_map/ppermute | solution.py:44
  61.7 17.2 %copy-start = (bf16[8,632,256]{2,1,0:T(8,128)(2,1)}, bf16[8,632,256]{2,1,0:T(8,128)(2,1)S(1)}, u32[]{:S(2)}) copy-start(bf16[8,632,256]{2,1,0:T(8,128)(2,1)S(1)} %all-to-all-done.through_in) | copy-start | bytes 7766020
  81.9 16.4 %collective-permute-start.15 = (bf16[8,632,256]{2,1,0:T(8,128)(2,1)}, bf16[8,632,256]{2,1,0:T(8,128)(2,1)S(1)}, u32[]{:S(2)}, u32[]{:S(2)}) collective-permute-start(bf16[8,632,256]{2,1,0:T(8,128)(2,1)} %get-tuple-element.29.own_ref), channel_id=1, source_target_pairs={{0,1},{1,0},{64,65},{65,64},{2,3},{3,2},{66,67},{67,66},{4,5},{5,4... | collective-permute-start | bytes 7766024 | tf_op jit(solution)/shard_map/ppermute | solution.py:44
  82.0 18.1 %collective-permute-start.13 = (bf16[8,64,1024]{2,1,0:T(8,128)(2,1)}, bf16[8,64,1024]{2,1,0:T(8,128)(2,1)}, u32[]{:S(2)}, u32[]{:S(2)}) collective-permute-start(bf16[8,64,1024]{2,1,0:T(8,128)(2,1)} %get-tuple-element.25), channel_id=1, source_target_pairs={{0,16},{1,65},{64,80},{65,3},{2,18},{3,67},{66,82},{67,1},{4,20},{... | collective-permute-start | bytes 3145736 | tf_op jit(solution)/shard_map/ppermute | solution.py:497
  82.6 17.5 %collective-permute-start.14 = (bf16[8,64,1024]{2,1,0:T(8,128)(2,1)}, bf16[8,64,1024]{2,1,0:T(8,128)(2,1)}, u32[]{:S(2)}, u32[]{:S(2)}) collective-permute-start(bf16[8,64,1024]{2,1,0:T(8,128)(2,1)} %get-tuple-element.26), channel_id=1, source_target_pairs={{0,48},{1,67},{64,112},{65,1},{2,50},{3,65},{66,114},{67,3},{4,52}... | collective-permute-start | bytes 3145736 | tf_op jit(solution)/shard_map/ppermute | solution.py:497
  85.3 13.0 %copy-start.1 = (bf16[8,632,256]{2,1,0:T(8,128)(2,1)S(1)}, bf16[8,632,256]{2,1,0:T(8,128)(2,1)}, u32[]{:S(2)}) copy-start(bf16[8,632,256]{2,1,0:T(8,128)(2,1)} %get-tuple-element.29.own_ref) | copy-start | bytes 7766020
  110.8 23.0 %all-to-all-start.1 = ((f32[64,24,128]{2,1,0:T(8,128)}), f32[64,24,128]{2,1,0:T(8,128)S(1)}, u32[]{:S(2)}, u32[]{:S(2)}) async-start(f32[64,24,128]{2,1,0:T(8,128)} %get-tuple-element.33), calls=%async_computation.1 | async-start | bytes 1572864 | tf_op jit(solution)/shard_map/all_to_all | solution.py:521
  139.2 33.5 %copy-start.6 = (bf16[256,256]{1,0:T(8,128)(2,1)S(1)}, bf16[256,256]{1,0:T(8,128)(2,1)}, u32[]{:S(2)}) copy-start(bf16[256,256]{1,0:T(8,128)(2,1)} %hidden_ref.1) | copy-start | bytes 393220
  139.2 33.5 %all-to-all-start.2 = ((bf16[16,501,128]{2,1,0:T(8,128)(2,1)}), bf16[16,501,128]{2,1,0:T(8,128)(2,1)S(1)}, u32[]{:S(2)}, u32[]{:S(2)}) async-start(bf16[16,501,128]{2,1,0:T(8,128)(2,1)} %copy-done.4), calls=%async_computation.2 | async-start | bytes 4128768 | tf_op jit(solution)/shard_map/all_to_all | solution.py:530
  144.5 1.1 collective-permute-start.16
  (12 other events, 38.6 us)
